TPU v7x, 32 devices: a whole 2x2x4 slice. The times are simulated.
32 devices in a mesh: parts: 1, axial: 8 (over y, x, core), radial: 4 (over z).
Axes of the slice: x: 2, y: 2, z: 4, core: 2. Of those that a mesh axis runs over, the one named last changes fastest.
Arguments:
- inputs: bfloat16 [64, 64, 8192], P(None, 'radial', ('parts', 'axial')), may hold values from -6 to 6
- saved_pre: bfloat16 [64, 64, 8192], P(None, 'radial', ('parts', 'axial')), may hold values from -6 to 6
- cotangent: bfloat16 [64, 64, 8192], P(None, 'radial', ('parts', 'axial')), may hold values from -24 to 24
- pointwise_weight: bfloat16 [64, 64], replicated, may hold values from -0.75 to 0.75
- spectral_weight: bfloat16 [32, 256, 64, 128], P('radial', 'axial'), may hold values from -3 to 3
Outputs:
- input_grad: bfloat16 [64, 64, 8192], P(None, 'radial', ('parts', 'axial'))
- spectral_grad: float32 [32, 256, 64, 128], P('radial', ('parts', 'axial'))
- weight_grad: float32 [64, 64], P('parts')
All inputs are finite; a program needn't handle non-finite values.
Results may differ from a plain program's by a relative error of at most 0.0053.
Values may be sent and summed in bfloat16 or wider, within the bound.
No kernel may reach another device: no remote copies, remote signals or barrier semaphores. Data moves between devices by JAX's collectives and lax.ppermute only.
A program may use at most 128 MiB of HBM per device.

v0:
```python
import math

import jax
import jax.numpy as jnp
from jax import lax
from jax.sharding import PartitionSpec as P

KA = 256
KR = 32


def axial_table(first, count, modes, total):
    points = first + jnp.arange(count, dtype=jnp.int32)
    orders = jnp.arange(modes, dtype=jnp.int32)
    phase = (points[:, None] * orders[None, :] % total).astype(jnp.float32) * (
        2.0 * math.pi / total
    )
    return (
        jnp.stack([jnp.cos(phase), -jnp.sin(phase)], axis=2)
        .reshape(count, 2 * modes)
        .astype(jnp.bfloat16)
    )


def radial_table(count, rows_first, rows_count, kept, total):
    orders = jnp.arange(count, dtype=jnp.int32)
    freqs = orders + jnp.where(orders >= kept // 2, total - kept, 0).astype(jnp.int32)
    rows = rows_first + jnp.arange(rows_count, dtype=jnp.int32)
    phase = (freqs[:, None] * rows[None, :] % total).astype(jnp.float32) * (2.0 * math.pi / total)
    return (jnp.cos(phase), jnp.sin(phase))


def gelu_slope(pre):
    value = pre.astype(jnp.float32)
    return 0.5 * (1.0 + jax.scipy.special.erf(value / math.sqrt(2.0))) + value * jnp.exp(
        -0.5 * value * value
    ) / math.sqrt(2.0 * math.pi)


def to_modes(axial_part, cos_r, sin_r, own_ax, channels, rad_rows):
    split = axial_part.reshape(own_ax, 2, channels, rad_rows)
    real_in = split[:, 0]
    imag_in = split[:, 1]
    high = lax.Precision.HIGHEST
    real_out = jnp.einsum("qr,kcr->qkc", cos_r, real_in, precision=high) + jnp.einsum(
        "qr,kcr->qkc", sin_r, imag_in, precision=high
    )
    imag_out = jnp.einsum("qr,kcr->qkc", cos_r, imag_in, precision=high) - jnp.einsum(
        "qr,kcr->qkc", sin_r, real_in, precision=high
    )
    return (real_out, imag_out)


def body(inputs, saved_pre, cotangent, pointwise_weight, spectral_weight):
    high = lax.Precision.HIGHEST
    channels, rad_rows, ax_cols = inputs.shape
    n_axial = lax.axis_size("axial")
    n_radial = lax.axis_size("radial")
    ax_index = lax.axis_index("axial")
    rad_index = lax.axis_index("radial")
    axial_total = ax_cols * n_axial
    radial_total = rad_rows * n_radial
    own_ax = KA // n_axial
    grad_pre = (cotangent.astype(jnp.float32) * gelu_slope(saved_pre)).astype(jnp.bfloat16)
    table = axial_table(ax_index * ax_cols, ax_cols, KA, axial_total)
    columns = table
    part_in = jnp.einsum("cra,aj->jcr", inputs, columns, preferred_element_type=jnp.float32)
    part_grad = jnp.einsum("cra,aj->jcr", grad_pre, columns, preferred_element_type=jnp.float32)
    summed = lax.psum_scatter(
        jnp.concatenate(
            [
                part_in.reshape(2 * own_ax * lax.axis_size("axial"), -1),
                part_grad.reshape(2 * own_ax * lax.axis_size("axial"), -1),
            ],
            axis=1,
        ),
        "axial",
        scatter_dimension=0,
        tiled=True,
    )
    half = channels * rad_rows
    spec_in = summed[:, :half].reshape(2 * own_ax, channels, rad_rows)
    spec_grad = summed[:, half:].reshape(2 * own_ax, channels, rad_rows)
    cos_r, sin_r = radial_table(KR, rad_index * rad_rows, rad_rows, KR, radial_total)
    x_real, x_imag = to_modes(spec_in, cos_r, sin_r, own_ax, channels, rad_rows)
    g_real, g_imag = to_modes(spec_grad, cos_r, sin_r, own_ax, channels, rad_rows)
    stacked = jnp.stack([x_real, x_imag, g_real, g_imag], axis=1)
    owned = lax.psum_scatter(stacked, "radial", scatter_dimension=0, tiled=True)
    orders = ax_index * own_ax + jnp.arange(own_ax, dtype=jnp.int32)
    scales = jnp.where(orders == 0, 1.0, 2.0).astype(jnp.float32) / (radial_total * axial_total)
    x_real = owned[:, 0]
    x_imag = owned[:, 1]
    dy_real = owned[:, 2] * scales[None, :, None]
    dy_imag = owned[:, 3] * scales[None, :, None]
    grad_real = (
        x_real[..., :, None] * dy_real[..., None, :] + x_imag[..., :, None] * dy_imag[..., None, :]
    )
    grad_imag = (
        x_real[..., :, None] * dy_imag[..., None, :] - x_imag[..., :, None] * dy_real[..., None, :]
    )
    spectral_grad = jnp.concatenate([grad_real, grad_imag], axis=3)
    w_real = spectral_weight[..., :channels].astype(jnp.float32)
    w_imag = spectral_weight[..., channels:].astype(jnp.float32)
    dx_real = jnp.einsum("qkio,qko->qki", w_real, dy_real, precision=high) + jnp.einsum(
        "qkio,qko->qki", w_imag, dy_imag, precision=high
    )
    dx_imag = jnp.einsum("qkio,qko->qki", w_real, dy_imag, precision=high) - jnp.einsum(
        "qkio,qko->qki", w_imag, dy_real, precision=high
    )
    mode_grad = jnp.stack([dx_real, dx_imag], axis=1)
    row_first = rad_index * rad_rows
    piece = lax.all_gather(mode_grad, "radial", axis=0, tiled=True)
    cos_q, sin_q = radial_table(piece.shape[0], row_first, rad_rows, KR, radial_total)
    piece_real = piece[:, 0]
    piece_imag = piece[:, 1]
    out_real = jnp.einsum("qr,qkc->kcr", cos_q, piece_real, precision=high) - jnp.einsum(
        "qr,qkc->kcr", sin_q, piece_imag, precision=high
    )
    out_imag = jnp.einsum("qr,qkc->kcr", sin_q, piece_real, precision=high) + jnp.einsum(
        "qr,qkc->kcr", cos_q, piece_imag, precision=high
    )
    back = jnp.stack([out_real, out_imag], axis=1)
    lines_back = back.astype(jnp.bfloat16).reshape(2 * own_ax, channels * rad_rows)
    columns = table
    spectral_part = jnp.einsum(
        "jm,aj->ma",
        lax.all_gather(lines_back, "axial", axis=0, tiled=True),
        columns,
        preferred_element_type=jnp.float32,
    )
    flat_grad = grad_pre.reshape(channels, rad_rows * ax_cols)
    flat_in = inputs.reshape(channels, rad_rows * ax_cols)
    point_part = jnp.dot(pointwise_weight, flat_grad, preferred_element_type=jnp.float32)
    input_grad = (
        (point_part + spectral_part.reshape(channels, rad_rows * ax_cols))
        .astype(jnp.bfloat16)
        .reshape(channels, rad_rows, ax_cols)
    )
    local_weight = lax.dot_general(
        flat_in, flat_grad, (((1,), (1,)), ((), ())), preferred_element_type=jnp.float32
    )
    weight_grad = lax.psum(local_weight, ("axial", "radial")) / math.sqrt(
        radial_total * axial_total
    )
    return (input_grad, spectral_grad, weight_grad)


def solution(mesh):
    placed = (
        P(None, "radial", ("parts", "axial")),
        P(None, "radial", ("parts", "axial")),
        P(None, "radial", ("parts", "axial")),
        P(),
        P("radial", "axial", None, None),
    )
    return jax.shard_map(
        body,
        mesh=mesh,
        in_specs=placed,
        out_specs=(
            P(None, "radial", ("parts", "axial")),
            P("radial", ("parts", "axial"), None, None),
            P("parts", None),
        ),
        check_vma=False,
    )
```

profile of v0, /device:TPU:0, one launch (start us, length us, event | category | flops | bytes accessed | tf_op | source)
XLA Modules:
  0.0 311.8 jit_solution(6213764440670143054)
XLA Ops:
  7.2 5.0 %fusion.44 = (bf16[1024,256,1]{1,0,2:T(8,128)(2,1)S(1)}, bf16[1024,256,1]{1,0,2:T(8,128)(2,1)S(1)}) fusion(s32[1024]{0:T(1024)S(1)} %iota_add_fusion), kind=kLoop, calls=%fused_computation.67 | loop fusion | flops 4456448 | bytes 1052672 | tf_op jit(solution)/shard_map/cos | solution.py:19
  12.4 2.1 copy.31
  16.0 3.9 %fusion.9 = bf16[64,16,1024]{2,1,0:T(8,128)(2,1)S(1)} fusion(bf16[64,16,1024]{2,1,0:T(8,128)(2,1)} %param.6, bf16[64,16,1024]{2,1,0:T(8,128)(2,1)} %param.7), kind=kLoop, calls=%fused_computation.18 | loop fusion | flops 12582912 | bytes 6291456 | tf_op jit(solution)/shard_map/convert_element_type | solution.py:64
  22.5 2.5 pad_maximum_fusion.1
  25.4 53.9 %reduce-scatter.3.cloned.1.call-done = f32[64,2048]{1,0:T(8,128)} async-done(((f32[512,2048]{1,0:T(8,128)}), f32[64,2048]{1,0:T(8,128)}) %reduce-scatter.3.cloned.1.call-update) | async-done | bytes 524304 | tf_op jit(solution)/shard_map/reduce_scatter | solution.py:69
  80.3 2.0 reshape_reshape.6
  82.4 4.3 %fusion.41 = f32[32,32,64]{2,0,1:T(8,128)S(1)} fusion(f32[32,2,64,16]{3,2,1,0:T(8,128)} %reshape_reshape.6, s32[16]{0:T(128)S(1)} %iota_add_fusion.1, s32[32]{0:T(128)S(1)} %fusion.84), kind=kOutput, calls=%fused_computation.62 | convolution fusion | flops 12590080 | bytes 1310912 | tf_op jit(solution)/shard_map/qr,kcr->qkc/dot_general | solution.py:48
  86.7 4.3 %fusion.40 = f32[32,32,64]{2,0,1:T(8,128)S(1)} fusion(f32[32,2,64,16]{3,2,1,0:T(8,128)} %reshape_reshape.6, s32[16]{0:T(128)S(1)} %iota_add_fusion.1, s32[32]{0:T(128)S(1)} %fusion.84), kind=kOutput, calls=%fused_computation.61 | convolution fusion | flops 12590080 | bytes 1310912 | tf_op jit(solution)/shard_map/qr,kcr->qkc/dot_general | solution.py:45
  91.0 2.0 reshape_reshape.7
  93.1 4.5 %fusion.43 = f32[32,32,64]{2,0,1:T(8,128)S(1)} fusion(f32[32,2,64,16]{3,2,1,0:T(8,128)} %reshape_reshape.7, s32[16]{0:T(128)S(1)} %iota_add_fusion.1, s32[32]{0:T(128)S(1)} %fusion.84), kind=kOutput, calls=%fused_computation.64 | convolution fusion | flops 12590080 | bytes 1310912 | tf_op jit(solution)/shard_map/qr,kcr->qkc/dot_general | solution.py:48
  97.6 4.3 %fusion.42 = f32[32,32,64]{2,0,1:T(8,128)S(1)} fusion(f32[32,2,64,16]{3,2,1,0:T(8,128)} %reshape_reshape.7, s32[16]{0:T(128)S(1)} %iota_add_fusion.1, s32[32]{0:T(128)S(1)} %fusion.84), kind=kOutput, calls=%fused_computation.63 | convolution fusion | flops 12590080 | bytes 1310912 | tf_op jit(solution)/shard_map/qr,kcr->qkc/dot_general | solution.py:45
  101.9 4.4 %fusion.23 = f32[32,1,32,64]{3,0,2,1:T(8,128)S(1)} fusion(f32[32,32,64]{2,0,1:T(8,128)S(1)} %fusion.41, f32[32,2,64,16]{3,2,1,0:T(8,128)} %reshape_reshape.6, s32[16]{0:T(128)S(1)} %iota_add_fusion.1, s32[32]{0:T(128)S(1)} %fusion.84), kind=kOutput, calls=%fused_computation.40 | convolution fusion | flops 12655616 | bytes 1573056 | tf_op jit(solution)/shard_map/qr,kcr->qkc/dot_general | solution.py:48
  106.3 3.2 %fusion.24 = f32[32,1,32,64]{3,0,2,1:T(8,128)S(1)} fusion(f32[32,32,64]{2,0,1:T(8,128)S(1)} %fusion.40, f32[32,2,64,16]{3,2,1,0:T(8,128)S(1)} %copy-done.2, s32[16]{0:T(128)S(1)} %iota_add_fusion.1, s32[32]{0:T(128)S(1)} %fusion.84), kind=kOutput, calls=%fused_computation.42 | convolution fusion | flops 12655616 | bytes 1836032 | tf_op jit(solution)/shard_map/qr,kcr->qkc/dot_general | solution.py:45
  109.5 3.6 %fusion.21 = f32[32,1,32,64]{3,0,2,1:T(8,128)S(1)} fusion(f32[32,32,64]{2,0,1:T(8,128)S(1)} %fusion.43, f32[32,2,64,16]{3,2,1,0:T(8,128)S(1)} %copy-done.3, s32[16]{0:T(128)S(1)} %iota_add_fusion.1, s32[32]{0:T(128)S(1)} %fusion.84), kind=kOutput, calls=%fused_computation.36 | convolution fusion | flops 12655616 | bytes 1836032 | tf_op jit(solution)/shard_map/qr,kcr->qkc/dot_general | solution.py:48
  113.1 3.1 %fusion.22 = f32[32,1,32,64]{3,0,2,1:T(8,128)S(1)} fusion(f32[32,32,64]{2,0,1:T(8,128)S(1)} %fusion.42, f32[32,2,64,16]{3,2,1,0:T(8,128)S(1)} %copy-done.3, s32[16]{0:T(128)S(1)} %iota_add_fusion.1, s32[32]{0:T(128)S(1)} %fusion.84), kind=kOutput, calls=%fused_computation.38 | convolution fusion | flops 12655616 | bytes 1836032 | tf_op jit(solution)/shard_map/qr,kcr->qkc/dot_general | solution.py:45
  116.2 1.6 pad_maximum_fusion.2
  117.9 44.0 %reduce-scatter.5.cloned.1.call-done = f32[8,4,32,64]{3,0,2,1:T(8,128)} async-done(((f32[32,4,32,64]{3,0,2,1:T(8,128)}), f32[8,4,32,64]{3,0,2,1:T(8,128)}) %reduce-scatter.5.cloned.1.call-update) | async-done | bytes 262160 | tf_op jit(solution)/shard_map/reduce_scatter | solution.py:88
  163.1 8.6 %fusion.10 = f32[8,32,1,64]{3,2,1,0:T(1,128)S(1)} fusion(bf16[8,32,64,128]{3,2,1,0:T(8,128)(2,1)} %param.9, f32[8,32,64,1]{2,0,1,3:T(8,128)S(1)} %bitcast.134), kind=kOutput, calls=%fused_computation.19 | convolution fusion | flops 12582912 | bytes 4325376 | tf_op jit(solution)/shard_map/qkio,qko->qki/dot_general | solution.py:107
  171.7 6.6 %fusion.16 = f32[8,32,1,64]{3,2,1,0:T(1,128)S(1)} fusion(bf16[8,32,64,128]{3,2,1,0:T(8,128)(2,1)S(1)} %copy-done.11, f32[8,32,64,1]{2,0,1,3:T(8,128)S(1)} %bitcast.135), kind=kOutput, calls=%fused_computation.25 | convolution fusion | flops 12582912 | bytes 4325376 | tf_op jit(solution)/shard_map/qkio,qko->qki/dot_general | solution.py:104
  178.3 6.6 %fusion.14 = f32[8,32,1,64]{3,2,1,0:T(1,128)S(1)} fusion(bf16[8,32,64,128]{3,2,1,0:T(8,128)(2,1)S(1)} %copy-done.11, f32[8,32,64,1]{2,0,1,3:T(8,128)S(1)} %bitcast.136), kind=kOutput, calls=%fused_computation.23 | convolution fusion | flops 12582912 | bytes 4325376 | tf_op jit(solution)/shard_map/qkio,qko->qki/dot_general | solution.py:107
  184.9 6.7 %fusion.12 = f32[8,32,1,64]{3,2,1,0:T(1,128)S(1)} fusion(bf16[8,32,64,128]{3,2,1,0:T(8,128)(2,1)S(1)} %copy-done.11, f32[8,32,64,1]{2,0,1,3:T(8,128)S(1)} %bitcast.137), kind=kOutput, calls=%fused_computation.21 | convolution fusion | flops 12582912 | bytes 4325376 | tf_op jit(solution)/shard_map/qkio,qko->qki/dot_general | solution.py:104
  191.9 21.4 %all_gather.6 = f32[32,2,32,64]{3,0,2,1:T(8,128)S(1)} all-gather(f32[8,2,32,64]{3,0,2,1:T(8,128)S(1)} %pad_maximum_fusion.3), channel_id=1, replica_groups=mesh['parts'=1,'axial'=8,'radial'=4] {'radial'}, dimensions={0}, use_global_device_ids=true | all-gather | bytes 655360 | tf_op jit(solution)/shard_map/all_gather | solution.py:112
  215.8 2.4 convert_element_type.61
  218.3 6.1 %fusion.29 = f32[64,64]{0,1:T(8,128)S(1)} fusion(bf16[64,16,1024]{2,1,0:T(8,128)(2,1)S(1)} %copy-done, bf16[64,16,1024]{2,1,0:T(8,128)(2,1)} %copy-done.4), kind=kOutput, calls=%fused_computation.49 | convolution fusion | flops 134217728 | bytes 4210688 | tf_op jit(solution)/shard_map/dot_general | solution.py:139
  224.4 39.2 %psum.7 = f32[64,64]{0,1:T(8,128)S(1)} all-reduce(f32[64,64]{0,1:T(8,128)S(1)} %fusion.29), channel_id=1, replica_groups=mesh['parts'=1,'axial'=8,'radial'=4] {'axial','radial'}, use_global_device_ids=true, to_apply=%region_2.3 | all-reduce | flops 4096 | bytes 32768 | tf_op jit(solution)/shard_map/psum | solution.py:142
  264.4 4.2 %copy.54 = bf16[8,8,16,1024]{3,1,2,0:T(8,128)(2,1)} copy(bf16[8,8,16,1024]{3,2,1,0:T(8,128)(2,1)} %bitcast.130) | data formatting | bytes 4194304
  268.7 8.5 %multiply_add_fusion = (f32[8,32,64,64]{3,2,1,0:T(8,128)}, f32[8,32,64,64]{3,2,1,0:T(8,128)}) fusion(f32[8,32,64]{2,1,0:T(8,128)S(1)} %copy.40, f32[8,32,64]{2,1,0:T(8,128)S(1)} %copy.39, f32[8,32,64]{2,1,0:T(8,128)S(1)} %copy.38, f32[8,32,64]{2,1,0:T(8,128)S(1)} %copy.37), kind=kLoop, calls=%fused_computation.5 | loop fusion | flops 6291456 | bytes 8650752 | tf_op jit(solution)/shard_map/add | solution.py:96
  277.2 12.2 %pad_maximum_fusion = f32[8,32,64,128]{3,2,1,0:T(8,128)} fusion(f32[8,32,64,64]{3,2,1,0:T(8,128)} %get-tuple-element.15, f32[8,32,64,64]{3,2,1,0:T(8,128)} %get-tuple-element.14), kind=kLoop, calls=%fused_computation.3 | loop fusion | flops 2097152 | bytes 16777216 | tf_op jit(solution)/shard_map/concatenate | solution.py:101
  289.4 4.5 %fusion.137 = f32[1024,1024]{1,0:T(8,128)} fusion(bf16[512,1024]{1,0:T(8,128)(2,1)} %all-gather.2.cloned.1.call-done, bf16[1024,512]{0,1:T(8,128)(2,1)S(1)} %copy-done.6), kind=kOutput, calls=%fused_computation.166 | convolution fusion | flops 1073741824 | bytes 6291456 | tf_op jit(solution)/shard_map/jm,aj->ma/dot_general | solution.py:125
  293.9 5.0 %reshape.173 = f32[64,16384]{1,0:T(8,128)} reshape(f32[1024,1024]{1,0:T(8,128)} %fusion.137) | data formatting | bytes 8388608 | tf_op jit(solution)/shard_map/reshape | solution.py:135
  298.9 3.7 %fusion.1 = bf16[64,16384]{1,0:T(8,128)(2,1)S(1)} fusion(f32[64,16384]{1,0:T(8,128)} %reshape.173, bf16[64,64]{1,0:T(8,128)(2,1)S(1)} %copy-done.10, bf16[64,16384]{1,0:T(8,128)(2,1)} %bitcast.131), kind=kOutput, calls=%fused_computation.2 | convolution fusion | flops 136314880 | bytes 8396800 | tf_op jit(solution)/shard_map/dot_general | solution.py:133
  302.5 2.5 copy.55
  (56 shorter events, 10.6 us)
Async XLA Ops:
  7.2 14.1 %copy-start = (bf16[64,16,1024]{2,1,0:T(8,128)(2,1)S(1)}, bf16[64,16,1024]{2,1,0:T(8,128)(2,1)}, u32[]{:S(2)}) copy-start(bf16[64,16,1024]{2,1,0:T(8,128)(2,1)} %param.5) | copy-start | bytes 6291460
  7.2 72.1 %reduce-scatter.3.cloned.1.call-start = ((), (), s32[]{:S(2)}) async-start(), calls=%async_computation.2 | async-start | bytes 4718592 | tf_op jit(solution)/shard_map/reduce_scatter | solution.py:69
  16.0 5.3 %copy-start.5 = (bf16[1024,512]{0,1:T(8,128)(2,1)}, bf16[1024,512]{0,1:T(8,128)(2,1)S(1)}, u32[]{:S(2)}) copy-start(bf16[1024,512]{0,1:T(8,128)(2,1)S(1)} %convert_element_type.60) | copy-start | bytes 3145732
  19.9 1.3 copy-start.4
  25.1 136.8 %reduce-scatter.5.cloned.1.call-start = ((), (), s32[]{:S(2)}) async-start(), calls=%async_computation.3 | async-start | bytes 2621440 | tf_op jit(solution)/shard_map/reduce_scatter | solution.py:88
  93.1 13.2 %copy-start.2 = (f32[32,2,64,16]{3,2,1,0:T(8,128)S(1)}, f32[32,2,64,16]{3,2,1,0:T(8,128)}, u32[]{:S(2)}) copy-start(f32[32,2,64,16]{3,2,1,0:T(8,128)} %reshape_reshape.6) | copy-start | bytes 786436
  93.1 16.4 %copy-start.3 = (f32[32,2,64,16]{3,2,1,0:T(8,128)S(1)}, f32[32,2,64,16]{3,2,1,0:T(8,128)}, u32[]{:S(2)}) copy-start(f32[32,2,64,16]{3,2,1,0:T(8,128)} %reshape_reshape.7) | copy-start | bytes 786436
  117.8 171.6 %all-gather.2.cloned.1.call-start = ((), (), s32[]{:S(2)}) async-start(), calls=%async_computation.4 | async-start | bytes 1179648 | tf_op jit(solution)/shard_map/all_gather | solution.py:127
  161.8 9.9 %copy-start.11 = (bf16[8,32,64,128]{3,2,1,0:T(8,128)(2,1)S(1)}, bf16[8,32,64,128]{3,2,1,0:T(8,128)(2,1)}, u32[]{:S(2)}) copy-start(bf16[8,32,64,128]{3,2,1,0:T(8,128)(2,1)} %param.9) | copy-start | bytes 12582916
  163.1 21.8 %copy-start.7 = (f32[8,32,64]{2,0,1:T(8,128)}, f32[8,32,64]{2,0,1:T(8,128)S(1)}, u32[]{:S(2)}) copy-start(f32[8,32,64]{2,0,1:T(8,128)S(1)} %get-tuple-element.12) | copy-start | bytes 196612
  218.3 50.3 %copy-start.8 = (f32[8,32,64]{2,0,1:T(8,128)S(1)}, f32[8,32,64]{2,0,1:T(8,128)}, u32[]{:S(2)}) copy-start(f32[8,32,64]{2,0,1:T(8,128)} %copy-done.7) | copy-start | bytes 196612
  218.3 50.3 %copy-start.9 = (f32[8,4,32,64]{3,0,2,1:T(8,128)S(1)}, f32[8,4,32,64]{3,0,2,1:T(8,128)}, u32[]{:S(2)}) copy-start(f32[8,4,32,64]{3,0,2,1:T(8,128)} %reduce-scatter.5.cloned.1.call-done) | copy-start | bytes 786436
  277.2 12.2 %copy-start.6 = (bf16[1024,512]{0,1:T(8,128)(2,1)S(1)}, bf16[1024,512]{0,1:T(8,128)(2,1)}, u32[]{:S(2)}) copy-start(bf16[1024,512]{0,1:T(8,128)(2,1)} %copy-done.5) | copy-start | bytes 3145732
  293.9 5.0 %copy-start.10 = (bf16[64,64]{1,0:T(8,128)(2,1)S(1)}, bf16[64,64]{1,0:T(8,128)(2,1)}, u32[]{:S(2)}) copy-start(bf16[64,64]{1,0:T(8,128)(2,1)} %param.8) | copy-start | bytes 24580
  298.9 6.2 %copy-start.1 = (bf16[64,16,1024]{2,1,0:T(8,128)(2,1)S(1)}, bf16[64,16,1024]{2,1,0:T(8,128)(2,1)}, u32[]{:S(2)}) copy-start(bf16[64,16,1024]{2,1,0:T(8,128)(2,1)} %param.5) | copy-start | bytes 6291460
Sparse Core Ops, SparseCore 0:
  25.2 53.9 reduce-scatter.2
  117.9 43.8 reduce-scatter.4
  218.4 23.6 all-gather.1
where the time goes:
time: 316 us; the launch traced here: 312 us
  waiting for transfers between devices  97.9 us (31%)
  matrix products  79 us (25%)
  blocking collectives  60.6 us (19%)
  other arithmetic  35.4 us (11%)
  local copies, waits for them, and re-layouts  24.2 us (8%)
  between operations  14.4 us (5%)
    reduce_scatter x1, waiting for transfers between devices, body(): lax.psum_scatter(jnp.concatenate([part_in.reshape(2 * own_ax * lax.axis_s...  53.9 us
    reduce_scatter x1, waiting for transfers between devices, body(): owned = lax.psum_scatter(stacked, 'radial', scatter_dimension=0, tiled=True)  44 us
    psum x1, blocking collectives, body(): lax.psum(local_weight, ('axial', 'radial'))  39.2 us
    all_gather x1, blocking collectives, body(): piece = lax.all_gather(mode_grad, 'radial', axis=0, tiled=True)  21.4 us
    concatenate x1, other arithmetic, body(): spectral_grad = jnp.concatenate([grad_real, grad_imag], axis=3)  12.2 us
    dot_general x2, matrix products, to_modes(): jnp.einsum('qr,kcr->qkc', cos_r, imag_in, precision=high)  8.81 us
    dot_general x2, matrix products, to_modes(): jnp.einsum('qr,kcr->qkc', cos_r, real_in, precision=high)  8.67 us
    dot_general x1, matrix products, body(): jnp.einsum('qkio,qko->qki', w_imag, dy_real, precision=high)  8.64 us
  transfers between devices with their start and end apart: 3, of which 2 were waited for; matrix products, arithmetic and copies ran while one was open for 10% of the time, Pallas kernels for 0%

commit v1 on v0

v1 whole, which is shorter than its diff:
```python
import functools
import math

import jax
import jax.numpy as jnp
import ml_dtypes
import numpy as np
from jax import lax
from jax.experimental import pallas as pl
from jax.experimental.pallas import tpu as pltpu
from jax.sharding import PartitionSpec as P

KA = 256
KR = 32
F32 = jnp.float32
BF16 = jnp.bfloat16
ANYSPACE = pl.ANY


def dot(a, b, dims=((1,), (0,))):
    return lax.dot_general(a, b, (dims, ((), ())), preferred_element_type=F32)


def tree_sum(values):
    while len(values) > 1:
        values = [values[i] + values[i + 1] for i in range(0, len(values), 2)]
    return values[0]


def split(value):
    high = value.astype(BF16)
    return high, (value - high.astype(F32)).astype(BF16)


class Sizes:
    def __init__(self, channels, rows, cols, n_axial, n_radial):
        self.c, self.r, self.a = channels, rows, cols
        self.n_axial, self.n_radial = n_axial, n_radial
        self.chips = n_axial // 2
        self.own = KA // n_axial
        self.j = 2 * self.own
        self.cr = channels * rows
        self.qo = KR // n_radial
        self.cg = 128 // self.qo
        self.ng = channels // self.cg
        self.kb = self.cg * rows
        self.half = KR * self.cg
        self.lanes = self.qo * channels
        self.blk = 256
        self.nblk = self.cr // self.blk
        self.axial_total = cols * n_axial
        self.radial_total = rows * n_radial
        self.ride_a = 16
        self.ride_b = channels * 128 // self.lanes


def axial_base(z):
    k = np.arange(KA, dtype=np.int64)
    a = np.arange(z.a, dtype=np.int64)
    m = (k[:, None] * a[None, :]) % z.axial_total
    phase = m * (2.0 * np.pi / z.axial_total)
    return np.cos(phase).astype(np.float32), np.sin(phase).astype(np.float32)


def axial_shift(z):
    k = np.arange(KA, dtype=np.int64)
    b = np.arange(z.n_axial, dtype=np.int64)
    m = (b[:, None] * k[None, :]) % z.n_axial
    phase = m * (2.0 * np.pi / z.n_axial)
    out = np.zeros((z.n_axial, KA, 128), np.float32)
    out[:, :, 0] = np.cos(phase)
    out[:, :, 1] = np.sin(phase)
    return out


def radial_freqs(z):
    q = np.arange(KR, dtype=np.int64)
    return q + np.where(q >= KR // 2, z.radial_total - KR, 0)


def radial_base(z):
    g = radial_freqs(z)
    r = np.arange(z.r, dtype=np.int64)
    m = (g[:, None] * r[None, :]) % z.radial_total
    phase = m * (2.0 * np.pi / z.radial_total)
    eye = np.eye(z.cg, dtype=np.float64)
    parts = [
        np.einsum("rq,cd->crqd", f(phase).T, eye).reshape(z.kb, z.half) for f in (np.cos, np.sin)
    ]
    table = np.concatenate(parts, axis=1).astype(np.float32)
    high = table.astype(ml_dtypes.bfloat16)
    low = (table - high.astype(np.float32)).astype(ml_dtypes.bfloat16)
    return high, low


def radial_shift(z):
    g = radial_freqs(z)
    first = np.arange(z.n_radial, dtype=np.int64) * z.r
    m = (first[:, None] * g[None, :]) % z.radial_total
    phase = m * (2.0 * np.pi / z.radial_total)
    out = np.zeros((z.n_radial, z.n_radial, 8, 128), np.float32)
    for row, f in ((0, np.cos), (1, np.sin)):
        lanes = np.repeat(f(phase), z.cg, axis=1)
        out[:, :, row, :] = lanes.reshape(z.n_radial, z.n_radial, 128)
    return out


def lane_sums():
    out = np.zeros((8, 2, 128, 128), np.float32)
    for kk in range(8):
        for h in range(2):
            out[kk, h, :, h * 64 + kk] = 1.0
    return out.reshape(2048, 128).astype(ml_dtypes.bfloat16)


def gelu_slope(value):
    return 0.5 * (1.0 + lax.erf(value * (1.0 / math.sqrt(2.0)))) + value * jnp.exp(
        -0.5 * value * value
    ) * (1.0 / math.sqrt(2.0 * math.pi))


def split_owners(z, idx, part, keep_ref, send_ref, stage):
    for o in range(z.n_axial):
        stage[o] = part[o * z.j : (o + 1) * z.j, :].astype(BF16)
    chip, core = idx[0] // 2, idx[0] % 2
    for d in range(z.chips):
        keep_ref[d, : z.j, :] = stage[(chip ^ d) * 2 + core]
        send_ref[d, : z.j, :] = stage[(chip ^ d) * 2 + (1 - core)]


def grad_kernel(z, idx, cos_ref, sin_ref, shift_ref, pre_ref, cot_ref, g_ref, t_ref, keep_ref, send_ref, stage):
    @pl.when(pl.program_id(0) == 0)
    def _():
        for o in range(z.n_axial):
            rows = pl.ds(o * z.own, z.own)
            c1, s1 = cos_ref[rows, :], sin_ref[rows, :]
            c2, s2 = shift_ref[0, rows, 0:1], shift_ref[0, rows, 1:2]
            t_ref[o * z.j : o * z.j + z.own, :] = (c1 * c2 - s1 * s2).astype(BF16)
            t_ref[o * z.j + z.own : (o + 1) * z.j, :] = (-(s1 * c2 + c1 * s2)).astype(BF16)

    g = (cot_ref[...].astype(F32) * gelu_slope(pre_ref[...].astype(F32))).astype(BF16)
    g_ref[...] = g
    part = dot(t_ref[...], g, ((1,), (1,)))
    split_owners(z, idx, part, keep_ref, send_ref, stage)


def input_kernel(z, idx, t_ref, x_ref, g_ref, keep_ref, send_ref, stage):
    x = x_ref[...]
    part = dot(t_ref[...], x, ((1,), (1,)))
    split_owners(z, idx, part, keep_ref, send_ref, stage)
    cross = dot(x, g_ref[...], ((1,), (1,)))
    row = lax.broadcasted_iota(jnp.int32, cross.shape, 0)
    col = lax.broadcasted_iota(jnp.int32, cross.shape, 1)
    cross = jnp.where(row % z.r == col % z.r, cross, 0.0)
    nc = z.blk // z.r
    cross = jnp.sum(cross.reshape(nc, z.r, z.cr), axis=1)
    high, low = split(cross)
    col = lax.broadcasted_iota(jnp.int32, (z.cr, 128), 0) // z.r
    lane = lax.broadcasted_iota(jnp.int32, (z.cr, 128), 1) % z.c
    pick = (col == lane).astype(F32).astype(BF16)
    both = dot(high, pick) + dot(low, pick)
    ride = high_low(z, both)
    ride = jnp.concatenate([ride[i * 8 : (i + 1) * 8] for i in range(nc // 8)], axis=1)
    ride = jnp.concatenate([ride, jnp.zeros_like(ride)], axis=0).astype(BF16)
    for d in range(z.chips):
        keep_ref[d, z.j :, :] = ride
        send_ref[d, z.j :, :] = ride


def high_low(z, both):
    lane = lax.broadcasted_iota(jnp.int32, both.shape, 1) % 128
    high = both.astype(BF16).astype(F32)
    return jnp.where(lane < z.c, high, both - high)


def fold(block):
    return block + pltpu.roll(block, 64, 1)


def add_kernel(z, ride, keep_ref, recv_ref, own_ref, *send_refs):
    for d, out in enumerate((own_ref,) + send_refs):
        total = keep_ref[d, : z.j, :].astype(F32) + recv_ref[d, : z.j, :].astype(F32)
        out[: z.j, :] = total.astype(out.dtype)
    if ride:
        total = keep_ref[0, z.j :, :].astype(F32) + recv_ref[0, z.j :, :].astype(F32)
        parts = [
            high_low(z, fold(total[:, i * 128 : (i + 1) * 128])) for i in range(z.cr // 128)
        ]
        total = jnp.concatenate(parts, axis=1).astype(BF16)
        for out in (own_ref,) + send_refs:
            out[z.j :, :] = total.astype(out.dtype)


def radial_kernel(z, ride, idx, high_ref, low_ref, shift_ref, *refs):
    pieces, outs, stage = refs[: z.chips], refs[z.chips : z.chips + z.n_radial], refs[-1]
    me = idx[1]
    value = tree_sum([p[: z.j, :].astype(F32) for p in pieces])
    t_high, t_low = high_ref[...], low_ref[...]
    for g in range(z.ng):
        high, low = split(value[:, g * z.kb : (g + 1) * z.kb])
        both = dot(jnp.concatenate([high, low], axis=0), t_high)
        total = both[: z.j] + both[z.j :] + dot(high, t_low)
        c, s = total[:, : z.half], total[:, z.half :]
        real = c[: z.own] + s[z.own :]
        imag = c[z.own :] - s[: z.own]
        for zz in range(z.n_radial):
            cos, sin = shift_ref[0, zz, 0:1, :], shift_ref[0, zz, 1:2, :]
            lanes = slice(zz * 128, (zz + 1) * 128)
            re, im = real[:, lanes], imag[:, lanes]
            stage[zz, : z.own, g * 128 : (g + 1) * 128] = cos * re + sin * im
            stage[zz, z.own : z.j, g * 128 : (g + 1) * 128] = cos * im - sin * re
    for d, out in enumerate(outs):
        out[: z.j, :] = stage[me ^ d].astype(out.dtype)
    if ride:
        total = tree_sum([p[z.j : z.j + 8, :].astype(F32) for p in pieces])
        parts = [
            high_low(z, fold(total[:, i * 128 : (i + 1) * 128])) for i in range(z.cr // 128)
        ]
        w = jnp.concatenate(parts, axis=0)
        n = z.ride_b
        w = jnp.concatenate([w[i * n : (i + 1) * n] for i in range(z.lanes // 128)], axis=1)
        w = w.astype(BF16)
        for out in outs:
            out[z.j :, :] = w.astype(out.dtype)


def channel_rows(z, value):
    if z.j < 128:
        value = jnp.concatenate([value, jnp.zeros((128 - z.j, z.lanes), F32)], axis=0)
    turned = value.T
    blocks = []
    for q in range(z.qo):
        starts = [(g * z.qo + q) * z.cg for g in range(z.ng)]
        blocks.append(jnp.concatenate([turned[s : s + z.cg] for s in starts], axis=0))
    return blocks


def mode_kernel(z, idx, w_ref, e_ref, *refs):
    pieces = refs[: z.n_radial]
    dx_ref, dy_ref, products, acc = refs[z.n_radial :]
    step = pl.program_id(0)

    @pl.when(step == 0)
    def _():
        value = tree_sum([p[...].astype(F32) for p in pieces])
        k = lax.broadcasted_iota(jnp.int32, value.shape, 0) % z.own + idx[0] * z.own
        scale = 1.0 / (z.radial_total * z.axial_total)
        value = value * jnp.where(k == 0, scale, 2.0 * scale)
        blocks = channel_rows(z, value)
        lane = lax.broadcasted_iota(jnp.int32, (z.own, 128), 1)
        for q in range(0, z.qo, 2):
            pair = jnp.concatenate(blocks[q : q + 2], axis=0).T
            re, im = pair[: z.own], pair[z.own : z.j]
            re2, im2 = pltpu.roll(re, 64, 1), pltpu.roll(im, 64, 1)
            dy_ref[q, 0] = jnp.where(lane < 64, re, im2)
            dy_ref[q, 1] = jnp.where(lane < 64, im, -re2)
            dy_ref[q + 1, 0] = jnp.where(lane < 64, re2, im)
            dy_ref[q + 1, 1] = jnp.where(lane < 64, im2, -re)
        acc[...] = jnp.zeros_like(acc)

    for q in range(z.qo):
        for kk in range(8):
            w = w_ref[q, kk].astype(F32)
            d0 = dy_ref[q, 0, pl.ds(step * 8 + kk, 1), :]
            d1 = dy_ref[q, 1, pl.ds(step * 8 + kk, 1), :]
            rows = slice(q * z.c, (q + 1) * z.c)
            products[rows, kk * 256 : kk * 256 + 128] = (w * d0).astype(BF16)
            products[rows, kk * 256 + 128 : kk * 256 + 256] = (w * d1).astype(BF16)
    sums = dot(products[...], e_ref[...])
    acc[...] += pltpu.roll(sums, step * 8, 1)

    @pl.when(step == pl.num_programs(0) - 1)
    def _():
        rows = []
        for g in range(z.ng):
            for q in range(z.qo):
                start = q * z.c + g * z.cg
                rows.append(acc[start : start + z.cg, :])
        turned = jnp.concatenate(rows, axis=0).T
        dx_ref[: z.own, :] = turned[: z.own].astype(BF16)
        dx_ref[z.own :, :] = turned[64 : 64 + z.own].astype(BF16)


def outer_kernel(z, dy_ref, *refs):
    pieces = refs[: z.n_radial]
    out_ref, wg_ref, x_rows = refs[z.n_radial :]
    step = pl.program_id(0)

    @pl.when(step == 0)
    def _():
        value = tree_sum([p[: z.j, :].astype(F32) for p in pieces])
        for q, block in enumerate(channel_rows(z, value)):
            x_rows[q] = block
        ride = tree_sum([p[z.j :, :].astype(F32) for p in pieces])
        n = z.lanes // 128
        ride = jnp.concatenate([fold(ride[:, i * 128 : (i + 1) * 128]) for i in range(n)], axis=0)
        wg_ref[...] = ride[:, : z.c] * (1.0 / math.sqrt(z.radial_total * z.axial_total))

    x = x_rows[step]
    for k in range(z.own):
        d0 = dy_ref[0, 0, k : k + 1, :]
        d1 = dy_ref[0, 1, k : k + 1, :]
        out_ref[0, k] = x[:, k : k + 1] * d0 + x[:, z.own + k : z.own + k + 1] * d1


def back_kernel(z, idx, high_ref, low_ref, shift_ref, *refs):
    pieces, (out_ref, stage) = refs[: z.n_radial], refs[z.n_radial :]
    me = idx[1]
    for d, piece in enumerate(pieces):
        zz = me ^ d
        cos, sin = shift_ref[0, zz, 0:1, :], shift_ref[0, zz, 1:2, :]
        for g in range(z.ng):
            block = piece[:, g * 128 : (g + 1) * 128].astype(F32)
            re, im = block[: z.own], block[z.own :]
            stage[zz, g, : z.own, :] = (cos * re - sin * im).astype(BF16)
            stage[zz, g, z.own :, :] = (sin * re + cos * im).astype(BF16)
    cos_high, sin_high = high_ref[:, : z.half], high_ref[:, z.half :]
    cos_low, sin_low = low_ref[:, : z.half], low_ref[:, z.half :]
    nt = ((1,), (1,))
    for g in range(z.ng):
        lhs = jnp.concatenate([stage[zz, g] for zz in range(z.n_radial)], axis=1)
        c = dot(lhs, cos_high, nt) + dot(lhs, cos_low, nt)
        s = dot(lhs, sin_high, nt) + dot(lhs, sin_low, nt)
        lanes = slice(g * z.kb, (g + 1) * z.kb)
        out_ref[: z.own, lanes] = (c[: z.own] - s[z.own :]).astype(BF16)
        out_ref[z.own :, lanes] = (s[: z.own] + c[z.own :]).astype(BF16)


def point_kernel(z, w_ref, g_ref, out_ref):
    n = z.blk // z.r
    row = lax.broadcasted_iota(jnp.int32, (z.blk, n), 0) // z.r
    pick = (row == lax.broadcasted_iota(jnp.int32, (z.blk, n), 1)).astype(F32).astype(BF16)
    tall = dot(pick, w_ref[...]).astype(BF16)
    col = lax.broadcasted_iota(jnp.int32, (z.c, z.cr), 1) // z.r
    pick = (col == lax.broadcasted_iota(jnp.int32, (z.c, z.cr), 0)).astype(F32).astype(BF16)
    full = dot(tall, pick)
    row = lax.broadcasted_iota(jnp.int32, full.shape, 0) % z.r
    col = lax.broadcasted_iota(jnp.int32, full.shape, 1) % z.r
    full = jnp.where(row == col, full, 0.0).astype(BF16)
    out_ref[...] = dot(full, g_ref[...])


def final_kernel(z, idx, t_ref, point_ref, *refs):
    pieces, (out_ref, stage) = refs[: z.n_axial], refs[z.n_axial :]

    @pl.when(pl.program_id(0) == 0)
    def _():
        for d, piece in enumerate(pieces):
            rows = pl.ds(pl.multiple_of((idx[0] ^ d) * z.j, z.j), z.j)
            for b in range(z.nblk):
                stage[b, rows, :] = piece[:, b * z.blk : (b + 1) * z.blk]

    lines = stage[pl.program_id(0)]
    out_ref[...] = (dot(lines, t_ref[...], ((0,), (0,))) + point_ref[...]).astype(BF16)


def whole_spec(shape):
    return pl.BlockSpec(shape, lambda *_: (0,) * len(shape))


def call(kernel, idx, grid, in_specs, out_specs, out_shape, scratch, args, flops, name):
    size = sum(math.prod(s.shape) * s.dtype.itemsize for s in jax.tree.leaves(out_shape))
    size += sum(math.prod(a.shape) * a.dtype.itemsize for a in args)
    return pl.pallas_call(
        kernel,
        out_shape=out_shape,
        grid_spec=pltpu.PrefetchScalarGridSpec(
            num_scalar_prefetch=0 if idx is None else 1,
            grid=grid,
            in_specs=in_specs,
            out_specs=out_specs,
            scratch_shapes=scratch,
        ),
        compiler_params=pltpu.CompilerParams(vmem_limit_bytes=48 << 20),
        cost_estimate=pl.CostEstimate(flops=flops, bytes_accessed=size, transcendentals=0),
        name=name,
    )(*(() if idx is None else (idx,)), *args)


def xor_permute(value, axis, size, d):
    return lax.ppermute(value, axis, [(i, i ^ d) for i in range(size)])


def body(inputs, saved_pre, cotangent, pointwise_weight, spectral_weight):
    channels, rows, cols = inputs.shape
    z = Sizes(channels, rows, cols, lax.axis_size("axial"), lax.axis_size("radial"))
    sds = jax.ShapeDtypeStruct
    idx = jnp.stack([lax.axis_index("axial"), lax.axis_index("radial")]).astype(jnp.int32)
    flat = (z.cr, z.a)
    x, pre, cot = (v.reshape(flat) for v in (inputs, saved_pre, cotangent))
    cos_a, sin_a = axial_base(z)
    r_high, r_low = radial_base(z)
    r_shift = radial_shift(z)
    row_block = pl.BlockSpec((z.blk, z.a), lambda i, *_: (i, 0))
    shift_block = pl.BlockSpec((1, z.n_radial, 8, 128), lambda i, idx: (idx[1], 0, 0, 0))

    def part_spec(extra):
        return pl.BlockSpec((z.chips, z.j + extra, z.blk), lambda i, *_: (0, 0, i))

    def part_shape(extra):
        return sds((z.chips, z.j + extra, z.cr), BF16)

    stage = [pltpu.VMEM((z.n_axial, z.j, z.blk), BF16)]
    mm = 2 * KA * z.cr * z.a * 2
    g, table, g_keep, g_send = call(
        functools.partial(grad_kernel, z), idx, (z.nblk,),
        [whole_spec(cos_a.shape), whole_spec(sin_a.shape),
         pl.BlockSpec((1, KA, 128), lambda i, idx: (idx[0], 0, 0)), row_block, row_block],
        [row_block, whole_spec((2 * KA, z.a)), part_spec(0), part_spec(0)],
        [sds(flat, BF16), sds((2 * KA, z.a), BF16), part_shape(0), part_shape(0)],
        stage, (jnp.asarray(cos_a), jnp.asarray(sin_a), jnp.asarray(axial_shift(z)), pre, cot),
        mm * 3, "grad_axial")

    def add(keep, recv, extra, name):
        shape = (z.j + extra, z.cr)
        return call(
            functools.partial(add_kernel, z, extra > 0), None, (1,),
            [whole_spec(keep.shape)] * 2, [whole_spec(shape)] * z.chips,
            [sds(shape, F32)] + [sds(shape, BF16)] * (z.chips - 1), [], (keep, recv), 0, name)

    def axial_exchange(parts):
        return [parts[0]] + [
            xor_permute(parts[d], "axial", z.n_axial, 2 * d) for d in range(1, z.chips)]

    def radial(pieces, extra_in, extra_out, name):
        shape = (z.j + extra_out, z.lanes)
        return call(
            functools.partial(radial_kernel, z, extra_in > 0), idx, (1,),
            [whole_spec(r_high.shape)] * 2 + [shift_block]
            + [whole_spec((z.j + extra_in, z.cr))] * z.chips,
            [whole_spec(shape)] * z.n_radial,
            [sds(shape, F32)] + [sds(shape, BF16)] * (z.n_radial - 1),
            [pltpu.VMEM((z.n_radial, z.j, z.lanes), F32)],
            (jnp.asarray(r_high), jnp.asarray(r_low), jnp.asarray(r_shift), *pieces),
            mm // 2, name)

    def radial_exchange(parts):
        return [parts[0]] + [
            xor_permute(parts[d], "radial", z.n_radial, d) for d in range(1, z.n_radial)]

    g_recv = xor_permute(g_send, "axial", z.n_axial, 1)
    x_keep, x_send = call(
        functools.partial(input_kernel, z), idx, (z.nblk,),
        [whole_spec((2 * KA, z.a)), row_block, whole_spec(flat)],
        [part_spec(z.ride_a)] * 2, [part_shape(z.ride_a)] * 2, stage, (table, x, g),
        mm * 3, "input_axial")
    g_parts = add(g_keep, g_recv, 0, "grad_add")
    g_pieces = axial_exchange(g_parts)
    x_recv = xor_permute(x_send, "axial", z.n_axial, 1)
    point = call(
        functools.partial(point_kernel, z), None, (z.nblk,),
        [pl.BlockSpec((z.blk // z.r, z.c), lambda i: (i, 0)), whole_spec(flat)],
        row_block, sds(flat, F32), [], (pointwise_weight, g), mm * 2, "pointwise")
    x_parts = add(x_keep, x_recv, z.ride_a, "input_add")

    g_modes = radial_exchange(radial(g_pieces, 0, 0, "grad_radial"))
    x_pieces = axial_exchange(x_parts)
    x_own = radial(x_pieces, z.ride_a, z.ride_b, "input_radial")

    piece_shape = (z.j, z.lanes)
    sums = lane_sums()
    d_x, d_y = call(
        functools.partial(mode_kernel, z), idx, (z.own // 8,),
        [pl.BlockSpec((z.qo, 8, z.c, 128), lambda i, *_: (0, i, 0, 0)), whole_spec(sums.shape)]
        + [whole_spec(piece_shape)] * z.n_radial,
        [whole_spec(piece_shape), whole_spec((z.qo, 2, z.own, 128))],
        [sds(piece_shape, BF16), sds((z.qo, 2, z.own, 128), F32)],
        [pltpu.VMEM((z.qo * z.c, 2048), BF16), pltpu.VMEM((z.qo * z.c, 128), F32)],
        (spectral_weight, jnp.asarray(sums), *g_modes), mm * 2, "mode_grad")
    d_pieces = radial_exchange([d_x] * z.n_radial)
    x_modes = radial_exchange(x_own)
    lines = call(
        functools.partial(back_kernel, z), idx, (1,),
        [whole_spec(r_high.shape)] * 2 + [shift_block] + [whole_spec(piece_shape)] * z.n_radial,
        whole_spec((z.j, z.cr)), sds((z.j, z.cr), BF16),
        [pltpu.VMEM((z.n_radial, z.ng, z.j, 128), BF16)],
        (jnp.asarray(r_high), jnp.asarray(r_low), jnp.asarray(r_shift), *d_pieces),
        mm // 2, "back_radial")
    near = [lines] + [xor_permute(lines, "axial", z.n_axial, 2 * d) for d in range(1, z.chips)]
    far = [xor_permute(v, "axial", z.n_axial, 1) for v in near]
    all_lines = [v for pair in zip(near, far) for v in pair]
    ride_shape = (z.j + z.ride_b, z.lanes)
    spectral_grad, weight_grad = call(
        functools.partial(outer_kernel, z), None, (z.qo,),
        [pl.BlockSpec((1, 2, z.own, 128), lambda i: (i, 0, 0, 0))]
        + [whole_spec(ride_shape)] * z.n_radial,
        [pl.BlockSpec((1, z.own, z.c, 128), lambda i: (i, 0, 0, 0)), whole_spec((z.c, z.c))],
        [sds((z.qo, z.own, z.c, 128), F32), sds((z.c, z.c), F32)],
        [pltpu.VMEM((z.qo, z.c, 128), F32)], (d_y, *x_modes), mm, "spectral_outer")
    input_grad = call(
        functools.partial(final_kernel, z), idx, (z.nblk,),
        [whole_spec((2 * KA, z.a)), row_block] + [whole_spec((z.j, z.cr))] * z.n_axial,
        row_block, sds(flat, BF16), [pltpu.VMEM((z.nblk, 2 * KA, z.blk), BF16)],
        (table, point, *all_lines), mm, "final_axial")
    return (input_grad.reshape(inputs.shape), spectral_grad, weight_grad)


def solution(mesh):
    placed = (
        P(None, "radial", ("parts", "axial")),
        P(None, "radial", ("parts", "axial")),
        P(None, "radial", ("parts", "axial")),
        P(),
        P("radial", "axial", None, None),
    )
    return jax.shard_map(
        body,
        mesh=mesh,
        in_specs=placed,
        out_specs=(
            P(None, "radial", ("parts", "axial")),
            P("radial", ("parts", "axial"), None, None),
            P("parts", None),
        ),
        check_vma=False,
    )
```

time: 316 us -> 92.7 us (0.29); the launches traced: 312 us -> 92.3 us
  matrix products: 79 us -> 0 us
  waiting for transfers between devices: 97.9 us -> 23.1 us
  blocking collectives: 60.6 us -> 0 us
  Pallas kernels: 0 us -> 42.4 us
  other arithmetic: 35.4 us -> 0.08 us
  starting transfers between devices: 0.34 us -> 22.3 us
  local copies, waits for them, and re-layouts: 24.2 us -> 3.71 us
  between operations: 14.4 us -> 0.77 us
    reduce_scatter x2 -> x0, waiting for transfers between devices: 97.8 us -> none  [the longest x1 53.9 us: body(): lax.psum_scatter(jnp.concatenate([part_in.reshape(2 * own_ax * lax.axis_s...]
    dot_general x21 -> x0, matrix products: 79 us -> none  [the longest x2 8.81 us: to_modes(): jnp.einsum('qr,kcr->qkc', cos_r, imag_in, precision=high)]
    pallas_call x0 -> x11, Pallas kernels: none -> 42.4 us  [call(): pl.pallas_call(kernel, out_shape=out_shape, grid_spec=pltpu.PrefetchScala...]
    psum x1 -> x0, blocking collectives: 39.2 us -> none  [body(): lax.psum(local_weight, ('axial', 'radial'))]
    ppermute x0 -> x24, waiting for transfers between devices: none -> 23.1 us  [xor_permute(): return lax.ppermute(value, axis, [(i, i ^ d) for i in range(size)])]
    ppermute x0 -> x24, starting transfers between devices: none -> 22.3 us  [xor_permute(): return lax.ppermute(value, axis, [(i, i ^ d) for i in range(size)])]
    all_gather x1 -> x0, blocking collectives: 21.4 us -> none  [body(): piece = lax.all_gather(mode_grad, 'radial', axis=0, tiled=True)]
    concatenate x2 -> x0, other arithmetic: 14.7 us -> none  [the longest x1 12.2 us: body(): spectral_grad = jnp.concatenate([grad_real, grad_imag], axis=3)]
  transfers between devices with their start and end apart: 3 -> 24, of which waited for: 2 -> 11; matrix products, arithmetic and copies ran while one was open for 10% -> 0% of each run, Pallas kernels for 0% -> 33%
where the time goes in v1:
time: 92.7 us; the launch traced here: 92.3 us
  Pallas kernels  42.4 us (46%)
  waiting for transfers between devices  23.1 us (25%)
  starting transfers between devices  22.3 us (24%)
  local copies, waits for them, and re-layouts  3.71 us (4%)
    pallas_call x11, Pallas kernels, call(): pl.pallas_call(kernel, out_shape=out_shape, grid_spec=pltpu.PrefetchScala...  42.4 us
    ppermute x24, waiting for transfers between devices, xor_permute(): return lax.ppermute(value, axis, [(i, i ^ d) for i in range(size)])  23.1 us
    ppermute x24, starting transfers between devices, xor_permute(): return lax.ppermute(value, axis, [(i, i ^ d) for i in range(size)])  22.3 us
    unnamed x22, local copies, waits for them, and re-layouts  3.71 us
  transfers between devices with their start and end apart: 24, of which 11 were waited for; matrix products, arithmetic and copies ran while one was open for 0% of the time, Pallas kernels for 33%

profile of v1, /device:TPU:0, one launch (start us, length us, event | category | flops | bytes accessed | tf_op | source)
XLA Modules:
  0.0 92.3 jit_solution(2722483561007561277)
XLA Ops:
  0.7 1.2 %copy-done.3 = f32[8,256,128]{2,1,0:T(8,128)S(1)} copy-done((f32[8,256,128]{2,1,0:T(8,128)S(1)}, f32[8,256,128]{2,1,0:T(8,128)}, u32[]{:S(2)}) %copy-start.3) | copy-done | bytes 1048600
  1.9 1.2 %copy-done.4 = f32[256,1024]{1,0:T(8,128)S(1)} copy-done((f32[256,1024]{1,0:T(8,128)S(1)}, f32[256,1024]{1,0:T(8,128)}, u32[]{:S(2)}) %copy-start.4) | copy-done | bytes 1048600
  3.2 1.2 %copy-done.5 = f32[256,1024]{1,0:T(8,128)S(1)} copy-done((f32[256,1024]{1,0:T(8,128)S(1)}, f32[256,1024]{1,0:T(8,128)}, u32[]{:S(2)}) %copy-start.5) | copy-done | bytes 1048600
  4.4 6.6 %grad_axial.1 = (bf16[1024,1024]{1,0:T(8,128)(2,1)}, bf16[512,1024]{1,0:T(8,128)(2,1)S(1)}, bf16[4,64,1024]{2,1,0:T(8,128)(2,1)S(1)}, bf16[4,64,1024]{2,1,0:T(8,128)(2,1)S(1)}) custom-call(s32[2]{0:T(128)S(1)} %pad_add_fusion.idx, f32[256,1024]{1,0:T(8,128)S(1)} %copy-done.5, f32[256,1024]{1,0:T(8,128)S(1)} %copy-done.4, f32[8,256,128]{2,1,0:T(8,128)S(1)} %copy-done.3, ...), custom_call_target="tpu_custom_call" | custom-call | flops 3221225472 | bytes 11534336 | tf_op jit(solution)/shard_map/grad_axial/pallas_call | solution.py:364
  11.5 7.9 %input_axial.1 = (bf16[4,80,1024]{2,1,0:T(8,128)(2,1)S(1)}, bf16[4,80,1024]{2,1,0:T(8,128)(2,1)S(1)}) custom-call(s32[2]{0:T(128)S(1)} %pad_add_fusion.idx, bf16[512,1024]{1,0:T(8,128)(2,1)S(1)} %get-tuple-element.29.t_ref, bf16[1024,1024]{1,0:T(8,128)(2,1)S(1)} %bitcast.6, bf16[1024,1024]{1,0:T(8,128)(2,1)} %get-tuple-element.30.g_ref), custom_call_target="tpu_custom_call" | custom-call | flops 3221225472 | bytes 6553600 | tf_op jit(solution)/shard_map/input_axial/pallas_call | solution.py:364
  19.7 3.0 %collective-permute-start.1 = (bf16[64,1024]{1,0:T(8,128)(2,1)S(1)}, bf16[64,1024]{1,0:T(8,128)(2,1)S(1)}, u32[]{:S(2)}, u32[]{:S(2)}) collective-permute-start(bf16[64,1024]{1,0:T(8,128)(2,1)S(1)} %get-tuple-element.34), channel_id=1, source_target_pairs={{0,8},{4,12},{8,0},{12,4},{16,24},{20,28},{24,16},{28,20},{1,9},{5... | collective-permute-start | bytes 393224 | tf_op jit(solution)/shard_map/ppermute | solution.py:381
  22.7 1.5 %collective-permute-start.2 = (bf16[64,1024]{1,0:T(8,128)(2,1)S(1)}, bf16[64,1024]{1,0:T(8,128)(2,1)S(1)}, u32[]{:S(2)}, u32[]{:S(2)}) collective-permute-start(bf16[64,1024]{1,0:T(8,128)(2,1)S(1)} %get-tuple-element.35), channel_id=1, source_target_pairs={{0,16},{4,20},{8,24},{12,28},{16,0},{20,4},{24,8},{28,12},{1,17},{... | collective-permute-start | bytes 393224 | tf_op jit(solution)/shard_map/ppermute | solution.py:381
  24.2 2.3 %collective-permute-done.1.refs_1_ = bf16[64,1024]{1,0:T(8,128)(2,1)S(1)} collective-permute-done((bf16[64,1024]{1,0:T(8,128)(2,1)S(1)}, bf16[64,1024]{1,0:T(8,128)(2,1)S(1)}, u32[]{:S(2)}, u32[]{:S(2)}) %collective-permute-start.1) | collective-permute-done | bytes 131104 | tf_op jit(solution)/shard_map/ppermute | solution.py:381
  26.6 4.1 %collective-permute-done.2.refs_2_ = bf16[64,1024]{1,0:T(8,128)(2,1)S(1)} collective-permute-done((bf16[64,1024]{1,0:T(8,128)(2,1)S(1)}, bf16[64,1024]{1,0:T(8,128)(2,1)S(1)}, u32[]{:S(2)}, u32[]{:S(2)}) %collective-permute-start.2) | collective-permute-done | bytes 131104 | tf_op jit(solution)/shard_map/ppermute | solution.py:381
  30.7 1.4 %grad_radial.1 = (f32[64,512]{1,0:T(8,128)S(1)}, bf16[64,512]{1,0:T(8,128)(2,1)S(1)}, bf16[64,512]{1,0:T(8,128)(2,1)S(1)}, bf16[64,512]{1,0:T(8,128)(2,1)S(1)}) custom-call(s32[2]{0:T(128)S(1)} %pad_add_fusion.idx, bf16[256,1024]{1,0:T(8,128)(2,1)S(1)} %copy-done.7, bf16[256,1024]{1,0:T(8,128)(2,1)S(1)} %copy-done.6, f32[4,4,8,128]{3,2,1,0:T(8,128)S(1)} %copy-done.9, ...), custom_call_target="tpu_custom_call" | custom-call | flops 536870912 | bytes 2097152 | tf_op jit(solution)/shard_map/grad_radial/pallas_call | solution.py:364
  32.1 1.6 %collective-permute-start.4 = (bf16[64,512]{1,0:T(8,128)(2,1)S(1)}, bf16[64,512]{1,0:T(8,128)(2,1)S(1)}, u32[]{:S(2)}, u32[]{:S(2)}) collective-permute-start(bf16[64,512]{1,0:T(8,128)(2,1)S(1)} %get-tuple-element.38), channel_id=1, source_target_pairs={{0,1},{1,0},{2,3},{3,2},{4,5},{5,4},{6,7},{7,6},{8,9},{9,8},{10,11... | collective-permute-start | bytes 196616 | tf_op jit(solution)/shard_map/ppermute | solution.py:381
  33.8 2.6 %collective-permute-start.5 = (bf16[64,512]{1,0:T(8,128)(2,1)S(1)}, bf16[64,512]{1,0:T(8,128)(2,1)S(1)}, u32[]{:S(2)}, u32[]{:S(2)}) collective-permute-start(bf16[64,512]{1,0:T(8,128)(2,1)S(1)} %get-tuple-element.39), channel_id=1, source_target_pairs={{0,2},{1,3},{2,0},{3,1},{4,6},{5,7},{6,4},{7,5},{8,10},{9,11},{10,... | collective-permute-start | bytes 196616 | tf_op jit(solution)/shard_map/ppermute | solution.py:381
  37.1 3.3 %collective-permute-done.5.refs_2_ = bf16[64,512]{1,0:T(8,128)(2,1)S(1)} collective-permute-done((bf16[64,512]{1,0:T(8,128)(2,1)S(1)}, bf16[64,512]{1,0:T(8,128)(2,1)S(1)}, u32[]{:S(2)}, u32[]{:S(2)}) %collective-permute-start.5) | collective-permute-done | bytes 65568 | tf_op jit(solution)/shard_map/ppermute | solution.py:381
  40.3 2.1 %collective-permute-done.6.refs_3_ = bf16[64,512]{1,0:T(8,128)(2,1)S(1)} collective-permute-done((bf16[64,512]{1,0:T(8,128)(2,1)S(1)}, bf16[64,512]{1,0:T(8,128)(2,1)S(1)}, u32[]{:S(2)}, u32[]{:S(2)}) %collective-permute-start.6) | collective-permute-done | bytes 65568 | tf_op jit(solution)/shard_map/ppermute | solution.py:381
  42.4 4.6 %mode_grad.1 = (bf16[64,512]{1,0:T(8,128)(2,1)S(1)}, f32[8,2,32,128]{3,2,1,0:T(8,128)S(1)}) custom-call(s32[2]{0:T(128)S(1)} %pad_add_fusion.idx, bf16[8,32,64,128]{3,2,1,0:T(8,128)(2,1)S(1)} %copy-done, bf16[2048,128]{1,0:T(8,128)(2,1)S(1)} %copy-done.8, f32[64,512]{1,0:T(8,128)S(1)} %get-tuple-element.37.refs_0_, ...), custom_call_target="tpu_custom_call" | custom-call | flops 2147483648 | bytes 5373952 | tf_op jit(solution)/shard_map/mode_grad/pallas_call | solution.py:364
  47.0 1.0 %collective-permute-start.9 = (bf16[64,512]{1,0:T(8,128)(2,1)S(1)}, bf16[64,512]{1,0:T(8,128)(2,1)S(1)}, u32[]{:S(2)}, u32[]{:S(2)}) collective-permute-start(bf16[64,512]{1,0:T(8,128)(2,1)S(1)} %get-tuple-element.41.refs_0_), channel_id=1, source_target_pairs={{0,3},{1,2},{2,1},{3,0},{4,7},{5,6},{6,5},{7,4},{8,11},{9,10},{10,... | collective-permute-start | bytes 196616 | tf_op jit(solution)/shard_map/ppermute | solution.py:381
  48.2 1.5 %collective-permute-start.18 = (bf16[80,1024]{1,0:T(8,128)(2,1)S(1)}, bf16[80,1024]{1,0:T(8,128)(2,1)S(1)}, u32[]{:S(2)}, u32[]{:S(2)}) collective-permute-start(bf16[80,1024]{1,0:T(8,128)(2,1)S(1)} %get-tuple-element.46), channel_id=1, source_target_pairs={{0,8},{4,12},{8,0},{12,4},{16,24},{20,28},{24,16},{28,20},{1,9},{5... | collective-permute-start | bytes 491528 | tf_op jit(solution)/shard_map/ppermute | solution.py:381
  50.4 1.4 %collective-permute-start.20 = (bf16[80,1024]{1,0:T(8,128)(2,1)S(1)}, bf16[80,1024]{1,0:T(8,128)(2,1)S(1)}, u32[]{:S(2)}, u32[]{:S(2)}) collective-permute-start(bf16[80,1024]{1,0:T(8,128)(2,1)S(1)} %get-tuple-element.48), channel_id=1, source_target_pairs={{0,24},{4,28},{8,16},{12,20},{16,8},{20,12},{24,0},{28,4},{1,25},{... | collective-permute-start | bytes 491528 | tf_op jit(solution)/shard_map/ppermute | solution.py:381
  51.8 1.6 %collective-permute-done.9.refs_3_ = bf16[64,512]{1,0:T(8,128)(2,1)S(1)} collective-permute-done((bf16[64,512]{1,0:T(8,128)(2,1)S(1)}, bf16[64,512]{1,0:T(8,128)(2,1)S(1)}, u32[]{:S(2)}, u32[]{:S(2)}) %collective-permute-start.9) | collective-permute-done | bytes 65568 | tf_op jit(solution)/shard_map/ppermute | solution.py:381
  53.4 1.9 %collective-permute-start.7 = (bf16[64,512]{1,0:T(8,128)(2,1)S(1)}, bf16[64,512]{1,0:T(8,128)(2,1)S(1)}, u32[]{:S(2)}, u32[]{:S(2)}) collective-permute-start(bf16[64,512]{1,0:T(8,128)(2,1)S(1)} %get-tuple-element.41.refs_0_), channel_id=1, source_target_pairs={{0,1},{1,0},{2,3},{3,2},{4,5},{5,4},{6,7},{7,6},{8,9},{9,8},{10,11... | collective-permute-start | bytes 196616 | tf_op jit(solution)/shard_map/ppermute | solution.py:381
  55.3 2.5 %collective-permute-done.8.refs_2_ = bf16[64,512]{1,0:T(8,128)(2,1)S(1)} collective-permute-done((bf16[64,512]{1,0:T(8,128)(2,1)S(1)}, bf16[64,512]{1,0:T(8,128)(2,1)S(1)}, u32[]{:S(2)}, u32[]{:S(2)}) %collective-permute-start.8) | collective-permute-done | bytes 65568 | tf_op jit(solution)/shard_map/ppermute | solution.py:381
  58.3 2.0 %back_radial.1.refs_0_ = bf16[64,1024]{1,0:T(8,128)(2,1)S(1)} custom-call(s32[2]{0:T(128)S(1)} %pad_add_fusion.idx, bf16[256,1024]{1,0:T(8,128)(2,1)S(1)} %copy-done.7, bf16[256,1024]{1,0:T(8,128)(2,1)S(1)} %copy-done.6, f32[4,4,8,128]{3,2,1,0:T(8,128)S(1)} %copy-done.9, bf16[64,512]{1,0:T(8,128)(2,1)S(1)} %get-tuple-element.41.refs_0_, ...), custom_call_target="tpu_custom_call" | custom-call | flops 536870912 | bytes 1507328 | tf_op jit(solution)/shard_map/back_radial/pallas_call | solution.py:364
  60.3 1.6 %collective-permute-start.15 = (bf16[64,1024]{1,0:T(8,128)(2,1)S(1)}, bf16[64,1024]{1,0:T(8,128)(2,1)S(1)}, u32[]{:S(2)}, u32[]{:S(2)}) collective-permute-start(bf16[64,1024]{1,0:T(8,128)(2,1)S(1)} %back_radial.1.refs_0_), channel_id=1, source_target_pairs={{0,24},{4,28},{8,16},{12,20},{16,8},{20,12},{24,0},{28,4},{1,25},{... | collective-permute-start | bytes 393224 | tf_op jit(solution)/shard_map/ppermute | solution.py:381
  61.8 1.3 %collective-permute-start.13 = (bf16[64,1024]{1,0:T(8,128)(2,1)S(1)}, bf16[64,1024]{1,0:T(8,128)(2,1)S(1)}, u32[]{:S(2)}, u32[]{:S(2)}) collective-permute-start(bf16[64,1024]{1,0:T(8,128)(2,1)S(1)} %back_radial.1.refs_0_), channel_id=1, source_target_pairs={{0,16},{4,20},{8,24},{12,28},{16,0},{20,4},{24,8},{28,12},{1,17},{... | collective-permute-start | bytes 393224 | tf_op jit(solution)/shard_map/ppermute | solution.py:381
  63.8 1.4 %input_radial.1 = (f32[80,512]{1,0:T(8,128)S(1)}, bf16[80,512]{1,0:T(8,128)(2,1)S(1)}, bf16[80,512]{1,0:T(8,128)(2,1)S(1)}, bf16[80,512]{1,0:T(8,128)(2,1)S(1)}) custom-call(s32[2]{0:T(128)S(1)} %pad_add_fusion.idx, bf16[256,1024]{1,0:T(8,128)(2,1)S(1)} %copy-done.7, bf16[256,1024]{1,0:T(8,128)(2,1)S(1)} %copy-done.6, f32[4,4,8,128]{3,2,1,0:T(8,128)S(1)} %copy-done.9, ...), custom_call_target="tpu_custom_call" | custom-call | flops 536870912 | bytes 2342912 | tf_op jit(solution)/shard_map/input_radial/pallas_call | solution.py:364
  65.3 1.3 %collective-permute-start.21 = (bf16[80,512]{1,0:T(8,128)(2,1)S(1)}, bf16[80,512]{1,0:T(8,128)(2,1)S(1)}, u32[]{:S(2)}, u32[]{:S(2)}) collective-permute-start(bf16[80,512]{1,0:T(8,128)(2,1)S(1)} %get-tuple-element.50), channel_id=1, source_target_pairs={{0,1},{1,0},{2,3},{3,2},{4,5},{5,4},{6,7},{7,6},{8,9},{9,8},{10,11... | collective-permute-start | bytes 245768 | tf_op jit(solution)/shard_map/ppermute | solution.py:381
  66.6 0.9 collective-permute-start.22
  67.5 2.3 %collective-permute-done.21.refs_1_ = bf16[80,512]{1,0:T(8,128)(2,1)S(1)} collective-permute-done((bf16[80,512]{1,0:T(8,128)(2,1)S(1)}, bf16[80,512]{1,0:T(8,128)(2,1)S(1)}, u32[]{:S(2)}, u32[]{:S(2)}) %collective-permute-start.21) | collective-permute-done | bytes 81952 | tf_op jit(solution)/shard_map/ppermute | solution.py:381
  69.8 3.0 %collective-permute-done.22.refs_2_ = bf16[80,512]{1,0:T(8,128)(2,1)S(1)} collective-permute-done((bf16[80,512]{1,0:T(8,128)(2,1)S(1)}, bf16[80,512]{1,0:T(8,128)(2,1)S(1)}, u32[]{:S(2)}, u32[]{:S(2)}) %collective-permute-start.22) | collective-permute-done | bytes 81952 | tf_op jit(solution)/shard_map/ppermute | solution.py:381
  73.4 4.8 %pointwise.1.point_ref = f32[1024,1024]{1,0:T(8,128)} custom-call(bf16[64,64]{1,0:T(8,128)(2,1)S(1)} %copy-done.2, bf16[1024,1024]{1,0:T(8,128)(2,1)S(1)} %copy-done.10), custom_call_target="tpu_custom_call" | custom-call | flops 2147483648 | bytes 6299648 | tf_op jit(solution)/shard_map/pointwise/pallas_call | solution.py:364
  79.0 7.6 %spectral_outer.1 = (f32[8,32,64,128]{3,2,1,0:T(8,128)}, f32[64,64]{1,0:T(8,128)}) custom-call(f32[8,2,32,128]{3,2,1,0:T(8,128)S(1)} %get-tuple-element.42.dy_ref, f32[80,512]{1,0:T(8,128)S(1)} %get-tuple-element.49.refs_0_, bf16[80,512]{1,0:T(8,128)(2,1)S(1)} %collective-permute-done.21.refs_1_, bf16[80,512]{1,0:T(8,128)(2,1)S(1)} %collective-permute-done.22.refs_2_, ...), custom_call_target="tpu_custom_call" | custom-call | flops 1073741824 | bytes 9076736 | tf_op jit(solution)/shard_map/spectral_outer/pallas_call | solution.py:364
  86.6 5.7 %final_axial.1 = bf16[1024,1024]{1,0:T(8,128)(2,1)} custom-call(s32[2]{0:T(128)S(1)} %pad_add_fusion.idx, bf16[512,1024]{1,0:T(8,128)(2,1)S(1)} %get-tuple-element.29.t_ref, f32[1024,1024]{1,0:T(8,128)} %pointwise.1.point_ref, bf16[64,1024]{1,0:T(8,128)(2,1)S(1)} %back_radial.1.refs_0_, bf16[64,1024]{1,0:T(8,128)(2,1)S(1)} %collective-permute-done.10.refs_1_, ...), custom_call_target="tpu_custom_call" | custom-call | flops 1073741824 | bytes 8388608 | tf_op jit(solution)/shard_map/final_axial/pallas_call | solution.py:364
  (50 shorter events, 5.1 us)
Async XLA Ops:
  4.4 7.1 %copy-start.1 = (bf16[64,16,1024]{2,1,0:T(8,128)(2,1)S(1)}, bf16[64,16,1024]{2,1,0:T(8,128)(2,1)}, u32[]{:S(2)}) copy-start(bf16[64,16,1024]{2,1,0:T(8,128)(2,1)} %param.12) | copy-start | bytes 6291460
  11.0 8.5 %collective-permute-start = (bf16[4,64,1024]{2,1,0:T(8,128)(2,1)S(1)}, bf16[4,64,1024]{2,1,0:T(8,128)(2,1)S(1)}, u32[]{:S(2)}, u32[]{:S(2)}) collective-permute-start(bf16[4,64,1024]{2,1,0:T(8,128)(2,1)S(1)} %get-tuple-element.32), channel_id=1, source_target_pairs={{0,4},{4,0},{8,12},{12,8},{16,20},{20,16},{24,28},{28,24},{1,5},{5... | collective-permute-start | bytes 1572872 | tf_op jit(solution)/shard_map/ppermute | solution.py:381
  11.5 19.2 %copy-start.6 = (bf16[256,1024]{1,0:T(8,128)(2,1)S(1)}, bf16[256,1024]{1,0:T(8,128)(2,1)}, u32[]{:S(2)}) copy-start(bf16[256,1024]{1,0:T(8,128)(2,1)} %constant.27.clone.low_ref) | copy-start | bytes 1572868
  11.5 19.2 %copy-start.7 = (bf16[256,1024]{1,0:T(8,128)(2,1)S(1)}, bf16[256,1024]{1,0:T(8,128)(2,1)}, u32[]{:S(2)}) copy-start(bf16[256,1024]{1,0:T(8,128)(2,1)} %constant.26.clone.high_ref) | copy-start | bytes 1572868
  11.5 19.2 %copy-start.9 = (f32[4,4,8,128]{3,2,1,0:T(8,128)S(1)}, f32[4,4,8,128]{3,2,1,0:T(8,128)}, u32[]{:S(2)}) copy-start(f32[4,4,8,128]{3,2,1,0:T(8,128)} %constant.28.clone.shift_ref) | copy-start | bytes 196612
  11.5 30.9 %copy-start = (bf16[8,32,64,128]{3,2,1,0:T(8,128)(2,1)S(1)}, bf16[8,32,64,128]{3,2,1,0:T(8,128)(2,1)}, u32[]{:S(2)}) copy-start(bf16[8,32,64,128]{3,2,1,0:T(8,128)(2,1)} %w_ref.3) | copy-start | bytes 12582916
  19.4 23.0 %copy-start.8 = (bf16[2048,128]{1,0:T(8,128)(2,1)S(1)}, bf16[2048,128]{1,0:T(8,128)(2,1)}, u32[]{:S(2)}) copy-start(bf16[2048,128]{1,0:T(8,128)(2,1)} %constant.29.clone.e_ref) | copy-start | bytes 1572868
  19.4 28.6 %collective-permute-start.17 = (bf16[4,80,1024]{2,1,0:T(8,128)(2,1)S(1)}, bf16[4,80,1024]{2,1,0:T(8,128)(2,1)S(1)}, u32[]{:S(2)}, u32[]{:S(2)}) collective-permute-start(bf16[4,80,1024]{2,1,0:T(8,128)(2,1)S(1)} %get-tuple-element.44), channel_id=1, source_target_pairs={{0,4},{4,0},{8,12},{12,8},{16,20},{20,16},{24,28},{28,24},{1,5},{5... | collective-permute-start | bytes 1966088 | tf_op jit(solution)/shard_map/ppermute | solution.py:381
  19.7 6.9 %collective-permute-start.1 = (bf16[64,1024]{1,0:T(8,128)(2,1)S(1)}, bf16[64,1024]{1,0:T(8,128)(2,1)S(1)}, u32[]{:S(2)}, u32[]{:S(2)}) collective-permute-start(bf16[64,1024]{1,0:T(8,128)(2,1)S(1)} %get-tuple-element.34), channel_id=1, source_target_pairs={{0,8},{4,12},{8,0},{12,4},{16,24},{20,28},{24,16},{28,20},{1,9},{5... | collective-permute-start | bytes 393224 | tf_op jit(solution)/shard_map/ppermute | solution.py:381
  22.7 8.0 %collective-permute-start.2 = (bf16[64,1024]{1,0:T(8,128)(2,1)S(1)}, bf16[64,1024]{1,0:T(8,128)(2,1)S(1)}, u32[]{:S(2)}, u32[]{:S(2)}) collective-permute-start(bf16[64,1024]{1,0:T(8,128)(2,1)S(1)} %get-tuple-element.35), channel_id=1, source_target_pairs={{0,16},{4,20},{8,24},{12,28},{16,0},{20,4},{24,8},{28,12},{1,17},{... | collective-permute-start | bytes 393224 | tf_op jit(solution)/shard_map/ppermute | solution.py:381
  24.2 6.5 %collective-permute-start.3 = (bf16[64,1024]{1,0:T(8,128)(2,1)S(1)}, bf16[64,1024]{1,0:T(8,128)(2,1)S(1)}, u32[]{:S(2)}, u32[]{:S(2)}) collective-permute-start(bf16[64,1024]{1,0:T(8,128)(2,1)S(1)} %get-tuple-element.36), channel_id=1, source_target_pairs={{0,24},{4,28},{8,16},{12,20},{16,8},{20,12},{24,0},{28,4},{1,25},{... | collective-permute-start | bytes 393224 | tf_op jit(solution)/shard_map/ppermute | solution.py:381
  32.1 5.0 %collective-permute-start.4 = (bf16[64,512]{1,0:T(8,128)(2,1)S(1)}, bf16[64,512]{1,0:T(8,128)(2,1)S(1)}, u32[]{:S(2)}, u32[]{:S(2)}) collective-permute-start(bf16[64,512]{1,0:T(8,128)(2,1)S(1)} %get-tuple-element.38), channel_id=1, source_target_pairs={{0,1},{1,0},{2,3},{3,2},{4,5},{5,4},{6,7},{7,6},{8,9},{9,8},{10,11... | collective-permute-start | bytes 196616 | tf_op jit(solution)/shard_map/ppermute | solution.py:381
  33.8 6.6 %collective-permute-start.5 = (bf16[64,512]{1,0:T(8,128)(2,1)S(1)}, bf16[64,512]{1,0:T(8,128)(2,1)S(1)}, u32[]{:S(2)}, u32[]{:S(2)}) collective-permute-start(bf16[64,512]{1,0:T(8,128)(2,1)S(1)} %get-tuple-element.39), channel_id=1, source_target_pairs={{0,2},{1,3},{2,0},{3,1},{4,6},{5,7},{6,4},{7,5},{8,10},{9,11},{10,... | collective-permute-start | bytes 196616 | tf_op jit(solution)/shard_map/ppermute | solution.py:381
  36.4 6.1 %collective-permute-start.6 = (bf16[64,512]{1,0:T(8,128)(2,1)S(1)}, bf16[64,512]{1,0:T(8,128)(2,1)S(1)}, u32[]{:S(2)}, u32[]{:S(2)}) collective-permute-start(bf16[64,512]{1,0:T(8,128)(2,1)S(1)} %get-tuple-element.40), channel_id=1, source_target_pairs={{0,3},{1,2},{2,1},{3,0},{4,7},{5,6},{6,5},{7,4},{8,11},{9,10},{10,... | collective-permute-start | bytes 196616 | tf_op jit(solution)/shard_map/ppermute | solution.py:381
  47.0 6.4 %collective-permute-start.9 = (bf16[64,512]{1,0:T(8,128)(2,1)S(1)}, bf16[64,512]{1,0:T(8,128)(2,1)S(1)}, u32[]{:S(2)}, u32[]{:S(2)}) collective-permute-start(bf16[64,512]{1,0:T(8,128)(2,1)S(1)} %get-tuple-element.41.refs_0_), channel_id=1, source_target_pairs={{0,3},{1,2},{2,1},{3,0},{4,7},{5,6},{6,5},{7,4},{8,11},{9,10},{10,... | collective-permute-start | bytes 196616 | tf_op jit(solution)/shard_map/ppermute | solution.py:381
  48.2 25.2 %copy-start.2 = (bf16[64,64]{1,0:T(8,128)(2,1)S(1)}, bf16[64,64]{1,0:T(8,128)(2,1)}, u32[]{:S(2)}) copy-start(bf16[64,64]{1,0:T(8,128)(2,1)} %w_ref.2) | copy-start | bytes 24580
  48.2 25.2 %copy-start.10 = (bf16[1024,1024]{1,0:T(8,128)(2,1)S(1)}, bf16[1024,1024]{1,0:T(8,128)(2,1)}, u32[]{:S(2)}) copy-start(bf16[1024,1024]{1,0:T(8,128)(2,1)} %get-tuple-element.30.g_ref) | copy-start | bytes 6291460
  48.2 14.9 %collective-permute-start.18 = (bf16[80,1024]{1,0:T(8,128)(2,1)S(1)}, bf16[80,1024]{1,0:T(8,128)(2,1)S(1)}, u32[]{:S(2)}, u32[]{:S(2)}) collective-permute-start(bf16[80,1024]{1,0:T(8,128)(2,1)S(1)} %get-tuple-element.46), channel_id=1, source_target_pairs={{0,8},{4,12},{8,0},{12,4},{16,24},{20,28},{24,16},{28,20},{1,9},{5... | collective-permute-start | bytes 491528 | tf_op jit(solution)/shard_map/ppermute | solution.py:381
  49.8 14.1 %collective-permute-start.19 = (bf16[80,1024]{1,0:T(8,128)(2,1)S(1)}, bf16[80,1024]{1,0:T(8,128)(2,1)S(1)}, u32[]{:S(2)}, u32[]{:S(2)}) collective-permute-start(bf16[80,1024]{1,0:T(8,128)(2,1)S(1)} %get-tuple-element.47), channel_id=1, source_target_pairs={{0,16},{4,20},{8,24},{12,28},{16,0},{20,4},{24,8},{28,12},{1,17},{... | collective-permute-start | bytes 491528 | tf_op jit(solution)/shard_map/ppermute | solution.py:381
  50.4 13.5 %collective-permute-start.20 = (bf16[80,1024]{1,0:T(8,128)(2,1)S(1)}, bf16[80,1024]{1,0:T(8,128)(2,1)S(1)}, u32[]{:S(2)}, u32[]{:S(2)}) collective-permute-start(bf16[80,1024]{1,0:T(8,128)(2,1)S(1)} %get-tuple-element.48), channel_id=1, source_target_pairs={{0,24},{4,28},{8,16},{12,20},{16,8},{20,12},{24,0},{28,4},{1,25},{... | collective-permute-start | bytes 491528 | tf_op jit(solution)/shard_map/ppermute | solution.py:381
  51.8 6.0 %collective-permute-start.8 = (bf16[64,512]{1,0:T(8,128)(2,1)S(1)}, bf16[64,512]{1,0:T(8,128)(2,1)S(1)}, u32[]{:S(2)}, u32[]{:S(2)}) collective-permute-start(bf16[64,512]{1,0:T(8,128)(2,1)S(1)} %get-tuple-element.41.refs_0_), channel_id=1, source_target_pairs={{0,2},{1,3},{2,0},{3,1},{4,6},{5,7},{6,4},{7,5},{8,10},{9,11},{10,... | collective-permute-start | bytes 196616 | tf_op jit(solution)/shard_map/ppermute | solution.py:381
  53.4 4.9 %collective-permute-start.7 = (bf16[64,512]{1,0:T(8,128)(2,1)S(1)}, bf16[64,512]{1,0:T(8,128)(2,1)S(1)}, u32[]{:S(2)}, u32[]{:S(2)}) collective-permute-start(bf16[64,512]{1,0:T(8,128)(2,1)S(1)} %get-tuple-element.41.refs_0_), channel_id=1, source_target_pairs={{0,1},{1,0},{2,3},{3,2},{4,5},{5,4},{6,7},{7,6},{8,9},{9,8},{10,11... | collective-permute-start | bytes 196616 | tf_op jit(solution)/shard_map/ppermute | solution.py:381
  60.3 12.6 %collective-permute-start.15 = (bf16[64,1024]{1,0:T(8,128)(2,1)S(1)}, bf16[64,1024]{1,0:T(8,128)(2,1)S(1)}, u32[]{:S(2)}, u32[]{:S(2)}) collective-permute-start(bf16[64,1024]{1,0:T(8,128)(2,1)S(1)} %back_radial.1.refs_0_), channel_id=1, source_target_pairs={{0,24},{4,28},{8,16},{12,20},{16,8},{20,12},{24,0},{28,4},{1,25},{... | collective-permute-start | bytes 393224 | tf_op jit(solution)/shard_map/ppermute | solution.py:381
  61.8 11.0 %collective-permute-start.13 = (bf16[64,1024]{1,0:T(8,128)(2,1)S(1)}, bf16[64,1024]{1,0:T(8,128)(2,1)S(1)}, u32[]{:S(2)}, u32[]{:S(2)}) collective-permute-start(bf16[64,1024]{1,0:T(8,128)(2,1)S(1)} %back_radial.1.refs_0_), channel_id=1, source_target_pairs={{0,16},{4,20},{8,24},{12,28},{16,0},{20,4},{24,8},{28,12},{1,17},{... | collective-permute-start | bytes 393224 | tf_op jit(solution)/shard_map/ppermute | solution.py:381
  63.1 10.3 %collective-permute-start.11 = (bf16[64,1024]{1,0:T(8,128)(2,1)S(1)}, bf16[64,1024]{1,0:T(8,128)(2,1)S(1)}, u32[]{:S(2)}, u32[]{:S(2)}) collective-permute-start(bf16[64,1024]{1,0:T(8,128)(2,1)S(1)} %back_radial.1.refs_0_), channel_id=1, source_target_pairs={{0,8},{4,12},{8,0},{12,4},{16,24},{20,28},{24,16},{28,20},{1,9},{5... | collective-permute-start | bytes 393224 | tf_op jit(solution)/shard_map/ppermute | solution.py:381
  65.3 4.5 %collective-permute-start.21 = (bf16[80,512]{1,0:T(8,128)(2,1)S(1)}, bf16[80,512]{1,0:T(8,128)(2,1)S(1)}, u32[]{:S(2)}, u32[]{:S(2)}) collective-permute-start(bf16[80,512]{1,0:T(8,128)(2,1)S(1)} %get-tuple-element.50), channel_id=1, source_target_pairs={{0,1},{1,0},{2,3},{3,2},{4,5},{5,4},{6,7},{7,6},{8,9},{9,8},{10,11... | collective-permute-start | bytes 245768 | tf_op jit(solution)/shard_map/ppermute | solution.py:381
  66.6 6.2 %collective-permute-start.22 = (bf16[80,512]{1,0:T(8,128)(2,1)S(1)}, bf16[80,512]{1,0:T(8,128)(2,1)S(1)}, u32[]{:S(2)}, u32[]{:S(2)}) collective-permute-start(bf16[80,512]{1,0:T(8,128)(2,1)S(1)} %get-tuple-element.51), channel_id=1, source_target_pairs={{0,2},{1,3},{2,0},{3,1},{4,6},{5,7},{6,4},{7,5},{8,10},{9,11},{10,... | collective-permute-start | bytes 245768 | tf_op jit(solution)/shard_map/ppermute | solution.py:381
  69.8 16.8 %collective-permute-start.10 = (bf16[64,1024]{1,0:T(8,128)(2,1)S(1)}, bf16[64,1024]{1,0:T(8,128)(2,1)S(1)}, u32[]{:S(2)}, u32[]{:S(2)}) collective-permute-start(bf16[64,1024]{1,0:T(8,128)(2,1)S(1)} %back_radial.1.refs_0_), channel_id=1, source_target_pairs={{0,4},{4,0},{8,12},{12,8},{16,20},{20,16},{24,28},{28,24},{1,5},{5... | collective-permute-start | bytes 393224 | tf_op jit(solution)/shard_map/ppermute | solution.py:381
  72.8 6.2 %collective-permute-start.23 = (bf16[80,512]{1,0:T(8,128)(2,1)S(1)}, bf16[80,512]{1,0:T(8,128)(2,1)S(1)}, u32[]{:S(2)}, u32[]{:S(2)}) collective-permute-start(bf16[80,512]{1,0:T(8,128)(2,1)S(1)} %get-tuple-element.52), channel_id=1, source_target_pairs={{0,3},{1,2},{2,1},{3,0},{4,7},{5,6},{6,5},{7,4},{8,11},{9,10},{10,... | collective-permute-start | bytes 245768 | tf_op jit(solution)/shard_map/ppermute | solution.py:381
  72.8 13.8 %collective-permute-start.16 = (bf16[64,1024]{1,0:T(8,128)(2,1)S(1)}, bf16[64,1024]{1,0:T(8,128)(2,1)S(1)}, u32[]{:S(2)}, u32[]{:S(2)}) collective-permute-start(bf16[64,1024]{1,0:T(8,128)(2,1)S(1)} %collective-permute-done.15.refs_6_), channel_id=1, source_target_pairs={{0,4},{4,0},{8,12},{12,8},{16,20},{20,16},{24,28},{28,24},{1,5},{5... | collective-permute-start | bytes 393224 | tf_op jit(solution)/shard_map/ppermute | solution.py:381
  72.8 13.8 %collective-permute-start.14 = (bf16[64,1024]{1,0:T(8,128)(2,1)S(1)}, bf16[64,1024]{1,0:T(8,128)(2,1)S(1)}, u32[]{:S(2)}, u32[]{:S(2)}) collective-permute-start(bf16[64,1024]{1,0:T(8,128)(2,1)S(1)} %collective-permute-done.13.refs_4_), channel_id=1, source_target_pairs={{0,4},{4,0},{8,12},{12,8},{16,20},{20,16},{24,28},{28,24},{1,5},{5... | collective-permute-start | bytes 393224 | tf_op jit(solution)/shard_map/ppermute | solution.py:381
  73.3 13.3 %collective-permute-start.12 = (bf16[64,1024]{1,0:T(8,128)(2,1)S(1)}, bf16[64,1024]{1,0:T(8,128)(2,1)S(1)}, u32[]{:S(2)}, u32[]{:S(2)}) collective-permute-start(bf16[64,1024]{1,0:T(8,128)(2,1)S(1)} %collective-permute-done.11.refs_2_), channel_id=1, source_target_pairs={{0,4},{4,0},{8,12},{12,8},{16,20},{20,16},{24,28},{28,24},{1,5},{5... | collective-permute-start | bytes 393224 | tf_op jit(solution)/shard_map/ppermute | solution.py:381
  (3 other events, 3.7 us)

commit v2 on v1

v2 whole, which is shorter than its diff:
```python
import functools
import math

import jax
import jax.numpy as jnp
import ml_dtypes
import numpy as np
from jax import lax
from jax.experimental import pallas as pl
from jax.experimental.pallas import tpu as pltpu
from jax.sharding import PartitionSpec as P

KA = 256
KR = 32
F32 = jnp.float32
BF16 = jnp.bfloat16


def dot(a, b, dims=((1,), (0,))):
    return lax.dot_general(a, b, (dims, ((), ())), preferred_element_type=F32)


def tree_sum(values):
    while len(values) > 1:
        values = [values[i] + values[i + 1] for i in range(0, len(values), 2)]
    return values[0]


def split(value):
    high = value.astype(BF16)
    return high, (value - high.astype(F32)).astype(BF16)


class Sizes:
    def __init__(self, channels, rows, cols, n_axial, n_radial):
        self.c, self.r, self.a = channels, rows, cols
        self.n_axial, self.n_radial = n_axial, n_radial
        self.chips = n_axial // 2
        self.own = KA // n_axial
        self.j = 2 * self.own
        self.cr = channels * rows
        self.qo = KR // n_radial
        self.cg = 128 // self.qo
        self.ng = channels // self.cg
        self.kb = self.cg * rows
        self.half = KR * self.cg
        self.lanes = self.qo * channels
        self.blk = 256
        self.nblk = self.cr // self.blk
        self.axial_total = cols * n_axial
        self.radial_total = rows * n_radial
        self.ride = 8
        self.ride_b = channels * 128 // self.lanes


def axial_base(z):
    k = np.arange(KA, dtype=np.int64)
    a = np.arange(128, dtype=np.int64)
    m = (k[:, None] * a[None, :]) % z.axial_total
    phase = m * (2.0 * np.pi / z.axial_total)
    return np.stack([np.cos(phase), np.sin(phase)]).astype(np.float32)


def axial_shift(z):
    k = np.arange(KA, dtype=np.int64)
    n = z.a // 128
    first = np.arange(z.n_axial * n, dtype=np.int64).reshape(z.n_axial, n) * 128
    m = (first[:, :, None] * k) % z.axial_total
    phase = m * (2.0 * np.pi / z.axial_total)
    return np.concatenate([np.cos(phase), np.sin(phase)], axis=1).astype(np.float32)


def radial_freqs(z):
    q = np.arange(KR, dtype=np.int64)
    return q + np.where(q >= KR // 2, z.radial_total - KR, 0)


def radial_base(z):
    g = radial_freqs(z)
    r = np.arange(z.r, dtype=np.int64)
    m = (g[:, None] * r[None, :]) % z.radial_total
    phase = m * (2.0 * np.pi / z.radial_total)
    eye = np.eye(z.cg, dtype=np.float64)
    parts = [
        np.einsum("rq,cd->crqd", f(phase).T, eye).reshape(z.kb, z.half) for f in (np.cos, np.sin)
    ]
    table = np.concatenate(parts, axis=1).astype(np.float32)
    high = table.astype(ml_dtypes.bfloat16)
    low = (table - high.astype(np.float32)).astype(ml_dtypes.bfloat16)
    return high, low


def radial_shift(z):
    g = radial_freqs(z)
    first = np.arange(z.n_radial, dtype=np.int64) * z.r
    m = (first[:, None] * g[None, :]) % z.radial_total
    phase = m * (2.0 * np.pi / z.radial_total)
    out = np.zeros((z.n_radial, z.n_radial, 8, 128), np.float32)
    for row, f in ((0, np.cos), (1, np.sin)):
        lanes = np.repeat(f(phase), z.cg, axis=1)
        out[:, :, row, :] = lanes.reshape(z.n_radial, z.n_radial, 128)
    return out


def lane_sums():
    out = np.zeros((8, 2, 128, 128), np.float32)
    for kk in range(8):
        for h in range(2):
            out[kk, h, :, h * 64 + kk] = 1.0
    return out.reshape(2048, 128).astype(ml_dtypes.bfloat16)


def gelu_slope(value):
    return 0.5 * (1.0 + lax.erf(value * (1.0 / math.sqrt(2.0)))) + value * jnp.exp(
        -0.5 * value * value
    ) * (1.0 / math.sqrt(2.0 * math.pi))


def split_owners(z, idx, part, keep_ref, send_ref, stage):
    for o in range(z.n_axial):
        stage[o] = part[o * z.j : (o + 1) * z.j, :].astype(BF16)
    chip, core = idx[0] // 2, idx[0] % 2
    for d in range(z.chips):
        keep_ref[d] = stage[(chip ^ d) * 2 + core]
        send_ref[d] = stage[(chip ^ d) * 2 + (1 - core)]


def grad_kernel(z, idx, base_ref, shift_ref, pre_ref, cot_ref, g_ref, t_ref, keep_ref, send_ref, stage):
    step = pl.program_id(0)

    @pl.when(step == 0)
    def _():
        n = z.a // 128
        shift = shift_ref[0]
        shift = jnp.concatenate([shift, jnp.zeros((128 - 2 * n, KA), F32)], axis=0).T
        cos1, sin1 = base_ref[0], base_ref[1]
        for i in range(n):
            cos2, sin2 = shift[:, i : i + 1], shift[:, n + i : n + i + 1]
            real = (cos1 * cos2 - sin1 * sin2).astype(BF16)
            imag = (-(sin1 * cos2 + cos1 * sin2)).astype(BF16)
            lanes = slice(i * 128, (i + 1) * 128)
            for o in range(z.n_axial):
                rows = slice(o * z.own, (o + 1) * z.own)
                t_ref[o * z.j : o * z.j + z.own, lanes] = real[rows]
                t_ref[o * z.j + z.own : (o + 1) * z.j, lanes] = imag[rows]

    g = (cot_ref[...].astype(F32) * gelu_slope(pre_ref[...].astype(F32))).astype(BF16)
    rows = pl.ds(pl.multiple_of(step * z.blk, z.blk), z.blk)
    g_ref[rows, :] = g
    part = dot(t_ref[...], g, ((1,), (1,)))
    split_owners(z, idx, part, keep_ref.at[:, :, rows], send_ref.at[:, :, rows], stage)


def input_kernel(z, idx, t_ref, x_ref, keep_ref, send_ref, stage):
    for b in range(z.nblk):
        rows = slice(b * z.blk, (b + 1) * z.blk)
        part = dot(t_ref[...], x_ref[rows, :], ((1,), (1,)))
        split_owners(z, idx, part, keep_ref.at[:, :, rows], send_ref.at[:, :, rows], stage.at[b])


def weight_kernel(z, x_ref, g_ref, *refs):
    out_ref = refs[-1]
    nc = z.blk // z.r
    row = lax.broadcasted_iota(jnp.int32, (z.blk, z.cr), 0)
    col = lax.broadcasted_iota(jnp.int32, (z.blk, z.cr), 1)
    same = ((row ^ col) & (z.r - 1)) == 0
    col = lax.broadcasted_iota(jnp.int32, (z.cr, 128), 0) // z.r
    lane = lax.broadcasted_iota(jnp.int32, (z.cr, 128), 1) & (z.c - 1)
    pick = (col == lane).astype(F32).astype(BF16)
    sums = []
    for b in range(z.nblk):
        cross = dot(x_ref[b * z.blk : (b + 1) * z.blk, :], g_ref[...], ((1,), (1,)))
        cross = jnp.where(same, cross, 0.0)
        sums.append(jnp.sum(cross.reshape(nc, z.r, z.cr), axis=1))
    high, low = split(jnp.concatenate(sums, axis=0))
    w = high_low(z, dot(high, pick) + dot(low, pick))
    w = [w[i * 8 : (i + 1) * 8] for i in range(z.cr // 128)]
    out_ref[...] = jnp.concatenate(w, axis=1).astype(BF16)


def high_low(z, both):
    lane = lax.broadcasted_iota(jnp.int32, both.shape, 1) & 127
    high = both.astype(BF16).astype(F32)
    return jnp.where(lane < z.c, high, both - high)


def fold(block):
    return block + pltpu.roll(block, 64, 1)


def fold_all(z, value):
    n = value.shape[1] // 128
    return [high_low(z, fold(value[:, i * 128 : (i + 1) * 128])) for i in range(n)]


def add_kernel(z, keep_ref, recv_ref, *refs):
    outs = refs[-z.chips :]
    for d, out in enumerate(outs):
        total = keep_ref[d].astype(F32) + recv_ref[d].astype(F32)
        out[: z.j, :] = total.astype(out.dtype)
        if out.shape[0] > z.j:
            out[z.j :, :] = refs[0][...].astype(out.dtype)


def radial_kernel(z, idx, high_ref, low_ref, shift_ref, *refs):
    pieces, outs, stage = refs[: z.chips], refs[-1 - z.n_radial : -1], refs[-1]
    me = idx[1]
    value = tree_sum([p[: z.j, :].astype(F32) for p in pieces])
    for g in range(z.ng):
        high, low = split(value[:, g * z.kb : (g + 1) * z.kb])
        both = dot(jnp.concatenate([high, low], axis=0), high_ref[...])
        total = both[: z.j] + both[z.j :] + dot(high, low_ref[...])
        c, s = total[:, : z.half], total[:, z.half :]
        real = c[: z.own] + s[z.own :]
        imag = c[z.own :] - s[: z.own]
        for zz in range(z.n_radial):
            cos, sin = shift_ref[me, zz, 0:1, :], shift_ref[me, zz, 1:2, :]
            lanes = slice(zz * 128, (zz + 1) * 128)
            re, im = real[:, lanes], imag[:, lanes]
            stage[zz, : z.own, g * 128 : (g + 1) * 128] = cos * re + sin * im
            stage[zz, z.own : z.j, g * 128 : (g + 1) * 128] = cos * im - sin * re
    for d, out in enumerate(outs):
        out[: z.j, :] = stage[me ^ d].astype(out.dtype)
    if outs[0].shape[0] > z.j:
        w, n = tree_sum([p[z.j :, :].astype(F32) for p in pieces]), z.ride_b
        w = jnp.concatenate(fold_all(z, w), axis=0)
        w = jnp.concatenate([w[i * n : (i + 1) * n] for i in range(z.lanes // 128)], axis=1)
        w = w.astype(BF16)
        for out in outs:
            out[z.j :, :] = w.astype(out.dtype)


def channel_rows(z, value):
    if z.j < 128:
        value = jnp.concatenate([value, jnp.zeros((128 - z.j, z.lanes), F32)], axis=0)
    turned = value.T
    blocks = []
    for q in range(z.qo):
        starts = [(g * z.qo + q) * z.cg for g in range(z.ng)]
        blocks.append(jnp.concatenate([turned[s : s + z.cg] for s in starts], axis=0))
    return blocks


def mode_kernel(z, idx, w_ref, e_ref, *refs):
    pieces = refs[: z.n_radial]
    dx_ref, dy_ref, even, odd, acc = refs[-5:]
    value = tree_sum([p[...].astype(F32) for p in pieces])
    k = (lax.broadcasted_iota(jnp.int32, value.shape, 0) & (z.own - 1)) + idx[0] * z.own
    scale = 1.0 / (z.radial_total * z.axial_total)
    value = value * jnp.where(k == 0, scale, 2.0 * scale)
    blocks = channel_rows(z, value)
    lane = lax.broadcasted_iota(jnp.int32, (z.own, 128), 1)
    for q in range(0, z.qo, 2):
        pair = jnp.concatenate(blocks[q : q + 2], axis=0).T
        re, im = pair[: z.own], pair[z.own : z.j]
        re2, im2 = pltpu.roll(re, 64, 1), pltpu.roll(im, 64, 1)
        dy_ref[q, 0] = jnp.where(lane < 64, re, im2)
        dy_ref[q, 1] = jnp.where(lane < 64, im, -re2)
        dy_ref[q + 1, 0] = jnp.where(lane < 64, re2, im)
        dy_ref[q + 1, 1] = jnp.where(lane < 64, im2, -re)
    total = None
    for i in range(z.own // 8):
        products = even if i % 2 == 0 else odd
        for q in range(z.qo):
            rows = slice(q * z.c, (q + 1) * z.c)
            for kk in range(8):
                k = i * 8 + kk
                w = w_ref[q, k].astype(F32)
                d0 = dy_ref[q, 0, k : k + 1, :]
                d1 = dy_ref[q, 1, k : k + 1, :]
                products[rows, kk * 256 : kk * 256 + 128] = (w * d0).astype(BF16)
                products[rows, kk * 256 + 128 : kk * 256 + 256] = (w * d1).astype(BF16)
        sums = dot(products[...], e_ref[...])
        sums = pltpu.roll(sums, i * 8, 1) if i else sums
        total = sums if total is None else total + sums
    acc[...] = total
    rows = []
    for g in range(z.ng):
        for q in range(z.qo):
            start = q * z.c + g * z.cg
            rows.append(acc[start : start + z.cg, :])
    turned = jnp.concatenate(rows, axis=0).T
    dx_ref[: z.own, :] = turned[: z.own].astype(BF16)
    dx_ref[z.own :, :] = turned[64 : 64 + z.own].astype(BF16)


def outer_kernel(z, dy_ref, *refs):
    pieces = refs[: z.n_radial]
    out_ref, w_ref, x_rows = refs[-3:]
    step = pl.program_id(0)

    @pl.when(step == 0)
    def _():
        value = tree_sum([p[: z.j, :].astype(F32) for p in pieces])
        for q, block in enumerate(channel_rows(z, value)):
            high, low = split(block)
            x_rows[q * z.c : (q + 1) * z.c, :128] = high
            x_rows[q * z.c : (q + 1) * z.c, 128:] = low
        w = fold_all(z, tree_sum([p[z.j :, :].astype(F32) for p in pieces]))
        w = jnp.concatenate(w, axis=0)
        w = [w[i * 8 : (i + 1) * 8] for i in range(z.cr // 128)]
        w_ref[...] = jnp.concatenate(w, axis=1)

    row = lax.broadcasted_iota(jnp.int32, (256, 256), 0) & 127
    lane = lax.broadcasted_iota(jnp.int32, (256, 256), 1)
    base = row - jnp.where(lane < 128, 0, z.own)
    for kk in range(8):
        k = step * 8 + kk
        spread = dot(x_rows[...], jnp.where(base == k, 1.0, 0.0).astype(BF16))
        for q in range(z.qo):
            d0 = dy_ref[q, 0, pl.ds(k, 1), :]
            d1 = dy_ref[q, 1, pl.ds(k, 1), :]
            x = spread[q * z.c : (q + 1) * z.c]
            out_ref[q, kk] = x[:, :128] * d0 + x[:, 128:] * d1


def back_kernel(z, idx, high_ref, low_ref, shift_ref, *refs):
    pieces, (out_ref, stage) = refs[: z.n_radial], refs[-2:]
    me = idx[1]
    for d, piece in enumerate(pieces):
        zz = me ^ d
        cos, sin = shift_ref[me, zz, 0:1, :], shift_ref[me, zz, 1:2, :]
        for g in range(z.ng):
            block = piece[:, g * 128 : (g + 1) * 128].astype(F32)
            re, im = block[: z.own], block[z.own :]
            stage[zz, g * z.j : g * z.j + z.own, :] = (cos * re - sin * im).astype(BF16)
            stage[zz, g * z.j + z.own : (g + 1) * z.j, :] = (sin * re + cos * im).astype(BF16)
    nt = ((1,), (1,))
    lhs = jnp.concatenate([stage[zz] for zz in range(z.n_radial)], axis=1)
    c = dot(lhs, high_ref[:, : z.half], nt) + dot(lhs, low_ref[:, : z.half], nt)
    s = dot(lhs, high_ref[:, z.half :], nt) + dot(lhs, low_ref[:, z.half :], nt)
    for g in range(z.ng):
        lanes = slice(g * z.kb, (g + 1) * z.kb)
        re, im = slice(g * z.j, g * z.j + z.own), slice(g * z.j + z.own, (g + 1) * z.j)
        out_ref[: z.own, lanes] = (c[re] - s[im]).astype(BF16)
        out_ref[z.own : z.j, lanes] = (s[re] + c[im]).astype(BF16)


def pack_kernel(z, w_ref, *refs):
    pieces, out_ref = refs[: z.chips], refs[-1]
    for d in range(z.chips):
        out_ref[d * z.j : (d + 1) * z.j, :] = pieces[d][...]
    w = w_ref[...]
    out_ref[KA :, :] = jnp.concatenate([w, jnp.zeros_like(w)], axis=0).astype(BF16)


def pick_table(z, idx, t_ref, stage, far):
    chip, core = idx[0] // 2, idx[0] % 2
    for d in range(z.chips):
        owner = (chip ^ d) * 2 + (1 - core if far else core)
        rows = pl.ds(pl.multiple_of(owner * z.j, z.j), z.j)
        stage[d * z.j : (d + 1) * z.j, :] = t_ref[rows, :]


def near_kernel(z, idx, t_ref, w_ref, g_ref, lines_ref, out_ref, stage):
    pick_table(z, idx, t_ref, stage, False)
    row = lax.broadcasted_iota(jnp.int32, (z.cr, z.c), 0) // z.r
    pick = (row == lax.broadcasted_iota(jnp.int32, (z.cr, z.c), 1)).astype(F32).astype(BF16)
    tall = dot(pick, w_ref[...]).astype(BF16)
    row = lax.broadcasted_iota(jnp.int32, (z.blk, z.cr), 0)
    col = lax.broadcasted_iota(jnp.int32, (z.blk, z.cr), 1)
    same = ((row ^ col) & (z.r - 1)) == 0
    for b in range(z.nblk):
        rows = slice(b * z.blk, (b + 1) * z.blk)
        full = dot(tall[rows], pick, ((1,), (1,)))
        full = jnp.where(same, full, 0.0).astype(BF16)
        near = dot(lines_ref[:KA, rows], stage[...], ((0,), (0,)))
        out_ref[rows, :] = dot(full, g_ref[...]) + near


def final_kernel(z, idx, t_ref, near_ref, pack_ref, lines_ref, out_ref, wg_ref, stage, result, sems):
    pick_table(z, idx, t_ref, stage, True)
    copies = []
    for b in range(z.nblk):
        rows = slice(b * z.blk, (b + 1) * z.blk)
        part = dot(lines_ref[:KA, rows], stage[...], ((0,), (0,)))
        result[b] = (part + near_ref[rows, :]).astype(BF16)
        copies.append(pltpu.make_async_copy(result.at[b], out_ref.at[rows, :], sems.at[b]))
        copies[-1].start()
    w = pack_ref[KA : KA + 8, :].astype(F32) + lines_ref[KA : KA + 8, :].astype(F32)
    w = [fold(w[:, i * 128 : (i + 1) * 128])[:, : z.c] for i in range(z.cr // 128)]
    scale = 1.0 / math.sqrt(z.radial_total * z.axial_total)
    wg_ref[...] = jnp.concatenate(w, axis=0) * scale
    for copy in copies:
        copy.wait()


def whole_spec(shape):
    return pl.BlockSpec(shape, lambda *_: (0,) * len(shape))


VSPEC = pl.BlockSpec(memory_space=pltpu.VMEM)
ASPEC = pl.BlockSpec(memory_space=pl.ANY)


def params(limit):
    return pltpu.CompilerParams(vmem_limit_bytes=limit << 20)


def cost(args, outs, flops):
    size = sum(math.prod(a.shape) * a.dtype.itemsize for a in (*args, *outs))
    return pl.CostEstimate(flops=flops, bytes_accessed=size, transcendentals=0)


def small(kernel, idx, args, outs, scratch, name, flops=0, after=(), out_specs=None, aliases=None):
    head = () if idx is None else (idx,)
    specs = [pl.BlockSpec(memory_space=pltpu.SMEM)] * len(head)
    return pl.pallas_call(
        kernel,
        out_shape=outs,
        in_specs=specs + [VSPEC] * len(args) + [ASPEC] * len(after),
        out_specs=out_specs or [VSPEC] * len(outs),
        scratch_shapes=scratch,
        compiler_params=params(20),
        cost_estimate=cost(args, outs, flops),
        input_output_aliases=aliases or {},
        name=name,
    )(*head, *args, *after)


def xor_permute(value, axis, size, d):
    return lax.ppermute(value, axis, [(i, i ^ d) for i in range(size)])


def body(inputs, saved_pre, cotangent, pointwise_weight, spectral_weight):
    channels, rows, cols = inputs.shape
    z = Sizes(channels, rows, cols, lax.axis_size("axial"), lax.axis_size("radial"))
    sds = jax.ShapeDtypeStruct
    idx = jnp.stack([lax.axis_index("axial"), lax.axis_index("radial")]).astype(jnp.int32)
    flat = (z.cr, z.a)
    x, pre, cot = (v.reshape(flat) for v in (inputs, saved_pre, cotangent))
    base, shift = axial_base(z), axial_shift(z)
    tables = tuple(jnp.asarray(v) for v in (*radial_base(z), radial_shift(z)))
    row_block = pl.BlockSpec((z.blk, z.a), lambda i, *_: (i, 0))
    parts_shape = sds((z.chips, z.j, z.cr), BF16)
    part_spec = pl.BlockSpec((z.chips, z.j, z.blk), lambda i, *_: (0, 0, i))
    mm = 2 * KA * z.cr * z.a * 2
    bind = functools.partial

    grad_out = [sds(flat, BF16), sds((2 * KA, z.a), BF16), parts_shape, parts_shape]
    grad_in = (jnp.asarray(base), jnp.asarray(shift), pre, cot)
    g, table, g_keep, g_send = pl.pallas_call(
        bind(grad_kernel, z),
        out_shape=grad_out,
        grid_spec=pltpu.PrefetchScalarGridSpec(
            num_scalar_prefetch=1,
            grid=(z.nblk,),
            in_specs=[
                whole_spec(base.shape),
                pl.BlockSpec((1,) + shift.shape[1:], lambda i, idx: (idx[0], 0, 0)),
                row_block,
                row_block,
            ],
            out_specs=[VSPEC] * 4,
            scratch_shapes=[pltpu.VMEM((z.n_axial, z.j, z.blk), BF16)],
        ),
        compiler_params=params(48),
        cost_estimate=cost(grad_in, grad_out, mm * 3),
        name="grad_axial",
    )(idx, *grad_in)

    def add(keep, recv, ride, name, after=()):
        shape = (z.j + (z.ride if ride else 0), z.cr)
        outs = [sds(shape, F32)] + [sds(shape, BF16)] * (z.chips - 1)
        return small(bind(add_kernel, z), None, (keep, recv, *ride), outs, [], name, after=after)

    def axial_exchange(parts):
        return [parts[0]] + [
            xor_permute(parts[d], "axial", z.n_axial, 2 * d) for d in range(1, z.chips)]

    def radial(pieces, ride, name, after=()):
        shape = (z.j + ride, z.lanes)
        outs = [sds(shape, F32)] + [sds(shape, BF16)] * (z.n_radial - 1)
        return small(
            bind(radial_kernel, z), idx, (*tables, *pieces), outs,
            [pltpu.VMEM((z.n_radial, z.j, z.lanes), F32)], name, mm // 2, after)

    def radial_exchange(parts):
        return [parts[0]] + [
            xor_permute(parts[d], "radial", z.n_radial, d) for d in range(1, z.n_radial)]

    g_recv = xor_permute(g_send, "axial", z.n_axial, 1)
    x_keep, x_send = small(
        bind(input_kernel, z), idx, (table, x), [parts_shape] * 2,
        [pltpu.VMEM((z.nblk, z.n_axial, z.j, z.blk), BF16)], "input_axial", mm)
    x_recv = xor_permute(x_send, "axial", z.n_axial, 1)
    g_parts = add(g_keep, g_recv, (), "grad_add", (x_keep,))
    g_pieces = axial_exchange(g_parts)
    (weight,) = small(
        bind(weight_kernel, z), None, (x, g), [sds((z.ride, z.cr), BF16)], [], "weight", mm * 2,
        (g_parts[0],))
    g_sends = radial(g_pieces, 0, "grad_radial", (weight,))
    g_modes = radial_exchange(g_sends)
    x_parts = add(x_keep, x_recv, (weight,), "input_add", (g_sends[0],))
    x_pieces = axial_exchange(x_parts)

    piece_shape = (z.j, z.lanes)
    d_x, d_y = small(
        bind(mode_kernel, z), idx, (spectral_weight, jnp.asarray(lane_sums()), *g_modes),
        [sds(piece_shape, BF16), sds((z.qo, 2, z.own, 128), F32)],
        [pltpu.VMEM((z.qo * z.c, 2048), BF16)] * 2 + [pltpu.VMEM((z.qo * z.c, 128), F32)],
        "mode_grad", mm * 2, (x_parts[0],))
    d_pieces = radial_exchange([d_x] * z.n_radial)
    x_sends = radial(x_pieces, z.ride_b, "input_radial", (d_x,))
    x_modes = radial_exchange(x_sends)
    (lines,) = small(
        bind(back_kernel, z), idx, (*tables, *d_pieces), [sds((z.j, z.cr), BF16)],
        [pltpu.VMEM((z.n_radial, z.ng * z.j, 128), BF16)], "back_radial", mm // 2, (x_sends[0],))
    near = [lines] + [xor_permute(lines, "axial", z.n_axial, 2 * d) for d in range(1, z.chips)]
    outer_out = [sds((z.qo, z.own, z.c, 128), F32), sds((z.ride, z.cr), F32)]
    outer_in = (d_y, *x_modes)
    spectral_grad, weight = pl.pallas_call(
        bind(outer_kernel, z),
        out_shape=outer_out,
        grid=(z.own // 8,),
        in_specs=[VSPEC] * len(outer_in) + [ASPEC],
        out_specs=[
            pl.BlockSpec((z.qo, 8, z.c, 128), lambda i: (0, i, 0, 0)),
            VSPEC,
        ],
        scratch_shapes=[pltpu.VMEM((z.qo * z.c, 256), BF16)],
        compiler_params=params(48),
        cost_estimate=cost(outer_in, outer_out, 0),
        name="spectral_outer",
    )(*outer_in, lines)
    half_shape = sds((KA + 16, z.cr), BF16)
    (packed,) = small(bind(pack_kernel, z), None, (weight, *near), [half_shape], [], "pack")
    far = xor_permute(packed, "axial", z.n_axial, 1)
    half_stage = pltpu.VMEM((KA, z.a), BF16)
    (near_sum,) = small(
        bind(near_kernel, z), idx, (table, pointwise_weight, g, packed), [sds(flat, F32)], [half_stage],
        "near_axial", mm // 2)
    input_grad, weight_grad = small(
        bind(final_kernel, z), idx, (table, near_sum, packed, far),
        [sds(flat, BF16), sds((z.c, z.c), F32)],
        [half_stage, pltpu.VMEM((z.nblk, z.blk, z.a), BF16), pltpu.SemaphoreType.DMA((z.nblk,))],
        "final_axial", mm // 2, (), [ASPEC, VSPEC])
    return (input_grad.reshape(inputs.shape), spectral_grad, weight_grad)


def solution(mesh):
    placed = (
        P(None, "radial", ("parts", "axial")),
        P(None, "radial", ("parts", "axial")),
        P(None, "radial", ("parts", "axial")),
        P(),
        P("radial", "axial", None, None),
    )
    return jax.shard_map(
        body,
        mesh=mesh,
        in_specs=placed,
        out_specs=(
            P(None, "radial", ("parts", "axial")),
            P("radial", ("parts", "axial"), None, None),
            P("parts", None),
        ),
        check_vma=False,
    )
```

time: 92.7 us -> 71.6 us (0.77)
  waiting for transfers between devices: 23.1 us -> 12 us
  Pallas kernels: 42.4 us -> 32.2 us
  starting transfers between devices: 22.3 us -> 24.3 us
  local copies, waits for them, and re-layouts: 3.71 us -> 1.88 us
    ppermute x24 -> x21, waiting for transfers between devices: 23.1 us -> 12 us  [xor_permute(): return lax.ppermute(value, axis, [(i, i ^ d) for i in range(size)])]
    pallas_call x11 -> x13, Pallas kernels: 42.4 us -> 32.2 us  [the longest x11 20.8 us: small(): pl.pallas_call(kernel, out_shape=outs, in_specs=specs + [VSPEC] * len(arg...]
    ppermute x24 -> x21, starting transfers between devices: 22.3 us -> 24.3 us  [xor_permute(): return lax.ppermute(value, axis, [(i, i ^ d) for i in range(size)])]
    unnamed x22 -> x18, local copies, waits for them, and re-layouts: 3.71 us -> 1.88 us
  transfers between devices with their start and end apart: 24 -> 21, of which waited for: 11 -> 7; matrix products, arithmetic and copies ran while one was open for 0% -> 0% of each run, Pallas kernels for 33% -> 32%
where the time goes in v2:
time: 71.6 us; the launch traced here: 71.3 us
  Pallas kernels  32.2 us (45%)
  starting transfers between devices  24.3 us (34%)
  waiting for transfers between devices  12 us (17%)
  local copies, waits for them, and re-layouts  1.88 us (3%)
  between operations  0.95 us (1%)
    ppermute x21, starting transfers between devices, xor_permute(): return lax.ppermute(value, axis, [(i, i ^ d) for i in range(size)])  24.3 us
    pallas_call x11, Pallas kernels, small(): pl.pallas_call(kernel, out_shape=outs, in_specs=specs + [VSPEC] * len(arg...  20.8 us
    ppermute x21, waiting for transfers between devices, xor_permute(): return lax.ppermute(value, axis, [(i, i ^ d) for i in range(size)])  12 us
    pallas_call x1, Pallas kernels, body(): pl.pallas_call(bind(grad_kernel, z), out_shape=grad_out, grid_spec=pltpu....  6.4 us
    pallas_call x1, Pallas kernels, body(): pl.pallas_call(bind(outer_kernel, z), out_shape=outer_out, grid=(z.own //...  5 us
    unnamed x18, local copies, waits for them, and re-layouts  1.88 us
  transfers between devices with their start and end apart: 21, of which 7 were waited for; matrix products, arithmetic and copies ran while one was open for 0% of the time, Pallas kernels for 32%

profile of v2, /device:TPU:0, one launch (start us, length us, event | category | flops | bytes accessed | tf_op | source)
XLA Modules:
  0.0 71.3 jit_solution(10369580756702026054)
XLA Ops:
  0.7 0.9 %copy-done.6 = f32[2,256,128]{2,1,0:T(8,128)S(1)} copy-done((f32[2,256,128]{2,1,0:T(8,128)S(1)}, f32[2,256,128]{2,1,0:T(8,128)}, u32[]{:S(2)}) %copy-start.6) | copy-done | bytes 262168
  1.7 0.9 %copy-done.7 = f32[8,16,256]{2,1,0:T(8,128)S(1)} copy-done((f32[8,16,256]{2,1,0:T(8,128)S(1)}, f32[8,16,256]{2,1,0:T(8,128)}, u32[]{:S(2)}) %copy-start.7) | copy-done | bytes 131096
  2.6 6.4 %grad_axial.1 = (bf16[1024,1024]{1,0:T(8,128)(2,1)S(1)}, bf16[512,1024]{1,0:T(8,128)(2,1)S(1)}, bf16[4,64,1024]{2,1,0:T(8,128)(2,1)S(1)}, bf16[4,64,1024]{2,1,0:T(8,128)(2,1)S(1)}) custom-call(s32[2]{0:T(128)S(1)} %pad_add_fusion.idx, f32[2,256,128]{2,1,0:T(8,128)S(1)} %copy-done.6, f32[8,16,256]{2,1,0:T(8,128)S(1)} %copy-done.7, ...), custom_call_target="tpu_custom_call" | custom-call | flops 3221225472 | bytes 8781824 | tf_op jit(solution)/shard_map/grad_axial/pallas_call | solution.py:442
  9.0 0.5 collective-permute-start
  9.5 2.0 %input_axial.1 = (bf16[4,64,1024]{2,1,0:T(8,128)(2,1)S(1)}, bf16[4,64,1024]{2,1,0:T(8,128)(2,1)S(1)}) custom-call(s32[2]{0:T(128)S(1)} %pad_add_fusion.idx, bf16[512,1024]{1,0:T(8,128)(2,1)S(1)} %get-tuple-element.31.t_ref, bf16[1024,1024]{1,0:T(8,128)(2,1)S(1)} %bitcast.6), custom_call_target="tpu_custom_call" | custom-call | flops 1073741824 | bytes 4194304 | tf_op jit(solution)/shard_map/input_axial/pallas_call | solution.py:408
  11.7 3.0 %collective-permute-start.1 = (bf16[64,1024]{1,0:T(8,128)(2,1)S(1)}, bf16[64,1024]{1,0:T(8,128)(2,1)S(1)}, u32[]{:S(2)}, u32[]{:S(2)}) collective-permute-start(bf16[64,1024]{1,0:T(8,128)(2,1)S(1)} %get-tuple-element.37), channel_id=1, source_target_pairs={{0,8},{4,12},{8,0},{12,4},{16,24},{20,28},{24,16},{28,20},{1,9},{5... | collective-permute-start | bytes 393224 | tf_op jit(solution)/shard_map/ppermute | solution.py:422
  14.7 1.5 %collective-permute-start.2 = (bf16[64,1024]{1,0:T(8,128)(2,1)S(1)}, bf16[64,1024]{1,0:T(8,128)(2,1)S(1)}, u32[]{:S(2)}, u32[]{:S(2)}) collective-permute-start(bf16[64,1024]{1,0:T(8,128)(2,1)S(1)} %get-tuple-element.38), channel_id=1, source_target_pairs={{0,16},{4,20},{8,24},{12,28},{16,0},{20,4},{24,8},{28,12},{1,17},{... | collective-permute-start | bytes 393224 | tf_op jit(solution)/shard_map/ppermute | solution.py:422
  16.3 2.9 %weight.1.refs_4_.refs_0_ = bf16[8,1024]{1,0:T(8,128)(2,1)S(1)} custom-call(bf16[1024,1024]{1,0:T(8,128)(2,1)S(1)} %bitcast.7, bf16[1024,1024]{1,0:T(8,128)(2,1)S(1)} %get-tuple-element.32.g_ref, f32[64,1024]{1,0:T(8,128)S(1)} %get-tuple-element.36.refs_0_), custom_call_target="tpu_custom_call" | custom-call | flops 2147483648 | bytes 4210688 | tf_op jit(solution)/shard_map/weight/pallas_call | solution.py:408
  19.2 3.5 %collective-permute-done.2.refs_2_ = bf16[64,1024]{1,0:T(8,128)(2,1)S(1)} collective-permute-done((bf16[64,1024]{1,0:T(8,128)(2,1)S(1)}, bf16[64,1024]{1,0:T(8,128)(2,1)S(1)}, u32[]{:S(2)}, u32[]{:S(2)}) %collective-permute-start.2) | collective-permute-done | bytes 131104 | tf_op jit(solution)/shard_map/ppermute | solution.py:422
  22.7 1.5 %grad_radial.1 = (f32[64,512]{1,0:T(8,128)S(1)}, bf16[64,512]{1,0:T(8,128)(2,1)S(1)}, bf16[64,512]{1,0:T(8,128)(2,1)S(1)}, bf16[64,512]{1,0:T(8,128)(2,1)S(1)}) custom-call(s32[2]{0:T(128)S(1)} %pad_add_fusion.idx, bf16[256,1024]{1,0:T(8,128)(2,1)S(1)} %copy-done.4, bf16[256,1024]{1,0:T(8,128)(2,1)S(1)} %copy-done.3, f32[4,4,8,128]{3,2,1,0:T(8,128)S(1)} %copy-done.8, ...), custom_call_target="tpu_custom_call" | custom-call | flops 536870912 | bytes 2097152 | tf_op jit(solution)/shard_map/grad_radial/pallas_call | solution.py:408
  24.2 1.6 %collective-permute-start.4 = (bf16[64,512]{1,0:T(8,128)(2,1)S(1)}, bf16[64,512]{1,0:T(8,128)(2,1)S(1)}, u32[]{:S(2)}, u32[]{:S(2)}) collective-permute-start(bf16[64,512]{1,0:T(8,128)(2,1)S(1)} %get-tuple-element.41), channel_id=1, source_target_pairs={{0,1},{1,0},{2,3},{3,2},{4,5},{5,4},{6,7},{7,6},{8,9},{9,8},{10,11... | collective-permute-start | bytes 196616 | tf_op jit(solution)/shard_map/ppermute | solution.py:422
  25.8 2.6 %collective-permute-start.5 = (bf16[64,512]{1,0:T(8,128)(2,1)S(1)}, bf16[64,512]{1,0:T(8,128)(2,1)S(1)}, u32[]{:S(2)}, u32[]{:S(2)}) collective-permute-start(bf16[64,512]{1,0:T(8,128)(2,1)S(1)} %get-tuple-element.42), channel_id=1, source_target_pairs={{0,2},{1,3},{2,0},{3,1},{4,6},{5,7},{6,4},{7,5},{8,10},{9,11},{10,... | collective-permute-start | bytes 196616 | tf_op jit(solution)/shard_map/ppermute | solution.py:422
  28.8 1.3 %collective-permute-start.8 = (bf16[72,1024]{1,0:T(8,128)(2,1)S(1)}, bf16[72,1024]{1,0:T(8,128)(2,1)S(1)}, u32[]{:S(2)}, u32[]{:S(2)}) collective-permute-start(bf16[72,1024]{1,0:T(8,128)(2,1)S(1)} %get-tuple-element.47), channel_id=1, source_target_pairs={{0,8},{4,12},{8,0},{12,4},{16,24},{20,28},{24,16},{28,20},{1,9},{5... | collective-permute-start | bytes 442376 | tf_op jit(solution)/shard_map/ppermute | solution.py:422
  30.1 0.8 %collective-permute-start.9 = (bf16[72,1024]{1,0:T(8,128)(2,1)S(1)}, bf16[72,1024]{1,0:T(8,128)(2,1)S(1)}, u32[]{:S(2)}, u32[]{:S(2)}) collective-permute-start(bf16[72,1024]{1,0:T(8,128)(2,1)S(1)} %get-tuple-element.48), channel_id=1, source_target_pairs={{0,16},{4,20},{8,24},{12,28},{16,0},{20,4},{24,8},{28,12},{1,17},{... | collective-permute-start | bytes 442376 | tf_op jit(solution)/shard_map/ppermute | solution.py:422
  30.9 1.4 %collective-permute-start.10 = (bf16[72,1024]{1,0:T(8,128)(2,1)S(1)}, bf16[72,1024]{1,0:T(8,128)(2,1)S(1)}, u32[]{:S(2)}, u32[]{:S(2)}) collective-permute-start(bf16[72,1024]{1,0:T(8,128)(2,1)S(1)} %get-tuple-element.49), channel_id=1, source_target_pairs={{0,24},{4,28},{8,16},{12,20},{16,8},{20,12},{24,0},{28,4},{1,25},{... | collective-permute-start | bytes 442376 | tf_op jit(solution)/shard_map/ppermute | solution.py:422
  32.4 2.1 %collective-permute-done.6.refs_3_ = bf16[64,512]{1,0:T(8,128)(2,1)S(1)} collective-permute-done((bf16[64,512]{1,0:T(8,128)(2,1)S(1)}, bf16[64,512]{1,0:T(8,128)(2,1)S(1)}, u32[]{:S(2)}, u32[]{:S(2)}) %collective-permute-start.6) | collective-permute-done | bytes 65568 | tf_op jit(solution)/shard_map/ppermute | solution.py:422
  34.5 4.6 %mode_grad.1 = (bf16[64,512]{1,0:T(8,128)(2,1)S(1)}, f32[8,2,32,128]{3,2,1,0:T(8,128)S(1)}) custom-call(s32[2]{0:T(128)S(1)} %pad_add_fusion.idx, bf16[8,32,64,128]{3,2,1,0:T(8,128)(2,1)S(1)} %copy-done.1, bf16[2048,128]{1,0:T(8,128)(2,1)S(1)} %copy-done.5, f32[64,512]{1,0:T(8,128)S(1)} %get-tuple-element.40.refs_1_.refs_0_, ...), custom_call_target="tpu_custom_call" | custom-call | flops 2147483648 | bytes 5373952 | tf_op jit(solution)/shard_map/mode_grad/pallas_call | solution.py:408
  39.1 1.5 %collective-permute-start.16 = (bf16[64,512]{1,0:T(8,128)(2,1)S(1)}, bf16[64,512]{1,0:T(8,128)(2,1)S(1)}, u32[]{:S(2)}, u32[]{:S(2)}) collective-permute-start(bf16[64,512]{1,0:T(8,128)(2,1)S(1)} %get-tuple-element.50.refs_4_.refs_0_), channel_id=1, source_target_pairs={{0,3},{1,2},{2,1},{3,0},{4,7},{5,6},{6,5},{7,4},{8,11},{9,10},{10,... | collective-permute-start | bytes 196616 | tf_op jit(solution)/shard_map/ppermute | solution.py:422
  40.6 2.9 %collective-permute-start.14 = (bf16[64,512]{1,0:T(8,128)(2,1)S(1)}, bf16[64,512]{1,0:T(8,128)(2,1)S(1)}, u32[]{:S(2)}, u32[]{:S(2)}) collective-permute-start(bf16[64,512]{1,0:T(8,128)(2,1)S(1)} %get-tuple-element.50.refs_4_.refs_0_), channel_id=1, source_target_pairs={{0,1},{1,0},{2,3},{3,2},{4,5},{5,4},{6,7},{7,6},{8,9},{9,8},{10,11... | collective-permute-start | bytes 196616 | tf_op jit(solution)/shard_map/ppermute | solution.py:422
  43.5 1.5 %input_radial.1 = (f32[80,512]{1,0:T(8,128)S(1)}, bf16[80,512]{1,0:T(8,128)(2,1)S(1)}, bf16[80,512]{1,0:T(8,128)(2,1)S(1)}, bf16[80,512]{1,0:T(8,128)(2,1)S(1)}) custom-call(s32[2]{0:T(128)S(1)} %pad_add_fusion.idx, bf16[256,1024]{1,0:T(8,128)(2,1)S(1)} %copy-done.4, bf16[256,1024]{1,0:T(8,128)(2,1)S(1)} %copy-done.3, f32[4,4,8,128]{3,2,1,0:T(8,128)S(1)} %copy-done.8, ...), custom_call_target="tpu_custom_call" | custom-call | flops 536870912 | bytes 2260992 | tf_op jit(solution)/shard_map/input_radial/pallas_call | solution.py:408
  45.1 0.6 collective-permute-done.16.refs_3_
  45.7 1.3 %collective-permute-done.15.refs_2_ = bf16[64,512]{1,0:T(8,128)(2,1)S(1)} collective-permute-done((bf16[64,512]{1,0:T(8,128)(2,1)S(1)}, bf16[64,512]{1,0:T(8,128)(2,1)S(1)}, u32[]{:S(2)}, u32[]{:S(2)}) %collective-permute-start.15) | collective-permute-done | bytes 65568 | tf_op jit(solution)/shard_map/ppermute | solution.py:422
  47.2 1.0 %back_radial.1.refs_4_.refs_0_ = bf16[64,1024]{1,0:T(8,128)(2,1)S(1)} custom-call(s32[2]{0:T(128)S(1)} %pad_add_fusion.idx, bf16[256,1024]{1,0:T(8,128)(2,1)S(1)} %copy-done.4, bf16[256,1024]{1,0:T(8,128)(2,1)S(1)} %copy-done.3, f32[4,4,8,128]{3,2,1,0:T(8,128)S(1)} %copy-done.8, bf16[64,512]{1,0:T(8,128)(2,1)S(1)} %get-tuple-element.50.refs_4_.refs_0_, ...), custom_call_target="tpu_custom_call" | custom-call | flops 536870912 | bytes 1507328 | tf_op jit(solution)/shard_map/back_radial/pallas_call | solution.py:408
  48.3 1.5 %collective-permute-start.19 = (bf16[64,1024]{1,0:T(8,128)(2,1)S(1)}, bf16[64,1024]{1,0:T(8,128)(2,1)S(1)}, u32[]{:S(2)}, u32[]{:S(2)}) collective-permute-start(bf16[64,1024]{1,0:T(8,128)(2,1)S(1)} %back_radial.1.refs_4_.refs_0_), channel_id=1, source_target_pairs={{0,24},{4,28},{8,16},{12,20},{16,8},{20,12},{24,0},{28,4},{1,25},{... | collective-permute-start | bytes 393224 | tf_op jit(solution)/shard_map/ppermute | solution.py:422
  49.8 1.3 %collective-permute-start.18 = (bf16[64,1024]{1,0:T(8,128)(2,1)S(1)}, bf16[64,1024]{1,0:T(8,128)(2,1)S(1)}, u32[]{:S(2)}, u32[]{:S(2)}) collective-permute-start(bf16[64,1024]{1,0:T(8,128)(2,1)S(1)} %back_radial.1.refs_4_.refs_0_), channel_id=1, source_target_pairs={{0,16},{4,20},{8,24},{12,28},{16,0},{20,4},{24,8},{28,12},{1,17},{... | collective-permute-start | bytes 393224 | tf_op jit(solution)/shard_map/ppermute | solution.py:422
  51.1 0.7 %collective-permute-start.17 = (bf16[64,1024]{1,0:T(8,128)(2,1)S(1)}, bf16[64,1024]{1,0:T(8,128)(2,1)S(1)}, u32[]{:S(2)}, u32[]{:S(2)}) collective-permute-start(bf16[64,1024]{1,0:T(8,128)(2,1)S(1)} %back_radial.1.refs_4_.refs_0_), channel_id=1, source_target_pairs={{0,8},{4,12},{8,0},{12,4},{16,24},{20,28},{24,16},{28,20},{1,9},{5... | collective-permute-start | bytes 393224 | tf_op jit(solution)/shard_map/ppermute | solution.py:422
  51.8 0.6 collective-permute-start.12
  52.4 2.3 %collective-permute-start.13 = (bf16[80,512]{1,0:T(8,128)(2,1)S(1)}, bf16[80,512]{1,0:T(8,128)(2,1)S(1)}, u32[]{:S(2)}, u32[]{:S(2)}) collective-permute-start(bf16[80,512]{1,0:T(8,128)(2,1)S(1)} %get-tuple-element.54), channel_id=1, source_target_pairs={{0,3},{1,2},{2,1},{3,0},{4,7},{5,6},{6,5},{7,4},{8,11},{9,10},{10,... | collective-permute-start | bytes 245768 | tf_op jit(solution)/shard_map/ppermute | solution.py:422
  54.8 4.2 %collective-permute-done.12.refs_2_ = bf16[80,512]{1,0:T(8,128)(2,1)S(1)} collective-permute-done((bf16[80,512]{1,0:T(8,128)(2,1)S(1)}, bf16[80,512]{1,0:T(8,128)(2,1)S(1)}, u32[]{:S(2)}, u32[]{:S(2)}) %collective-permute-start.12) | collective-permute-done | bytes 81952 | tf_op jit(solution)/shard_map/ppermute | solution.py:422
  58.9 5.0 %spectral_outer.1 = (f32[8,32,64,128]{3,2,1,0:T(8,128)}, f32[8,1024]{1,0:T(8,128)S(1)}) custom-call(f32[8,2,32,128]{3,2,1,0:T(8,128)S(1)} %get-tuple-element.46.dy_ref, f32[80,512]{1,0:T(8,128)S(1)} %get-tuple-element.51.refs_4_.refs_0_, bf16[80,512]{1,0:T(8,128)(2,1)S(1)} %collective-permute-done.11.refs_1_, ...), custom_call_target="tpu_custom_call" | custom-call | bytes 9093120 | tf_op jit(solution)/shard_map/spectral_outer/pallas_call | solution.py:512
  64.1 4.2 %near_axial.1.near_ref = f32[1024,1024]{1,0:T(8,128)S(1)} custom-call(s32[2]{0:T(128)S(1)} %pad_add_fusion.idx, bf16[512,1024]{1,0:T(8,128)(2,1)S(1)} %get-tuple-element.31.t_ref, bf16[64,64]{1,0:T(8,128)(2,1)S(1)} %copy-done, bf16[1024,1024]{1,0:T(8,128)(2,1)S(1)} %get-tuple-element.32.g_ref, bf16[272,1024]{1,0:T(8,128)(2,1)S(1)} %pack.1.lines_ref.pack_ref), custom_call_target="tpu_custom_call" | custom-call | flops 536870912 | bytes 7905280 | tf_op jit(solution)/shard_map/near_axial/pallas_call | solution.py:408
  68.3 2.8 %final_axial.1 = (bf16[1024,1024]{1,0:T(8,128)(2,1)}, f32[64,64]{1,0:T(8,128)}) custom-call(s32[2]{0:T(128)S(1)} %pad_add_fusion.idx, bf16[512,1024]{1,0:T(8,128)(2,1)S(1)} %get-tuple-element.31.t_ref, f32[1024,1024]{1,0:T(8,128)S(1)} %near_axial.1.near_ref, bf16[272,1024]{1,0:T(8,128)(2,1)S(1)} %pack.1.lines_ref.pack_ref, ...), custom_call_target="tpu_custom_call" | custom-call | flops 536870912 | bytes 8470528 | tf_op jit(solution)/shard_map/final_axial/pallas_call | solution.py:408
  (42 shorter events, 1.3 us)
Async XLA Ops:
  0.7 1.0 %copy-start.6 = (f32[2,256,128]{2,1,0:T(8,128)S(1)}, f32[2,256,128]{2,1,0:T(8,128)}, u32[]{:S(2)}) copy-start(f32[2,256,128]{2,1,0:T(8,128)} %constant.24.clone.base_ref) | copy-start | bytes 786436
  1.7 0.9 %copy-start.7 = (f32[8,16,256]{2,1,0:T(8,128)S(1)}, f32[8,16,256]{2,1,0:T(8,128)}, u32[]{:S(2)}) copy-start(f32[8,16,256]{2,1,0:T(8,128)} %constant.25.clone.shift_ref) | copy-start | bytes 393220
  2.6 6.9 %copy-start.2 = (bf16[64,16,1024]{2,1,0:T(8,128)(2,1)S(1)}, bf16[64,16,1024]{2,1,0:T(8,128)(2,1)}, u32[]{:S(2)}) copy-start(bf16[64,16,1024]{2,1,0:T(8,128)(2,1)} %param.11) | copy-start | bytes 6291460
  9.0 2.6 %collective-permute-start = (bf16[4,64,1024]{2,1,0:T(8,128)(2,1)S(1)}, bf16[4,64,1024]{2,1,0:T(8,128)(2,1)S(1)}, u32[]{:S(2)}, u32[]{:S(2)}) collective-permute-start(bf16[4,64,1024]{2,1,0:T(8,128)(2,1)S(1)} %get-tuple-element.34), channel_id=1, source_target_pairs={{0,4},{4,0},{8,12},{12,8},{16,20},{20,16},{24,28},{28,24},{1,5},{5... | collective-permute-start | bytes 1572872 | tf_op jit(solution)/shard_map/ppermute | solution.py:422
  11.5 17.2 %collective-permute-start.7 = (bf16[4,64,1024]{2,1,0:T(8,128)(2,1)S(1)}, bf16[4,64,1024]{2,1,0:T(8,128)(2,1)S(1)}, u32[]{:S(2)}, u32[]{:S(2)}) collective-permute-start(bf16[4,64,1024]{2,1,0:T(8,128)(2,1)S(1)} %get-tuple-element.44), channel_id=1, source_target_pairs={{0,4},{4,0},{8,12},{12,8},{16,20},{20,16},{24,28},{28,24},{1,5},{5... | collective-permute-start | bytes 1572872 | tf_op jit(solution)/shard_map/ppermute | solution.py:422
  11.7 7.5 %collective-permute-start.1 = (bf16[64,1024]{1,0:T(8,128)(2,1)S(1)}, bf16[64,1024]{1,0:T(8,128)(2,1)S(1)}, u32[]{:S(2)}, u32[]{:S(2)}) collective-permute-start(bf16[64,1024]{1,0:T(8,128)(2,1)S(1)} %get-tuple-element.37), channel_id=1, source_target_pairs={{0,8},{4,12},{8,0},{12,4},{16,24},{20,28},{24,16},{28,20},{1,9},{5... | collective-permute-start | bytes 393224 | tf_op jit(solution)/shard_map/ppermute | solution.py:422
  14.7 8.0 %collective-permute-start.2 = (bf16[64,1024]{1,0:T(8,128)(2,1)S(1)}, bf16[64,1024]{1,0:T(8,128)(2,1)S(1)}, u32[]{:S(2)}, u32[]{:S(2)}) collective-permute-start(bf16[64,1024]{1,0:T(8,128)(2,1)S(1)} %get-tuple-element.38), channel_id=1, source_target_pairs={{0,16},{4,20},{8,24},{12,28},{16,0},{20,4},{24,8},{28,12},{1,17},{... | collective-permute-start | bytes 393224 | tf_op jit(solution)/shard_map/ppermute | solution.py:422
  16.3 6.4 %collective-permute-start.3 = (bf16[64,1024]{1,0:T(8,128)(2,1)S(1)}, bf16[64,1024]{1,0:T(8,128)(2,1)S(1)}, u32[]{:S(2)}, u32[]{:S(2)}) collective-permute-start(bf16[64,1024]{1,0:T(8,128)(2,1)S(1)} %get-tuple-element.39), channel_id=1, source_target_pairs={{0,24},{4,28},{8,16},{12,20},{16,8},{20,12},{24,0},{28,4},{1,25},{... | collective-permute-start | bytes 393224 | tf_op jit(solution)/shard_map/ppermute | solution.py:422
  16.3 6.4 %copy-start.3 = (bf16[256,1024]{1,0:T(8,128)(2,1)S(1)}, bf16[256,1024]{1,0:T(8,128)(2,1)}, u32[]{:S(2)}) copy-start(bf16[256,1024]{1,0:T(8,128)(2,1)} %constant.22.clone.low_ref) | copy-start | bytes 1572868
  16.3 6.4 %copy-start.4 = (bf16[256,1024]{1,0:T(8,128)(2,1)S(1)}, bf16[256,1024]{1,0:T(8,128)(2,1)}, u32[]{:S(2)}) copy-start(bf16[256,1024]{1,0:T(8,128)(2,1)} %constant.21.clone.high_ref) | copy-start | bytes 1572868
  16.3 6.4 %copy-start.8 = (f32[4,4,8,128]{3,2,1,0:T(8,128)S(1)}, f32[4,4,8,128]{3,2,1,0:T(8,128)}, u32[]{:S(2)}) copy-start(f32[4,4,8,128]{3,2,1,0:T(8,128)} %constant.23.clone.shift_ref) | copy-start | bytes 196612
  16.3 18.2 %copy-start.1 = (bf16[8,32,64,128]{3,2,1,0:T(8,128)(2,1)S(1)}, bf16[8,32,64,128]{3,2,1,0:T(8,128)(2,1)}, u32[]{:S(2)}) copy-start(bf16[8,32,64,128]{3,2,1,0:T(8,128)(2,1)} %w_ref.2) | copy-start | bytes 12582916
  19.2 15.3 %copy-start.5 = (bf16[2048,128]{1,0:T(8,128)(2,1)S(1)}, bf16[2048,128]{1,0:T(8,128)(2,1)}, u32[]{:S(2)}) copy-start(bf16[2048,128]{1,0:T(8,128)(2,1)} %constant.26.clone.e_ref) | copy-start | bytes 1572868
  24.2 6.7 %collective-permute-start.4 = (bf16[64,512]{1,0:T(8,128)(2,1)S(1)}, bf16[64,512]{1,0:T(8,128)(2,1)S(1)}, u32[]{:S(2)}, u32[]{:S(2)}) collective-permute-start(bf16[64,512]{1,0:T(8,128)(2,1)S(1)} %get-tuple-element.41), channel_id=1, source_target_pairs={{0,1},{1,0},{2,3},{3,2},{4,5},{5,4},{6,7},{7,6},{8,9},{9,8},{10,11... | collective-permute-start | bytes 196616 | tf_op jit(solution)/shard_map/ppermute | solution.py:422
  25.8 6.6 %collective-permute-start.5 = (bf16[64,512]{1,0:T(8,128)(2,1)S(1)}, bf16[64,512]{1,0:T(8,128)(2,1)S(1)}, u32[]{:S(2)}, u32[]{:S(2)}) collective-permute-start(bf16[64,512]{1,0:T(8,128)(2,1)S(1)} %get-tuple-element.42), channel_id=1, source_target_pairs={{0,2},{1,3},{2,0},{3,1},{4,6},{5,7},{6,4},{7,5},{8,10},{9,11},{10,... | collective-permute-start | bytes 196616 | tf_op jit(solution)/shard_map/ppermute | solution.py:422
  28.4 6.1 %collective-permute-start.6 = (bf16[64,512]{1,0:T(8,128)(2,1)S(1)}, bf16[64,512]{1,0:T(8,128)(2,1)S(1)}, u32[]{:S(2)}, u32[]{:S(2)}) collective-permute-start(bf16[64,512]{1,0:T(8,128)(2,1)S(1)} %get-tuple-element.43), channel_id=1, source_target_pairs={{0,3},{1,2},{2,1},{3,0},{4,7},{5,6},{6,5},{7,4},{8,11},{9,10},{10,... | collective-permute-start | bytes 196616 | tf_op jit(solution)/shard_map/ppermute | solution.py:422
  28.8 11.8 %collective-permute-start.8 = (bf16[72,1024]{1,0:T(8,128)(2,1)S(1)}, bf16[72,1024]{1,0:T(8,128)(2,1)S(1)}, u32[]{:S(2)}, u32[]{:S(2)}) collective-permute-start(bf16[72,1024]{1,0:T(8,128)(2,1)S(1)} %get-tuple-element.47), channel_id=1, source_target_pairs={{0,8},{4,12},{8,0},{12,4},{16,24},{20,28},{24,16},{28,20},{1,9},{5... | collective-permute-start | bytes 442376 | tf_op jit(solution)/shard_map/ppermute | solution.py:422
  30.1 13.4 %collective-permute-start.9 = (bf16[72,1024]{1,0:T(8,128)(2,1)S(1)}, bf16[72,1024]{1,0:T(8,128)(2,1)S(1)}, u32[]{:S(2)}, u32[]{:S(2)}) collective-permute-start(bf16[72,1024]{1,0:T(8,128)(2,1)S(1)} %get-tuple-element.48), channel_id=1, source_target_pairs={{0,16},{4,20},{8,24},{12,28},{16,0},{20,4},{24,8},{28,12},{1,17},{... | collective-permute-start | bytes 442376 | tf_op jit(solution)/shard_map/ppermute | solution.py:422
  30.9 12.6 %collective-permute-start.10 = (bf16[72,1024]{1,0:T(8,128)(2,1)S(1)}, bf16[72,1024]{1,0:T(8,128)(2,1)S(1)}, u32[]{:S(2)}, u32[]{:S(2)}) collective-permute-start(bf16[72,1024]{1,0:T(8,128)(2,1)S(1)} %get-tuple-element.49), channel_id=1, source_target_pairs={{0,24},{4,28},{8,16},{12,20},{16,8},{20,12},{24,0},{28,4},{1,25},{... | collective-permute-start | bytes 442376 | tf_op jit(solution)/shard_map/ppermute | solution.py:422
  39.1 6.6 %collective-permute-start.16 = (bf16[64,512]{1,0:T(8,128)(2,1)S(1)}, bf16[64,512]{1,0:T(8,128)(2,1)S(1)}, u32[]{:S(2)}, u32[]{:S(2)}) collective-permute-start(bf16[64,512]{1,0:T(8,128)(2,1)S(1)} %get-tuple-element.50.refs_4_.refs_0_), channel_id=1, source_target_pairs={{0,3},{1,2},{2,1},{3,0},{4,7},{5,6},{6,5},{7,4},{8,11},{9,10},{10,... | collective-permute-start | bytes 196616 | tf_op jit(solution)/shard_map/ppermute | solution.py:422
  40.6 6.4 %collective-permute-start.15 = (bf16[64,512]{1,0:T(8,128)(2,1)S(1)}, bf16[64,512]{1,0:T(8,128)(2,1)S(1)}, u32[]{:S(2)}, u32[]{:S(2)}) collective-permute-start(bf16[64,512]{1,0:T(8,128)(2,1)S(1)} %get-tuple-element.50.refs_4_.refs_0_), channel_id=1, source_target_pairs={{0,2},{1,3},{2,0},{3,1},{4,6},{5,7},{6,4},{7,5},{8,10},{9,11},{10,... | collective-permute-start | bytes 196616 | tf_op jit(solution)/shard_map/ppermute | solution.py:422
  40.6 6.6 %collective-permute-start.14 = (bf16[64,512]{1,0:T(8,128)(2,1)S(1)}, bf16[64,512]{1,0:T(8,128)(2,1)S(1)}, u32[]{:S(2)}, u32[]{:S(2)}) collective-permute-start(bf16[64,512]{1,0:T(8,128)(2,1)S(1)} %get-tuple-element.50.refs_4_.refs_0_), channel_id=1, source_target_pairs={{0,1},{1,0},{2,3},{3,2},{4,5},{5,4},{6,7},{7,6},{8,9},{9,8},{10,11... | collective-permute-start | bytes 196616 | tf_op jit(solution)/shard_map/ppermute | solution.py:422
  45.0 19.1 %copy-start = (bf16[64,64]{1,0:T(8,128)(2,1)S(1)}, bf16[64,64]{1,0:T(8,128)(2,1)}, u32[]{:S(2)}) copy-start(bf16[64,64]{1,0:T(8,128)(2,1)} %w_ref.3) | copy-start | bytes 24580
  45.0 7.4 %collective-permute-start.11 = (bf16[80,512]{1,0:T(8,128)(2,1)S(1)}, bf16[80,512]{1,0:T(8,128)(2,1)S(1)}, u32[]{:S(2)}, u32[]{:S(2)}) collective-permute-start(bf16[80,512]{1,0:T(8,128)(2,1)S(1)} %get-tuple-element.52), channel_id=1, source_target_pairs={{0,1},{1,0},{2,3},{3,2},{4,5},{5,4},{6,7},{7,6},{8,9},{9,8},{10,11... | collective-permute-start | bytes 245768 | tf_op jit(solution)/shard_map/ppermute | solution.py:422
  48.3 15.7 %collective-permute-start.19 = (bf16[64,1024]{1,0:T(8,128)(2,1)S(1)}, bf16[64,1024]{1,0:T(8,128)(2,1)S(1)}, u32[]{:S(2)}, u32[]{:S(2)}) collective-permute-start(bf16[64,1024]{1,0:T(8,128)(2,1)S(1)} %back_radial.1.refs_4_.refs_0_), channel_id=1, source_target_pairs={{0,24},{4,28},{8,16},{12,20},{16,8},{20,12},{24,0},{28,4},{1,25},{... | collective-permute-start | bytes 393224 | tf_op jit(solution)/shard_map/ppermute | solution.py:422
  49.8 14.1 %collective-permute-start.18 = (bf16[64,1024]{1,0:T(8,128)(2,1)S(1)}, bf16[64,1024]{1,0:T(8,128)(2,1)S(1)}, u32[]{:S(2)}, u32[]{:S(2)}) collective-permute-start(bf16[64,1024]{1,0:T(8,128)(2,1)S(1)} %back_radial.1.refs_4_.refs_0_), channel_id=1, source_target_pairs={{0,16},{4,20},{8,24},{12,28},{16,0},{20,4},{24,8},{28,12},{1,17},{... | collective-permute-start | bytes 393224 | tf_op jit(solution)/shard_map/ppermute | solution.py:422
  51.1 12.8 %collective-permute-start.17 = (bf16[64,1024]{1,0:T(8,128)(2,1)S(1)}, bf16[64,1024]{1,0:T(8,128)(2,1)S(1)}, u32[]{:S(2)}, u32[]{:S(2)}) collective-permute-start(bf16[64,1024]{1,0:T(8,128)(2,1)S(1)} %back_radial.1.refs_4_.refs_0_), channel_id=1, source_target_pairs={{0,8},{4,12},{8,0},{12,4},{16,24},{20,28},{24,16},{28,20},{1,9},{5... | collective-permute-start | bytes 393224 | tf_op jit(solution)/shard_map/ppermute | solution.py:422
  51.8 7.1 %collective-permute-start.12 = (bf16[80,512]{1,0:T(8,128)(2,1)S(1)}, bf16[80,512]{1,0:T(8,128)(2,1)S(1)}, u32[]{:S(2)}, u32[]{:S(2)}) collective-permute-start(bf16[80,512]{1,0:T(8,128)(2,1)S(1)} %get-tuple-element.53), channel_id=1, source_target_pairs={{0,2},{1,3},{2,0},{3,1},{4,6},{5,7},{6,4},{7,5},{8,10},{9,11},{10,... | collective-permute-start | bytes 245768 | tf_op jit(solution)/shard_map/ppermute | solution.py:422
  52.4 6.5 %collective-permute-start.13 = (bf16[80,512]{1,0:T(8,128)(2,1)S(1)}, bf16[80,512]{1,0:T(8,128)(2,1)S(1)}, u32[]{:S(2)}, u32[]{:S(2)}) collective-permute-start(bf16[80,512]{1,0:T(8,128)(2,1)S(1)} %get-tuple-element.54), channel_id=1, source_target_pairs={{0,3},{1,2},{2,1},{3,0},{4,7},{5,6},{6,5},{7,4},{8,11},{9,10},{10,... | collective-permute-start | bytes 245768 | tf_op jit(solution)/shard_map/ppermute | solution.py:422
  64.0 4.3 %collective-permute-start.20 = (bf16[272,1024]{1,0:T(8,128)(2,1)S(1)}, bf16[272,1024]{1,0:T(8,128)(2,1)S(1)}, u32[]{:S(2)}, u32[]{:S(2)}) collective-permute-start(bf16[272,1024]{1,0:T(8,128)(2,1)S(1)} %pack.1.lines_ref.pack_ref), channel_id=1, source_target_pairs={{0,4},{4,0},{8,12},{12,8},{16,20},{20,16},{24,28},{28,24},{1,5},{5... | collective-permute-start | bytes 1671176 | tf_op jit(solution)/shard_map/ppermute | solution.py:422

commit v3 on v2

--- a/solution.py
+++ b/solution.py
@@ -50,24 +50,7 @@
         self.axial_total = cols * n_axial
         self.radial_total = rows * n_radial
         self.ride = 8
-        self.ride_b = channels * 128 // self.lanes
-
-
-def axial_base(z):
-    k = np.arange(KA, dtype=np.int64)
-    a = np.arange(128, dtype=np.int64)
-    m = (k[:, None] * a[None, :]) % z.axial_total
-    phase = m * (2.0 * np.pi / z.axial_total)
-    return np.stack([np.cos(phase), np.sin(phase)]).astype(np.float32)
-
-
-def axial_shift(z):
-    k = np.arange(KA, dtype=np.int64)
-    n = z.a // 128
-    first = np.arange(z.n_axial * n, dtype=np.int64).reshape(z.n_axial, n) * 128
-    m = (first[:, :, None] * k) % z.axial_total
-    phase = m * (2.0 * np.pi / z.axial_total)
-    return np.concatenate([np.cos(phase), np.sin(phase)], axis=1).astype(np.float32)
+        self.ride_b = channels * channels // self.lanes
 
 
 def radial_freqs(z):
@@ -102,14 +85,6 @@
     return out
 
 
-def lane_sums():
-    out = np.zeros((8, 2, 128, 128), np.float32)
-    for kk in range(8):
-        for h in range(2):
-            out[kk, h, :, h * 64 + kk] = 1.0
-    return out.reshape(2048, 128).astype(ml_dtypes.bfloat16)
-
-
 def gelu_slope(value):
     return 0.5 * (1.0 + lax.erf(value * (1.0 / math.sqrt(2.0)))) + value * jnp.exp(
         -0.5 * value * value
@@ -125,30 +100,55 @@
         send_ref[d] = stage[(chip ^ d) * 2 + (1 - core)]
 
 
-def grad_kernel(z, idx, base_ref, shift_ref, pre_ref, cot_ref, g_ref, t_ref, keep_ref, send_ref, stage):
-    step = pl.program_id(0)
-
-    @pl.when(step == 0)
-    def _():
-        n = z.a // 128
-        shift = shift_ref[0]
-        shift = jnp.concatenate([shift, jnp.zeros((128 - 2 * n, KA), F32)], axis=0).T
-        cos1, sin1 = base_ref[0], base_ref[1]
-        for i in range(n):
-            cos2, sin2 = shift[:, i : i + 1], shift[:, n + i : n + i + 1]
-            real = (cos1 * cos2 - sin1 * sin2).astype(BF16)
-            imag = (-(sin1 * cos2 + cos1 * sin2)).astype(BF16)
-            lanes = slice(i * 128, (i + 1) * 128)
-            for o in range(z.n_axial):
-                rows = slice(o * z.own, (o + 1) * z.own)
-                t_ref[o * z.j : o * z.j + z.own, lanes] = real[rows]
-                t_ref[o * z.j + z.own : (o + 1) * z.j, lanes] = imag[rows]
-
-    g = (cot_ref[...].astype(F32) * gelu_slope(pre_ref[...].astype(F32))).astype(BF16)
-    rows = pl.ds(pl.multiple_of(step * z.blk, z.blk), z.blk)
-    g_ref[rows, :] = g
-    part = dot(t_ref[...], g, ((1,), (1,)))
-    split_owners(z, idx, part, keep_ref.at[:, :, rows], send_ref.at[:, :, rows], stage)
+def turn(m, total):
+    u = m.astype(F32) * (math.pi / total)
+    v = u * u
+    s = jnp.full_like(v, 1.0 / math.factorial(13))
+    c = jnp.full_like(v, 1.0 / math.factorial(12))
+    for n in range(5, -1, -1):
+        s = s * v + (-1) ** n / math.factorial(2 * n + 1)
+        c = c * v + (-1) ** n / math.factorial(2 * n)
+    s = s * u
+    return 1.0 - 2.0 * s * s, 2.0 * s * c
+
+
+def make_table(z, idx, t_ref):
+    k = lax.broadcasted_iota(jnp.int32, (KA, 128), 0)
+    lane = lax.broadcasted_iota(jnp.int32, (KA, 128), 1)
+    half, mask = z.axial_total // 2, z.axial_total - 1
+    cos1, sin1 = turn(((k * lane + half) & mask) - half, z.axial_total)
+    shift = k * ((idx[0] * (z.a // 128) + lane) * 128)
+    cos2, sin2 = turn(((shift + half) & mask) - half, z.axial_total)
+    for i in range(z.a // 128):
+        c, s = cos2[:, i : i + 1], sin2[:, i : i + 1]
+        real = (cos1 * c - sin1 * s).astype(BF16)
+        imag = (-(sin1 * c + cos1 * s)).astype(BF16)
+        lanes = slice(i * 128, (i + 1) * 128)
+        for o in range(z.n_axial):
+            rows = slice(o * z.own, (o + 1) * z.own)
+            t_ref[o * z.j : o * z.j + z.own, lanes] = real[rows]
+            t_ref[o * z.j + z.own : (o + 1) * z.j, lanes] = imag[rows]
+
+
+def grad_kernel(z, idx, pre_hbm, cot_hbm, g_ref, t_ref, keep_ref, send_ref, pre_ref, cot_ref, stage, sems):
+    copies = []
+    for b in range(z.nblk):
+        rows = slice(b * z.blk, (b + 1) * z.blk)
+        pair = []
+        for i, (source, target) in enumerate(((pre_hbm, pre_ref), (cot_hbm, cot_ref))):
+            pair.append(pltpu.make_async_copy(source.at[rows, :], target.at[rows, :], sems.at[i, b]))
+            pair[-1].start()
+        copies.append(pair)
+    make_table(z, idx, t_ref)
+    for b in range(z.nblk):
+        rows = slice(b * z.blk, (b + 1) * z.blk)
+        for copy in copies[b]:
+            copy.wait()
+        slope = gelu_slope(pre_ref[rows, :].astype(F32))
+        g = (cot_ref[rows, :].astype(F32) * slope).astype(BF16)
+        g_ref[rows, :] = g
+        part = dot(t_ref[...], g, ((1,), (1,)))
+        split_owners(z, idx, part, keep_ref.at[:, :, rows], send_ref.at[:, :, rows], stage.at[b])
 
 
 def input_kernel(z, idx, t_ref, x_ref, keep_ref, send_ref, stage):
@@ -206,10 +206,13 @@
     pieces, outs, stage = refs[: z.chips], refs[-1 - z.n_radial : -1], refs[-1]
     me = idx[1]
     value = tree_sum([p[: z.j, :].astype(F32) for p in pieces])
+    value = jnp.concatenate([value[:, g * z.kb : (g + 1) * z.kb] for g in range(z.ng)], axis=0)
+    high, low = split(value)
+    rows = z.ng * z.j
+    both = dot(jnp.concatenate([high, low], axis=0), high_ref[...])
+    both = both[:rows] + both[rows:] + dot(high, low_ref[...])
     for g in range(z.ng):
-        high, low = split(value[:, g * z.kb : (g + 1) * z.kb])
-        both = dot(jnp.concatenate([high, low], axis=0), high_ref[...])
-        total = both[: z.j] + both[z.j :] + dot(high, low_ref[...])
+        total = both[g * z.j : (g + 1) * z.j]
         c, s = total[:, : z.half], total[:, z.half :]
         real = c[: z.own] + s[z.own :]
         imag = c[z.own :] - s[: z.own]
@@ -222,12 +225,19 @@
     for d, out in enumerate(outs):
         out[: z.j, :] = stage[me ^ d].astype(out.dtype)
     if outs[0].shape[0] > z.j:
-        w, n = tree_sum([p[z.j :, :].astype(F32) for p in pieces]), z.ride_b
-        w = jnp.concatenate(fold_all(z, w), axis=0)
+        w = tree_sum([p[z.j :, :].astype(F32) for p in pieces])
+        w = [fold(w[:, i * 128 : (i + 1) * 128]) for i in range(z.cr // 128)]
+        w = pair_rows(z, jnp.concatenate(w, axis=0))
+        n = w.shape[0] // (z.lanes // 128)
         w = jnp.concatenate([w[i * n : (i + 1) * n] for i in range(z.lanes // 128)], axis=1)
         w = w.astype(BF16)
         for out in outs:
             out[z.j :, :] = w.astype(out.dtype)
+
+
+def pair_rows(z, w):
+    lane = lax.broadcasted_iota(jnp.int32, (z.c // 2, 128), 1)
+    return jnp.where(lane < z.c, w[: z.c // 2], w[z.c // 2 :])
 
 
 def channel_rows(z, value):
@@ -241,9 +251,9 @@
     return blocks
 
 
-def mode_kernel(z, idx, w_ref, e_ref, *refs):
+def mode_kernel(z, idx, w_ref, *refs):
     pieces = refs[: z.n_radial]
-    dx_ref, dy_ref, even, odd, acc = refs[-5:]
+    dx_ref, dy_ref, acc = refs[-3:]
     value = tree_sum([p[...].astype(F32) for p in pieces])
     k = (lax.broadcasted_iota(jnp.int32, value.shape, 0) & (z.own - 1)) + idx[0] * z.own
     scale = 1.0 / (z.radial_total * z.axial_total)
@@ -258,60 +268,58 @@
         dy_ref[q, 1] = jnp.where(lane < 64, im, -re2)
         dy_ref[q + 1, 0] = jnp.where(lane < 64, re2, im)
         dy_ref[q + 1, 1] = jnp.where(lane < 64, im2, -re)
-    total = None
-    for i in range(z.own // 8):
-        products = even if i % 2 == 0 else odd
-        for q in range(z.qo):
-            rows = slice(q * z.c, (q + 1) * z.c)
-            for kk in range(8):
-                k = i * 8 + kk
-                w = w_ref[q, k].astype(F32)
-                d0 = dy_ref[q, 0, k : k + 1, :]
-                d1 = dy_ref[q, 1, k : k + 1, :]
-                products[rows, kk * 256 : kk * 256 + 128] = (w * d0).astype(BF16)
-                products[rows, kk * 256 + 128 : kk * 256 + 256] = (w * d1).astype(BF16)
-        sums = dot(products[...], e_ref[...])
-        sums = pltpu.roll(sums, i * 8, 1) if i else sums
-        total = sums if total is None else total + sums
-    acc[...] = total
+    mode = lax.broadcasted_iota(jnp.int32, (128, 128), 1) & (z.own - 1)
+    for q in range(z.qo):
+        d = [dy_ref[q, 0], dy_ref[q, 1], jnp.zeros((128 - z.j, 128), F32)]
+        d = jnp.concatenate(d, axis=0).T
+        right = [jnp.where(mode == k, d, 0.0).astype(BF16) for k in range(z.own)]
+        left = jnp.concatenate([w_ref[q, k] for k in range(z.own)], axis=1)
+        acc[q * z.c : (q + 1) * z.c, :] = dot(left, jnp.concatenate(right, axis=0))
     rows = []
     for g in range(z.ng):
         for q in range(z.qo):
             start = q * z.c + g * z.cg
             rows.append(acc[start : start + z.cg, :])
-    turned = jnp.concatenate(rows, axis=0).T
-    dx_ref[: z.own, :] = turned[: z.own].astype(BF16)
-    dx_ref[z.own :, :] = turned[64 : 64 + z.own].astype(BF16)
-
-
-def outer_kernel(z, dy_ref, *refs):
-    pieces = refs[: z.n_radial]
-    out_ref, w_ref, x_rows = refs[-3:]
-    step = pl.program_id(0)
-
-    @pl.when(step == 0)
-    def _():
-        value = tree_sum([p[: z.j, :].astype(F32) for p in pieces])
-        for q, block in enumerate(channel_rows(z, value)):
-            high, low = split(block)
-            x_rows[q * z.c : (q + 1) * z.c, :128] = high
-            x_rows[q * z.c : (q + 1) * z.c, 128:] = low
-        w = fold_all(z, tree_sum([p[z.j :, :].astype(F32) for p in pieces]))
-        w = jnp.concatenate(w, axis=0)
-        w = [w[i * 8 : (i + 1) * 8] for i in range(z.cr // 128)]
-        w_ref[...] = jnp.concatenate(w, axis=1)
-
+    dx_ref[...] = jnp.concatenate(rows, axis=0).T[: z.j].astype(BF16)
+
+
+def gather_kernel(z, *refs):
+    pieces = [refs[0]] + list(refs[1 : z.n_radial])[::-1]
+    x_ref, w_ref = refs[-2:]
+    value = tree_sum([p[: z.j, :].astype(F32) for p in pieces])
+    for q, block in enumerate(channel_rows(z, value)):
+        high, low = split(block)
+        x_ref[q * z.c : (q + 1) * z.c, :128] = high
+        x_ref[q * z.c : (q + 1) * z.c, 128:] = low
+    w = tree_sum([p[z.j :, :].astype(F32) for p in pieces])
+    w = [w[:, i * 128 : (i + 1) * 128] for i in range(z.lanes // 128)]
+    w = jnp.concatenate(split(jnp.concatenate(w, axis=0)), axis=0)
+    w_ref[...] = jnp.concatenate([w[i * 8 : (i + 1) * 8] for i in range(z.c // 8)], axis=1)
+
+
+def outer_kernel(z, idx, dy_ref, x_rows, t_ref, point_ref, lines_ref, grad_ref, near_ref, result, stage, sems):
     row = lax.broadcasted_iota(jnp.int32, (256, 256), 0) & 127
     lane = lax.broadcasted_iota(jnp.int32, (256, 256), 1)
     base = row - jnp.where(lane < 128, 0, z.own)
-    for kk in range(8):
-        k = step * 8 + kk
+    copies = []
+    for k in range(z.own):
         spread = dot(x_rows[...], jnp.where(base == k, 1.0, 0.0).astype(BF16))
         for q in range(z.qo):
-            d0 = dy_ref[q, 0, pl.ds(k, 1), :]
-            d1 = dy_ref[q, 1, pl.ds(k, 1), :]
+            d0, d1 = dy_ref[q, 0, k : k + 1, :], dy_ref[q, 1, k : k + 1, :]
             x = spread[q * z.c : (q + 1) * z.c]
-            out_ref[q, kk] = x[:, :128] * d0 + x[:, 128:] * d1
+            result[q, k] = x[:, :128] * d0 + x[:, 128:] * d1
+        if k % 4 == 3:
+            part = slice(k - 3, k + 1)
+            copies.append(
+                pltpu.make_async_copy(result.at[:, part], grad_ref.at[:, part], sems.at[k // 4])
+            )
+            copies[-1].start()
+    pick_table(z, idx, t_ref, stage, False)
+    for b in range(z.nblk):
+        rows = slice(b * z.blk, (b + 1) * z.blk)
+        near_ref[rows, :] = dot(lines_ref[:KA, rows], stage[...], ((0,), (0,))) + point_ref[rows, :]
+    for copy in copies:
+        copy.wait()
 
 
 def back_kernel(z, idx, high_ref, low_ref, shift_ref, *refs):
@@ -336,12 +344,26 @@
         out_ref[z.own : z.j, lanes] = (s[re] + c[im]).astype(BF16)
 
 
+def point_kernel(z, w_ref, g_ref, *refs):
+    out_ref = refs[-1]
+    row = lax.broadcasted_iota(jnp.int32, (z.cr, z.c), 0) // z.r
+    pick = (row == lax.broadcasted_iota(jnp.int32, (z.cr, z.c), 1)).astype(F32).astype(BF16)
+    tall = dot(pick, w_ref[...]).astype(BF16)
+    row = lax.broadcasted_iota(jnp.int32, (z.blk, z.cr), 0)
+    col = lax.broadcasted_iota(jnp.int32, (z.blk, z.cr), 1)
+    same = ((row ^ col) & (z.r - 1)) == 0
+    for b in range(z.nblk):
+        rows = slice(b * z.blk, (b + 1) * z.blk)
+        full = dot(tall[rows], pick, ((1,), (1,)))
+        full = jnp.where(same, full, 0.0).astype(BF16)
+        out_ref[rows, :] = dot(full, g_ref[...])
+
+
 def pack_kernel(z, w_ref, *refs):
-    pieces, out_ref = refs[: z.chips], refs[-1]
     for d in range(z.chips):
-        out_ref[d * z.j : (d + 1) * z.j, :] = pieces[d][...]
+        refs[-1][d * z.j : (d + 1) * z.j, :] = refs[d][...]
     w = w_ref[...]
-    out_ref[KA :, :] = jnp.concatenate([w, jnp.zeros_like(w)], axis=0).astype(BF16)
+    refs[-1][KA :, :] = jnp.concatenate([w, jnp.zeros_like(w)], axis=0)
 
 
 def pick_table(z, idx, t_ref, stage, far):
@@ -352,35 +374,21 @@
         stage[d * z.j : (d + 1) * z.j, :] = t_ref[rows, :]
 
 
-def near_kernel(z, idx, t_ref, w_ref, g_ref, lines_ref, out_ref, stage):
-    pick_table(z, idx, t_ref, stage, False)
-    row = lax.broadcasted_iota(jnp.int32, (z.cr, z.c), 0) // z.r
-    pick = (row == lax.broadcasted_iota(jnp.int32, (z.cr, z.c), 1)).astype(F32).astype(BF16)
-    tall = dot(pick, w_ref[...]).astype(BF16)
-    row = lax.broadcasted_iota(jnp.int32, (z.blk, z.cr), 0)
-    col = lax.broadcasted_iota(jnp.int32, (z.blk, z.cr), 1)
-    same = ((row ^ col) & (z.r - 1)) == 0
-    for b in range(z.nblk):
-        rows = slice(b * z.blk, (b + 1) * z.blk)
-        full = dot(tall[rows], pick, ((1,), (1,)))
-        full = jnp.where(same, full, 0.0).astype(BF16)
-        near = dot(lines_ref[:KA, rows], stage[...], ((0,), (0,)))
-        out_ref[rows, :] = dot(full, g_ref[...]) + near
-
-
-def final_kernel(z, idx, t_ref, near_ref, pack_ref, lines_ref, out_ref, wg_ref, stage, result, sems):
+def final_kernel(z, idx, t_ref, near_ref, pack_ref, lines_ref, out_ref, wg_hbm, stage, result, wg_ref, sems):
+    w = pack_ref[KA : KA + 8, :].astype(F32) + lines_ref[KA : KA + 8, :].astype(F32)
+    w = jnp.concatenate([w[:, i * 128 : (i + 1) * 128] for i in range(z.c // 8)], axis=0)
+    w = w[: z.c // 2] + w[z.c // 2 :]
+    w = jnp.concatenate([w[:, : z.c], pltpu.roll(w, 64, 1)[:, : z.c]], axis=0)
+    wg_ref[...] = w * (1.0 / math.sqrt(z.radial_total * z.axial_total))
+    copies = [pltpu.make_async_copy(wg_ref, wg_hbm, sems.at[z.nblk])]
+    copies[-1].start()
     pick_table(z, idx, t_ref, stage, True)
-    copies = []
     for b in range(z.nblk):
         rows = slice(b * z.blk, (b + 1) * z.blk)
         part = dot(lines_ref[:KA, rows], stage[...], ((0,), (0,)))
         result[b] = (part + near_ref[rows, :]).astype(BF16)
         copies.append(pltpu.make_async_copy(result.at[b], out_ref.at[rows, :], sems.at[b]))
         copies[-1].start()
-    w = pack_ref[KA : KA + 8, :].astype(F32) + lines_ref[KA : KA + 8, :].astype(F32)
-    w = [fold(w[:, i * 128 : (i + 1) * 128])[:, : z.c] for i in range(z.cr // 128)]
-    scale = 1.0 / math.sqrt(z.radial_total * z.axial_total)
-    wg_ref[...] = jnp.concatenate(w, axis=0) * scale
     for copy in copies:
         copy.wait()
 
@@ -398,6 +406,8 @@
 
 
 def cost(args, outs, flops):
+    if flops is None:
+        return pl.CostEstimate(flops=0, bytes_accessed=0, transcendentals=0)
     size = sum(math.prod(a.shape) * a.dtype.itemsize for a in (*args, *outs))
     return pl.CostEstimate(flops=flops, bytes_accessed=size, transcendentals=0)
 
@@ -429,35 +439,27 @@
     idx = jnp.stack([lax.axis_index("axial"), lax.axis_index("radial")]).astype(jnp.int32)
     flat = (z.cr, z.a)
     x, pre, cot = (v.reshape(flat) for v in (inputs, saved_pre, cotangent))
-    base, shift = axial_base(z), axial_shift(z)
     tables = tuple(jnp.asarray(v) for v in (*radial_base(z), radial_shift(z)))
-    row_block = pl.BlockSpec((z.blk, z.a), lambda i, *_: (i, 0))
     parts_shape = sds((z.chips, z.j, z.cr), BF16)
-    part_spec = pl.BlockSpec((z.chips, z.j, z.blk), lambda i, *_: (0, 0, i))
     mm = 2 * KA * z.cr * z.a * 2
     bind = functools.partial
 
     grad_out = [sds(flat, BF16), sds((2 * KA, z.a), BF16), parts_shape, parts_shape]
-    grad_in = (jnp.asarray(base), jnp.asarray(shift), pre, cot)
     g, table, g_keep, g_send = pl.pallas_call(
         bind(grad_kernel, z),
         out_shape=grad_out,
-        grid_spec=pltpu.PrefetchScalarGridSpec(
-            num_scalar_prefetch=1,
-            grid=(z.nblk,),
-            in_specs=[
-                whole_spec(base.shape),
-                pl.BlockSpec((1,) + shift.shape[1:], lambda i, idx: (idx[0], 0, 0)),
-                row_block,
-                row_block,
-            ],
-            out_specs=[VSPEC] * 4,
-            scratch_shapes=[pltpu.VMEM((z.n_axial, z.j, z.blk), BF16)],
-        ),
+        in_specs=[pl.BlockSpec(memory_space=pltpu.SMEM)] + [ASPEC] * 2,
+        out_specs=[VSPEC] * 4,
+        scratch_shapes=[
+            pltpu.VMEM(flat, BF16),
+            pltpu.VMEM(flat, BF16),
+            pltpu.VMEM((z.nblk, z.n_axial, z.j, z.blk), BF16),
+            pltpu.SemaphoreType.DMA((2, z.nblk)),
+        ],
         compiler_params=params(48),
-        cost_estimate=cost(grad_in, grad_out, mm * 3),
+        cost_estimate=cost((pre, cot), grad_out, mm * 3),
         name="grad_axial",
-    )(idx, *grad_in)
+    )(idx, pre, cot)
 
     def add(keep, recv, ride, name, after=()):
         shape = (z.j + (z.ride if ride else 0), z.cr)
@@ -476,8 +478,9 @@
             [pltpu.VMEM((z.n_radial, z.j, z.lanes), F32)], name, mm // 2, after)
 
     def radial_exchange(parts):
-        return [parts[0]] + [
-            xor_permute(parts[d], "radial", z.n_radial, d) for d in range(1, z.n_radial)]
+        order = range(z.n_radial - 1, 0, -1)
+        moved = {d: xor_permute(parts[d], "radial", z.n_radial, d) for d in order}
+        return [parts[0]] + [moved[d] for d in range(1, z.n_radial)]
 
     g_recv = xor_permute(g_send, "axial", z.n_axial, 1)
     x_keep, x_send = small(
@@ -489,16 +492,19 @@
     (weight,) = small(
         bind(weight_kernel, z), None, (x, g), [sds((z.ride, z.cr), BF16)], [], "weight", mm * 2,
         (g_parts[0],))
-    g_sends = radial(g_pieces, 0, "grad_radial", (weight,))
+    (point,) = small(
+        bind(point_kernel, z), None, (pointwise_weight, g), [sds(flat, F32)], [], "pointwise",
+        mm * 2, (weight,))
+    g_sends = radial(g_pieces, 0, "grad_radial", (point,))
     g_modes = radial_exchange(g_sends)
     x_parts = add(x_keep, x_recv, (weight,), "input_add", (g_sends[0],))
     x_pieces = axial_exchange(x_parts)
 
     piece_shape = (z.j, z.lanes)
     d_x, d_y = small(
-        bind(mode_kernel, z), idx, (spectral_weight, jnp.asarray(lane_sums()), *g_modes),
+        bind(mode_kernel, z), idx, (spectral_weight, *g_modes),
         [sds(piece_shape, BF16), sds((z.qo, 2, z.own, 128), F32)],
-        [pltpu.VMEM((z.qo * z.c, 2048), BF16)] * 2 + [pltpu.VMEM((z.qo * z.c, 128), F32)],
+        [pltpu.VMEM((z.qo * z.c, 128), F32)],
         "mode_grad", mm * 2, (x_parts[0],))
     d_pieces = radial_exchange([d_x] * z.n_radial)
     x_sends = radial(x_pieces, z.ride_b, "input_radial", (d_x,))
@@ -507,34 +513,27 @@
         bind(back_kernel, z), idx, (*tables, *d_pieces), [sds((z.j, z.cr), BF16)],
         [pltpu.VMEM((z.n_radial, z.ng * z.j, 128), BF16)], "back_radial", mm // 2, (x_sends[0],))
     near = [lines] + [xor_permute(lines, "axial", z.n_axial, 2 * d) for d in range(1, z.chips)]
-    outer_out = [sds((z.qo, z.own, z.c, 128), F32), sds((z.ride, z.cr), F32)]
-    outer_in = (d_y, *x_modes)
-    spectral_grad, weight = pl.pallas_call(
-        bind(outer_kernel, z),
-        out_shape=outer_out,
-        grid=(z.own // 8,),
-        in_specs=[VSPEC] * len(outer_in) + [ASPEC],
-        out_specs=[
-            pl.BlockSpec((z.qo, 8, z.c, 128), lambda i: (0, i, 0, 0)),
-            VSPEC,
-        ],
-        scratch_shapes=[pltpu.VMEM((z.qo * z.c, 256), BF16)],
-        compiler_params=params(48),
-        cost_estimate=cost(outer_in, outer_out, 0),
-        name="spectral_outer",
-    )(*outer_in, lines)
+    x_rows, weight = small(
+        bind(gather_kernel, z), None, (x_modes[0], *x_modes[:0:-1]),
+        [sds((z.qo * z.c, 256), BF16), sds((z.ride, z.c // 8 * 128), BF16)], [], "gather", 0,
+        (lines,))
     half_shape = sds((KA + 16, z.cr), BF16)
-    (packed,) = small(bind(pack_kernel, z), None, (weight, *near), [half_shape], [], "pack")
+    (packed,) = small(
+        bind(pack_kernel, z), None, (weight, *near), [half_shape], [], "pack", 0, (x_rows,))
     far = xor_permute(packed, "axial", z.n_axial, 1)
     half_stage = pltpu.VMEM((KA, z.a), BF16)
-    (near_sum,) = small(
-        bind(near_kernel, z), idx, (table, pointwise_weight, g, packed), [sds(flat, F32)], [half_stage],
-        "near_axial", mm // 2)
+    grad_shape = (z.qo, z.own, z.c, 128)
+    spectral_grad, near_sum = small(
+        bind(outer_kernel, z), idx, (d_y, x_rows, table, point, packed),
+        [sds(grad_shape, F32), sds(flat, F32)],
+        [pltpu.VMEM(grad_shape, F32), half_stage, pltpu.SemaphoreType.DMA((z.own // 4,))],
+        "spectral_outer", mm, (), [ASPEC, VSPEC])
     input_grad, weight_grad = small(
         bind(final_kernel, z), idx, (table, near_sum, packed, far),
         [sds(flat, BF16), sds((z.c, z.c), F32)],
-        [half_stage, pltpu.VMEM((z.nblk, z.blk, z.a), BF16), pltpu.SemaphoreType.DMA((z.nblk,))],
-        "final_axial", mm // 2, (), [ASPEC, VSPEC])
+        [half_stage, pltpu.VMEM((z.nblk, z.blk, z.a), BF16), pltpu.VMEM((z.c, z.c), F32),
+         pltpu.SemaphoreType.DMA((z.nblk + 1,))],
+        "final_axial", mm // 2, (), [ASPEC, ASPEC])
     return (input_grad.reshape(inputs.shape), spectral_grad, weight_grad)
 
 

time: 71.6 us -> 60.1 us (0.84)
  Pallas kernels: 32.2 us -> 26.1 us
  waiting for transfers between devices: 12 us -> 6.95 us
  local copies, waits for them, and re-layouts: 1.88 us -> 0.03 us
  starting transfers between devices: 24.3 us -> 25.7 us
    pallas_call x2 -> x1, Pallas kernels: 11.4 us -> 5.27 us  [body(): pl.pallas_call(bind(grad_kernel, z), out_shape=grad_out, in_specs=[pl.Blo...]
    ppermute x21, waiting for transfers between devices: 12 us -> 6.95 us  [xor_permute(): return lax.ppermute(value, axis, [(i, i ^ d) for i in range(size)])]
    unnamed x18 -> x12, local copies, waits for them, and re-layouts: 1.88 us -> 0.03 us
    ppermute x21, starting transfers between devices: 24.3 us -> 25.7 us  [xor_permute(): return lax.ppermute(value, axis, [(i, i ^ d) for i in range(size)])]
    pallas_call x11 -> x13, Pallas kernels: 20.8 us -> 20.9 us  [small(): pl.pallas_call(kernel, out_shape=outs, in_specs=specs + [VSPEC] * len(arg...]
  transfers between devices with their start and end apart: 21 -> 21, of which waited for: 7 -> 5; matrix products, arithmetic and copies ran while one was open for 0% -> 0% of each run, Pallas kernels for 32% -> 31%
where the time goes in v3:
time: 60.1 us; the launch traced here: 59.9 us
  Pallas kernels  26.1 us (43%)
  starting transfers between devices  25.7 us (43%)
  waiting for transfers between devices  6.95 us (12%)
  between operations  1 us (2%)
    ppermute x21, starting transfers between devices, xor_permute(): return lax.ppermute(value, axis, [(i, i ^ d) for i in range(size)])  25.7 us
    pallas_call x13, Pallas kernels, small(): pl.pallas_call(kernel, out_shape=outs, in_specs=specs + [VSPEC] * len(arg...  20.9 us
    ppermute x21, waiting for transfers between devices, xor_permute(): return lax.ppermute(value, axis, [(i, i ^ d) for i in range(size)])  6.95 us
    pallas_call x1, Pallas kernels, body(): pl.pallas_call(bind(grad_kernel, z), out_shape=grad_out, in_specs=[pl.Blo...  5.27 us
  transfers between devices with their start and end apart: 21, of which 5 were waited for; matrix products, arithmetic and copies ran while one was open for 0% of the time, Pallas kernels for 31%

profile of v3, /device:TPU:0, one launch (start us, length us, event | category | flops | bytes accessed | tf_op | source)
XLA Modules:
  0.0 59.9 jit_solution(5913812345716432723)
XLA Ops:
  0.7 5.3 %grad_axial.1 = (bf16[1024,1024]{1,0:T(8,128)(2,1)S(1)}, bf16[512,1024]{1,0:T(8,128)(2,1)S(1)}, bf16[4,64,1024]{2,1,0:T(8,128)(2,1)S(1)}, bf16[4,64,1024]{2,1,0:T(8,128)(2,1)S(1)}) custom-call(s32[2]{0:T(128)S(1)} %pad_add_fusion.idx, bf16[1024,1024]{1,0:T(8,128)(2,1)} %bitcast.8, bf16[1024,1024]{1,0:T(8,128)(2,1)} %bitcast.9), custom_call_target="tpu_custom_call" | custom-call | flops 3221225472 | bytes 8388608 | tf_op jit(solution)/shard_map/grad_axial/pallas_call | solution.py:448
  6.0 0.5 collective-permute-start
  6.5 2.0 %input_axial.1 = (bf16[4,64,1024]{2,1,0:T(8,128)(2,1)S(1)}, bf16[4,64,1024]{2,1,0:T(8,128)(2,1)S(1)}) custom-call(s32[2]{0:T(128)S(1)} %pad_add_fusion.idx, bf16[512,1024]{1,0:T(8,128)(2,1)S(1)} %get-tuple-element.33.t_ref, bf16[1024,1024]{1,0:T(8,128)(2,1)S(1)} %bitcast.6), custom_call_target="tpu_custom_call" | custom-call | flops 1073741824 | bytes 4194304 | tf_op jit(solution)/shard_map/input_axial/pallas_call | solution.py:418
  8.8 3.0 %collective-permute-start.1 = (bf16[64,1024]{1,0:T(8,128)(2,1)S(1)}, bf16[64,1024]{1,0:T(8,128)(2,1)S(1)}, u32[]{:S(2)}, u32[]{:S(2)}) collective-permute-start(bf16[64,1024]{1,0:T(8,128)(2,1)S(1)} %get-tuple-element.38), channel_id=1, source_target_pairs={{0,8},{4,12},{8,0},{12,4},{16,24},{20,28},{24,16},{28,20},{1,9},{5... | collective-permute-start | bytes 393224 | tf_op jit(solution)/shard_map/ppermute | solution.py:432
  11.8 1.5 %collective-permute-start.2 = (bf16[64,1024]{1,0:T(8,128)(2,1)S(1)}, bf16[64,1024]{1,0:T(8,128)(2,1)S(1)}, u32[]{:S(2)}, u32[]{:S(2)}) collective-permute-start(bf16[64,1024]{1,0:T(8,128)(2,1)S(1)} %get-tuple-element.39), channel_id=1, source_target_pairs={{0,16},{4,20},{8,24},{12,28},{16,0},{20,4},{24,8},{28,12},{1,17},{... | collective-permute-start | bytes 393224 | tf_op jit(solution)/shard_map/ppermute | solution.py:432
  13.3 2.9 %weight.1.refs_0_ = bf16[8,1024]{1,0:T(8,128)(2,1)S(1)} custom-call(bf16[1024,1024]{1,0:T(8,128)(2,1)S(1)} %bitcast.7, bf16[1024,1024]{1,0:T(8,128)(2,1)S(1)} %get-tuple-element.41.g_ref, f32[64,1024]{1,0:T(8,128)S(1)} %get-tuple-element.37.refs_0_), custom_call_target="tpu_custom_call" | custom-call | flops 2147483648 | bytes 4210688 | tf_op jit(solution)/shard_map/weight/pallas_call | solution.py:418
  16.2 3.1 %pointwise.1.refs_4_.point_ref = f32[1024,1024]{1,0:T(8,128)S(1)} custom-call(bf16[64,64]{1,0:T(8,128)(2,1)S(1)} %copy-done.5, bf16[1024,1024]{1,0:T(8,128)(2,1)S(1)} %get-tuple-element.41.g_ref, bf16[8,1024]{1,0:T(8,128)(2,1)S(1)} %weight.1.refs_0_), custom_call_target="tpu_custom_call" | custom-call | flops 2147483648 | bytes 6299648 | tf_op jit(solution)/shard_map/pointwise/pallas_call | solution.py:418
  19.4 0.3 collective-permute-done.2.refs_2_
  19.7 1.2 %grad_radial.1 = (f32[64,512]{1,0:T(8,128)S(1)}, bf16[64,512]{1,0:T(8,128)(2,1)S(1)}, bf16[64,512]{1,0:T(8,128)(2,1)S(1)}, bf16[64,512]{1,0:T(8,128)(2,1)S(1)}) custom-call(s32[2]{0:T(128)S(1)} %pad_add_fusion.idx, bf16[256,1024]{1,0:T(8,128)(2,1)S(1)} %copy-done, bf16[256,1024]{1,0:T(8,128)(2,1)S(1)} %copy-done.1, f32[4,4,8,128]{3,2,1,0:T(8,128)S(1)} %copy-done.2, ...), custom_call_target="tpu_custom_call" | custom-call | flops 536870912 | bytes 2097152 | tf_op jit(solution)/shard_map/grad_radial/pallas_call | solution.py:418
  20.9 1.8 %collective-permute-start.4 = (bf16[64,512]{1,0:T(8,128)(2,1)S(1)}, bf16[64,512]{1,0:T(8,128)(2,1)S(1)}, u32[]{:S(2)}, u32[]{:S(2)}) collective-permute-start(bf16[64,512]{1,0:T(8,128)(2,1)S(1)} %get-tuple-element.43), channel_id=1, source_target_pairs={{0,1},{1,0},{2,3},{3,2},{4,5},{5,4},{6,7},{7,6},{8,9},{9,8},{10,11... | collective-permute-start | bytes 196616 | tf_op jit(solution)/shard_map/ppermute | solution.py:432
  22.8 2.6 %collective-permute-start.5 = (bf16[64,512]{1,0:T(8,128)(2,1)S(1)}, bf16[64,512]{1,0:T(8,128)(2,1)S(1)}, u32[]{:S(2)}, u32[]{:S(2)}) collective-permute-start(bf16[64,512]{1,0:T(8,128)(2,1)S(1)} %get-tuple-element.44), channel_id=1, source_target_pairs={{0,2},{1,3},{2,0},{3,1},{4,6},{5,7},{6,4},{7,5},{8,10},{9,11},{10,... | collective-permute-start | bytes 196616 | tf_op jit(solution)/shard_map/ppermute | solution.py:432
  25.5 2.7 %collective-permute-start.10 = (bf16[72,1024]{1,0:T(8,128)(2,1)S(1)}, bf16[72,1024]{1,0:T(8,128)(2,1)S(1)}, u32[]{:S(2)}, u32[]{:S(2)}) collective-permute-start(bf16[72,1024]{1,0:T(8,128)(2,1)S(1)} %get-tuple-element.51), channel_id=1, source_target_pairs={{0,24},{4,28},{8,16},{12,20},{16,8},{20,12},{24,0},{28,4},{1,25},{... | collective-permute-start | bytes 442376 | tf_op jit(solution)/shard_map/ppermute | solution.py:432
  28.2 0.5 collective-permute-start.8
  28.7 0.3 collective-permute-start.9
  29.1 0.3 collective-permute-done.5.refs_2_
  29.4 2.0 %collective-permute-done.6.refs_3_ = bf16[64,512]{1,0:T(8,128)(2,1)S(1)} collective-permute-done((bf16[64,512]{1,0:T(8,128)(2,1)S(1)}, bf16[64,512]{1,0:T(8,128)(2,1)S(1)}, u32[]{:S(2)}, u32[]{:S(2)}) %collective-permute-start.6) | collective-permute-done | bytes 65568 | tf_op jit(solution)/shard_map/ppermute | solution.py:432
  31.4 2.4 %mode_grad.1 = (bf16[64,512]{1,0:T(8,128)(2,1)S(1)}, f32[8,2,32,128]{3,2,1,0:T(8,128)S(1)}) custom-call(s32[2]{0:T(128)S(1)} %pad_add_fusion.idx, bf16[8,32,64,128]{3,2,1,0:T(8,128)(2,1)S(1)} %copy-done.3, f32[64,512]{1,0:T(8,128)S(1)} %get-tuple-element.42.refs_1_.refs_0_, bf16[64,512]{1,0:T(8,128)(2,1)S(1)} %collective-permute-done.4.refs_1_, ...), custom_call_target="tpu_custom_call" | custom-call | flops 2147483648 | bytes 4849664 | tf_op jit(solution)/shard_map/mode_grad/pallas_call | solution.py:418
  33.9 2.0 %collective-permute-start.15 = (bf16[64,512]{1,0:T(8,128)(2,1)S(1)}, bf16[64,512]{1,0:T(8,128)(2,1)S(1)}, u32[]{:S(2)}, u32[]{:S(2)}) collective-permute-start(bf16[64,512]{1,0:T(8,128)(2,1)S(1)} %get-tuple-element.52.refs_4_.refs_0_), channel_id=1, source_target_pairs={{0,2},{1,3},{2,0},{3,1},{4,6},{5,7},{6,4},{7,5},{8,10},{9,11},{10,... | collective-permute-start | bytes 196616 | tf_op jit(solution)/shard_map/ppermute | solution.py:432
  35.9 2.4 %collective-permute-start.16 = (bf16[64,512]{1,0:T(8,128)(2,1)S(1)}, bf16[64,512]{1,0:T(8,128)(2,1)S(1)}, u32[]{:S(2)}, u32[]{:S(2)}) collective-permute-start(bf16[64,512]{1,0:T(8,128)(2,1)S(1)} %get-tuple-element.52.refs_4_.refs_0_), channel_id=1, source_target_pairs={{0,3},{1,2},{2,1},{3,0},{4,7},{5,6},{6,5},{7,4},{8,11},{9,10},{10,... | collective-permute-start | bytes 196616 | tf_op jit(solution)/shard_map/ppermute | solution.py:432
  38.3 1.2 %input_radial.1 = (f32[72,512]{1,0:T(8,128)S(1)}, bf16[72,512]{1,0:T(8,128)(2,1)S(1)}, bf16[72,512]{1,0:T(8,128)(2,1)S(1)}, bf16[72,512]{1,0:T(8,128)(2,1)S(1)}) custom-call(s32[2]{0:T(128)S(1)} %pad_add_fusion.idx, bf16[256,1024]{1,0:T(8,128)(2,1)S(1)} %copy-done, bf16[256,1024]{1,0:T(8,128)(2,1)S(1)} %copy-done.1, f32[4,4,8,128]{3,2,1,0:T(8,128)S(1)} %copy-done.2, ...), custom_call_target="tpu_custom_call" | custom-call | flops 536870912 | bytes 2220032 | tf_op jit(solution)/shard_map/input_radial/pallas_call | solution.py:418
  39.5 1.5 %collective-permute-start.11 = (bf16[72,512]{1,0:T(8,128)(2,1)S(1)}, bf16[72,512]{1,0:T(8,128)(2,1)S(1)}, u32[]{:S(2)}, u32[]{:S(2)}) collective-permute-start(bf16[72,512]{1,0:T(8,128)(2,1)S(1)} %get-tuple-element.54), channel_id=1, source_target_pairs={{0,3},{1,2},{2,1},{3,0},{4,7},{5,6},{6,5},{7,4},{8,11},{9,10},{10,... | collective-permute-start | bytes 221192 | tf_op jit(solution)/shard_map/ppermute | solution.py:432
  41.0 1.1 %collective-permute-done.16.refs_3_ = bf16[64,512]{1,0:T(8,128)(2,1)S(1)} collective-permute-done((bf16[64,512]{1,0:T(8,128)(2,1)S(1)}, bf16[64,512]{1,0:T(8,128)(2,1)S(1)}, u32[]{:S(2)}, u32[]{:S(2)}) %collective-permute-start.16) | collective-permute-done | bytes 65568 | tf_op jit(solution)/shard_map/ppermute | solution.py:432
  42.1 1.0 %back_radial.1.refs_4_.refs_0_ = bf16[64,1024]{1,0:T(8,128)(2,1)S(1)} custom-call(s32[2]{0:T(128)S(1)} %pad_add_fusion.idx, bf16[256,1024]{1,0:T(8,128)(2,1)S(1)} %copy-done, bf16[256,1024]{1,0:T(8,128)(2,1)S(1)} %copy-done.1, f32[4,4,8,128]{3,2,1,0:T(8,128)S(1)} %copy-done.2, bf16[64,512]{1,0:T(8,128)(2,1)S(1)} %get-tuple-element.52.refs_4_.refs_0_, ...), custom_call_target="tpu_custom_call" | custom-call | flops 536870912 | bytes 1507328 | tf_op jit(solution)/shard_map/back_radial/pallas_call | solution.py:418
  43.2 1.6 %collective-permute-start.17 = (bf16[64,1024]{1,0:T(8,128)(2,1)S(1)}, bf16[64,1024]{1,0:T(8,128)(2,1)S(1)}, u32[]{:S(2)}, u32[]{:S(2)}) collective-permute-start(bf16[64,1024]{1,0:T(8,128)(2,1)S(1)} %back_radial.1.refs_4_.refs_0_), channel_id=1, source_target_pairs={{0,8},{4,12},{8,0},{12,4},{16,24},{20,28},{24,16},{28,20},{1,9},{5... | collective-permute-start | bytes 393224 | tf_op jit(solution)/shard_map/ppermute | solution.py:432
  44.7 1.5 %collective-permute-start.18 = (bf16[64,1024]{1,0:T(8,128)(2,1)S(1)}, bf16[64,1024]{1,0:T(8,128)(2,1)S(1)}, u32[]{:S(2)}, u32[]{:S(2)}) collective-permute-start(bf16[64,1024]{1,0:T(8,128)(2,1)S(1)} %back_radial.1.refs_4_.refs_0_), channel_id=1, source_target_pairs={{0,16},{4,20},{8,24},{12,28},{16,0},{20,4},{24,8},{28,12},{1,17},{... | collective-permute-start | bytes 393224 | tf_op jit(solution)/shard_map/ppermute | solution.py:432
  46.2 0.5 collective-permute-start.19
  46.7 0.7 %collective-permute-start.12 = (bf16[72,512]{1,0:T(8,128)(2,1)S(1)}, bf16[72,512]{1,0:T(8,128)(2,1)S(1)}, u32[]{:S(2)}, u32[]{:S(2)}) collective-permute-start(bf16[72,512]{1,0:T(8,128)(2,1)S(1)} %get-tuple-element.55), channel_id=1, source_target_pairs={{0,2},{1,3},{2,0},{3,1},{4,6},{5,7},{6,4},{7,5},{8,10},{9,11},{10,... | collective-permute-start | bytes 221192 | tf_op jit(solution)/shard_map/ppermute | solution.py:432
  47.4 2.2 %collective-permute-start.13 = (bf16[72,512]{1,0:T(8,128)(2,1)S(1)}, bf16[72,512]{1,0:T(8,128)(2,1)S(1)}, u32[]{:S(2)}, u32[]{:S(2)}) collective-permute-start(bf16[72,512]{1,0:T(8,128)(2,1)S(1)} %get-tuple-element.56), channel_id=1, source_target_pairs={{0,1},{1,0},{2,3},{3,2},{4,5},{5,4},{6,7},{7,6},{8,9},{9,8},{10,11... | collective-permute-start | bytes 221192 | tf_op jit(solution)/shard_map/ppermute | solution.py:432
  49.6 3.1 %collective-permute-done.12.refs_2_ = bf16[72,512]{1,0:T(8,128)(2,1)S(1)} collective-permute-done((bf16[72,512]{1,0:T(8,128)(2,1)S(1)}, bf16[72,512]{1,0:T(8,128)(2,1)S(1)}, u32[]{:S(2)}, u32[]{:S(2)}) %collective-permute-start.12) | collective-permute-done | bytes 73760 | tf_op jit(solution)/shard_map/ppermute | solution.py:432
  52.8 0.2 gather.1
  53.1 4.3 %spectral_outer.1 = (f32[8,32,64,128]{3,2,1,0:T(8,128)}, f32[1024,1024]{1,0:T(8,128)S(1)}) custom-call(s32[2]{0:T(128)S(1)} %pad_add_fusion.idx, f32[8,2,32,128]{3,2,1,0:T(8,128)S(1)} %get-tuple-element.48.dy_ref, bf16[512,256]{1,0:T(8,128)(2,1)S(1)} %get-tuple-element.57.refs_4_.x_rows, bf16[512,1024]{1,0:T(8,128)(2,1)S(1)} %get-tuple-element.33.t_ref, ...), custom_call_target="tpu_custom_call" | custom-call | flops 1073741824 | bytes 18907136 | tf_op jit(solution)/shard_map/spectral_outer/pallas_call | solution.py:418
  57.4 2.3 %final_axial.1 = (bf16[1024,1024]{1,0:T(8,128)(2,1)}, f32[64,64]{1,0:T(8,128)}) custom-call(s32[2]{0:T(128)S(1)} %pad_add_fusion.idx, bf16[512,1024]{1,0:T(8,128)(2,1)S(1)} %get-tuple-element.33.t_ref, f32[1024,1024]{1,0:T(8,128)S(1)} %get-tuple-element.59.near_ref, bf16[272,1024]{1,0:T(8,128)(2,1)S(1)} %pack.1.lines_ref.pack_ref, ...), custom_call_target="tpu_custom_call" | custom-call | flops 536870912 | bytes 8470528 | tf_op jit(solution)/shard_map/final_axial/pallas_call | solution.py:418
  (37 shorter events, 0.7 us)
Async XLA Ops:
  0.7 5.8 %copy-start.4 = (bf16[64,16,1024]{2,1,0:T(8,128)(2,1)S(1)}, bf16[64,16,1024]{2,1,0:T(8,128)(2,1)}, u32[]{:S(2)}) copy-start(bf16[64,16,1024]{2,1,0:T(8,128)(2,1)} %param.8) | copy-start | bytes 6291460
  6.0 2.6 %collective-permute-start = (bf16[4,64,1024]{2,1,0:T(8,128)(2,1)S(1)}, bf16[4,64,1024]{2,1,0:T(8,128)(2,1)S(1)}, u32[]{:S(2)}, u32[]{:S(2)}) collective-permute-start(bf16[4,64,1024]{2,1,0:T(8,128)(2,1)S(1)} %get-tuple-element.35), channel_id=1, source_target_pairs={{0,4},{4,0},{8,12},{12,8},{16,20},{20,16},{24,28},{28,24},{1,5},{5... | collective-permute-start | bytes 1572872 | tf_op jit(solution)/shard_map/ppermute | solution.py:432
  8.5 16.9 %collective-permute-start.7 = (bf16[4,64,1024]{2,1,0:T(8,128)(2,1)S(1)}, bf16[4,64,1024]{2,1,0:T(8,128)(2,1)S(1)}, u32[]{:S(2)}, u32[]{:S(2)}) collective-permute-start(bf16[4,64,1024]{2,1,0:T(8,128)(2,1)S(1)} %get-tuple-element.46), channel_id=1, source_target_pairs={{0,4},{4,0},{8,12},{12,8},{16,20},{20,16},{24,28},{28,24},{1,5},{5... | collective-permute-start | bytes 1572872 | tf_op jit(solution)/shard_map/ppermute | solution.py:432
  8.8 10.6 %collective-permute-start.1 = (bf16[64,1024]{1,0:T(8,128)(2,1)S(1)}, bf16[64,1024]{1,0:T(8,128)(2,1)S(1)}, u32[]{:S(2)}, u32[]{:S(2)}) collective-permute-start(bf16[64,1024]{1,0:T(8,128)(2,1)S(1)} %get-tuple-element.38), channel_id=1, source_target_pairs={{0,8},{4,12},{8,0},{12,4},{16,24},{20,28},{24,16},{28,20},{1,9},{5... | collective-permute-start | bytes 393224 | tf_op jit(solution)/shard_map/ppermute | solution.py:432
  11.8 8.0 %collective-permute-start.2 = (bf16[64,1024]{1,0:T(8,128)(2,1)S(1)}, bf16[64,1024]{1,0:T(8,128)(2,1)S(1)}, u32[]{:S(2)}, u32[]{:S(2)}) collective-permute-start(bf16[64,1024]{1,0:T(8,128)(2,1)S(1)} %get-tuple-element.39), channel_id=1, source_target_pairs={{0,16},{4,20},{8,24},{12,28},{16,0},{20,4},{24,8},{28,12},{1,17},{... | collective-permute-start | bytes 393224 | tf_op jit(solution)/shard_map/ppermute | solution.py:432
  13.3 6.4 %collective-permute-start.3 = (bf16[64,1024]{1,0:T(8,128)(2,1)S(1)}, bf16[64,1024]{1,0:T(8,128)(2,1)S(1)}, u32[]{:S(2)}, u32[]{:S(2)}) collective-permute-start(bf16[64,1024]{1,0:T(8,128)(2,1)S(1)} %get-tuple-element.40), channel_id=1, source_target_pairs={{0,24},{4,28},{8,16},{12,20},{16,8},{20,12},{24,0},{28,4},{1,25},{... | collective-permute-start | bytes 393224 | tf_op jit(solution)/shard_map/ppermute | solution.py:432
  13.3 2.9 %copy-start.5 = (bf16[64,64]{1,0:T(8,128)(2,1)S(1)}, bf16[64,64]{1,0:T(8,128)(2,1)}, u32[]{:S(2)}) copy-start(bf16[64,64]{1,0:T(8,128)(2,1)} %w_ref.2) | copy-start | bytes 24580
  16.2 3.5 %copy-start = (bf16[256,1024]{1,0:T(8,128)(2,1)S(1)}, bf16[256,1024]{1,0:T(8,128)(2,1)}, u32[]{:S(2)}) copy-start(bf16[256,1024]{1,0:T(8,128)(2,1)} %constant.15.clone.high_ref) | copy-start | bytes 1572868
  16.2 3.5 %copy-start.1 = (bf16[256,1024]{1,0:T(8,128)(2,1)S(1)}, bf16[256,1024]{1,0:T(8,128)(2,1)}, u32[]{:S(2)}) copy-start(bf16[256,1024]{1,0:T(8,128)(2,1)} %constant.16.clone.low_ref) | copy-start | bytes 1572868
  16.2 3.5 %copy-start.2 = (f32[4,4,8,128]{3,2,1,0:T(8,128)S(1)}, f32[4,4,8,128]{3,2,1,0:T(8,128)}, u32[]{:S(2)}) copy-start(f32[4,4,8,128]{3,2,1,0:T(8,128)} %constant.17.clone.shift_ref) | copy-start | bytes 196612
  19.4 12.0 %copy-start.3 = (bf16[8,32,64,128]{3,2,1,0:T(8,128)(2,1)S(1)}, bf16[8,32,64,128]{3,2,1,0:T(8,128)(2,1)}, u32[]{:S(2)}) copy-start(bf16[8,32,64,128]{3,2,1,0:T(8,128)(2,1)} %w_ref.3) | copy-start | bytes 12582916
  20.9 7.8 %collective-permute-start.4 = (bf16[64,512]{1,0:T(8,128)(2,1)S(1)}, bf16[64,512]{1,0:T(8,128)(2,1)S(1)}, u32[]{:S(2)}, u32[]{:S(2)}) collective-permute-start(bf16[64,512]{1,0:T(8,128)(2,1)S(1)} %get-tuple-element.43), channel_id=1, source_target_pairs={{0,1},{1,0},{2,3},{3,2},{4,5},{5,4},{6,7},{7,6},{8,9},{9,8},{10,11... | collective-permute-start | bytes 196616 | tf_op jit(solution)/shard_map/ppermute | solution.py:432
  22.8 6.6 %collective-permute-start.5 = (bf16[64,512]{1,0:T(8,128)(2,1)S(1)}, bf16[64,512]{1,0:T(8,128)(2,1)S(1)}, u32[]{:S(2)}, u32[]{:S(2)}) collective-permute-start(bf16[64,512]{1,0:T(8,128)(2,1)S(1)} %get-tuple-element.44), channel_id=1, source_target_pairs={{0,2},{1,3},{2,0},{3,1},{4,6},{5,7},{6,4},{7,5},{8,10},{9,11},{10,... | collective-permute-start | bytes 196616 | tf_op jit(solution)/shard_map/ppermute | solution.py:432
  25.4 6.1 %collective-permute-start.6 = (bf16[64,512]{1,0:T(8,128)(2,1)S(1)}, bf16[64,512]{1,0:T(8,128)(2,1)S(1)}, u32[]{:S(2)}, u32[]{:S(2)}) collective-permute-start(bf16[64,512]{1,0:T(8,128)(2,1)S(1)} %get-tuple-element.45), channel_id=1, source_target_pairs={{0,3},{1,2},{2,1},{3,0},{4,7},{5,6},{6,5},{7,4},{8,11},{9,10},{10,... | collective-permute-start | bytes 196616 | tf_op jit(solution)/shard_map/ppermute | solution.py:432
  25.5 10.4 %collective-permute-start.10 = (bf16[72,1024]{1,0:T(8,128)(2,1)S(1)}, bf16[72,1024]{1,0:T(8,128)(2,1)S(1)}, u32[]{:S(2)}, u32[]{:S(2)}) collective-permute-start(bf16[72,1024]{1,0:T(8,128)(2,1)S(1)} %get-tuple-element.51), channel_id=1, source_target_pairs={{0,24},{4,28},{8,16},{12,20},{16,8},{20,12},{24,0},{28,4},{1,25},{... | collective-permute-start | bytes 442376 | tf_op jit(solution)/shard_map/ppermute | solution.py:432
  28.2 10.1 %collective-permute-start.8 = (bf16[72,1024]{1,0:T(8,128)(2,1)S(1)}, bf16[72,1024]{1,0:T(8,128)(2,1)S(1)}, u32[]{:S(2)}, u32[]{:S(2)}) collective-permute-start(bf16[72,1024]{1,0:T(8,128)(2,1)S(1)} %get-tuple-element.49), channel_id=1, source_target_pairs={{0,8},{4,12},{8,0},{12,4},{16,24},{20,28},{24,16},{28,20},{1,9},{5... | collective-permute-start | bytes 442376 | tf_op jit(solution)/shard_map/ppermute | solution.py:432
  28.7 9.5 %collective-permute-start.9 = (bf16[72,1024]{1,0:T(8,128)(2,1)S(1)}, bf16[72,1024]{1,0:T(8,128)(2,1)S(1)}, u32[]{:S(2)}, u32[]{:S(2)}) collective-permute-start(bf16[72,1024]{1,0:T(8,128)(2,1)S(1)} %get-tuple-element.50), channel_id=1, source_target_pairs={{0,16},{4,20},{8,24},{12,28},{16,0},{20,4},{24,8},{28,12},{1,17},{... | collective-permute-start | bytes 442376 | tf_op jit(solution)/shard_map/ppermute | solution.py:432
  33.8 7.2 %collective-permute-start.14 = (bf16[64,512]{1,0:T(8,128)(2,1)S(1)}, bf16[64,512]{1,0:T(8,128)(2,1)S(1)}, u32[]{:S(2)}, u32[]{:S(2)}) collective-permute-start(bf16[64,512]{1,0:T(8,128)(2,1)S(1)} %get-tuple-element.52.refs_4_.refs_0_), channel_id=1, source_target_pairs={{0,1},{1,0},{2,3},{3,2},{4,5},{5,4},{6,7},{7,6},{8,9},{9,8},{10,11... | collective-permute-start | bytes 196616 | tf_op jit(solution)/shard_map/ppermute | solution.py:432
  33.9 7.1 %collective-permute-start.15 = (bf16[64,512]{1,0:T(8,128)(2,1)S(1)}, bf16[64,512]{1,0:T(8,128)(2,1)S(1)}, u32[]{:S(2)}, u32[]{:S(2)}) collective-permute-start(bf16[64,512]{1,0:T(8,128)(2,1)S(1)} %get-tuple-element.52.refs_4_.refs_0_), channel_id=1, source_target_pairs={{0,2},{1,3},{2,0},{3,1},{4,6},{5,7},{6,4},{7,5},{8,10},{9,11},{10,... | collective-permute-start | bytes 196616 | tf_op jit(solution)/shard_map/ppermute | solution.py:432
  35.9 6.2 %collective-permute-start.16 = (bf16[64,512]{1,0:T(8,128)(2,1)S(1)}, bf16[64,512]{1,0:T(8,128)(2,1)S(1)}, u32[]{:S(2)}, u32[]{:S(2)}) collective-permute-start(bf16[64,512]{1,0:T(8,128)(2,1)S(1)} %get-tuple-element.52.refs_4_.refs_0_), channel_id=1, source_target_pairs={{0,3},{1,2},{2,1},{3,0},{4,7},{5,6},{6,5},{7,4},{8,11},{9,10},{10,... | collective-permute-start | bytes 196616 | tf_op jit(solution)/shard_map/ppermute | solution.py:432
  39.5 8.0 %collective-permute-start.11 = (bf16[72,512]{1,0:T(8,128)(2,1)S(1)}, bf16[72,512]{1,0:T(8,128)(2,1)S(1)}, u32[]{:S(2)}, u32[]{:S(2)}) collective-permute-start(bf16[72,512]{1,0:T(8,128)(2,1)S(1)} %get-tuple-element.54), channel_id=1, source_target_pairs={{0,3},{1,2},{2,1},{3,0},{4,7},{5,6},{6,5},{7,4},{8,11},{9,10},{10,... | collective-permute-start | bytes 221192 | tf_op jit(solution)/shard_map/ppermute | solution.py:432
  43.2 9.8 %collective-permute-start.17 = (bf16[64,1024]{1,0:T(8,128)(2,1)S(1)}, bf16[64,1024]{1,0:T(8,128)(2,1)S(1)}, u32[]{:S(2)}, u32[]{:S(2)}) collective-permute-start(bf16[64,1024]{1,0:T(8,128)(2,1)S(1)} %back_radial.1.refs_4_.refs_0_), channel_id=1, source_target_pairs={{0,8},{4,12},{8,0},{12,4},{16,24},{20,28},{24,16},{28,20},{1,9},{5... | collective-permute-start | bytes 393224 | tf_op jit(solution)/shard_map/ppermute | solution.py:432
  44.7 8.2 %collective-permute-start.18 = (bf16[64,1024]{1,0:T(8,128)(2,1)S(1)}, bf16[64,1024]{1,0:T(8,128)(2,1)S(1)}, u32[]{:S(2)}, u32[]{:S(2)}) collective-permute-start(bf16[64,1024]{1,0:T(8,128)(2,1)S(1)} %back_radial.1.refs_4_.refs_0_), channel_id=1, source_target_pairs={{0,16},{4,20},{8,24},{12,28},{16,0},{20,4},{24,8},{28,12},{1,17},{... | collective-permute-start | bytes 393224 | tf_op jit(solution)/shard_map/ppermute | solution.py:432
  46.2 6.7 %collective-permute-start.19 = (bf16[64,1024]{1,0:T(8,128)(2,1)S(1)}, bf16[64,1024]{1,0:T(8,128)(2,1)S(1)}, u32[]{:S(2)}, u32[]{:S(2)}) collective-permute-start(bf16[64,1024]{1,0:T(8,128)(2,1)S(1)} %back_radial.1.refs_4_.refs_0_), channel_id=1, source_target_pairs={{0,24},{4,28},{8,16},{12,20},{16,8},{20,12},{24,0},{28,4},{1,25},{... | collective-permute-start | bytes 393224 | tf_op jit(solution)/shard_map/ppermute | solution.py:432
  46.7 6.0 %collective-permute-start.12 = (bf16[72,512]{1,0:T(8,128)(2,1)S(1)}, bf16[72,512]{1,0:T(8,128)(2,1)S(1)}, u32[]{:S(2)}, u32[]{:S(2)}) collective-permute-start(bf16[72,512]{1,0:T(8,128)(2,1)S(1)} %get-tuple-element.55), channel_id=1, source_target_pairs={{0,2},{1,3},{2,0},{3,1},{4,6},{5,7},{6,4},{7,5},{8,10},{9,11},{10,... | collective-permute-start | bytes 221192 | tf_op jit(solution)/shard_map/ppermute | solution.py:432
  47.4 5.3 %collective-permute-start.13 = (bf16[72,512]{1,0:T(8,128)(2,1)S(1)}, bf16[72,512]{1,0:T(8,128)(2,1)S(1)}, u32[]{:S(2)}, u32[]{:S(2)}) collective-permute-start(bf16[72,512]{1,0:T(8,128)(2,1)S(1)} %get-tuple-element.56), channel_id=1, source_target_pairs={{0,1},{1,0},{2,3},{3,2},{4,5},{5,4},{6,7},{7,6},{8,9},{9,8},{10,11... | collective-permute-start | bytes 221192 | tf_op jit(solution)/shard_map/ppermute | solution.py:432
  53.0 4.4 %collective-permute-start.20 = (bf16[272,1024]{1,0:T(8,128)(2,1)S(1)}, bf16[272,1024]{1,0:T(8,128)(2,1)S(1)}, u32[]{:S(2)}, u32[]{:S(2)}) collective-permute-start(bf16[272,1024]{1,0:T(8,128)(2,1)S(1)} %pack.1.lines_ref.pack_ref), channel_id=1, source_target_pairs={{0,4},{4,0},{8,12},{12,8},{16,20},{20,16},{24,28},{28,24},{1,5},{5... | collective-permute-start | bytes 1671176 | tf_op jit(solution)/shard_map/ppermute | solution.py:432
